TPU v7x, 32 devices: a whole 2x2x4 slice. The times are simulated.
32 devices in a mesh: clip: 8 (over z, x), head: 4 (over y, core).
Axes of the slice: x: 2, y: 2, z: 4, core: 2. Of those that a mesh axis runs over, the one named last changes fastest.
Arguments:
- patches: bfloat16 [8, 8, 196, 768], P('clip', None, 'head'), may hold values from -6 to 6
- cls_token: bfloat16 [8, 768], P('clip'), may hold values from -6 to 6
- keep_mask: int32 [8, 8, 196], P('clip'), may hold values 0 or 1
- gain_time: float32 [768], replicated, may hold values from 0.25 to 1.75
- qkv_time: bfloat16 [768, 12, 3, 64], P(None, 'head'), may hold values from -0.3125 to 0.3125
- proj_time: bfloat16 [12, 64, 768], P('head'), may hold values from -0.3125 to 0.3125
- temporal_fc: bfloat16 [768, 768], replicated, may hold values from -0.21875 to 0.21875
- gain_space: float32 [768], replicated, may hold values from 0.25 to 1.75
- qkv_space: bfloat16 [768, 12, 3, 64], P(None, 'head'), may hold values from -0.3125 to 0.3125
- proj_space: bfloat16 [12, 64, 768], P('head'), may hold values from -0.875 to 0.875
- gain_mlp: float32 [768], replicated, may hold values from 0.25 to 1.75
- mlp_in: bfloat16 [768, 3072], P(None, 'head'), may hold values from -0.21875 to 0.21875
- mlp_out: bfloat16 [3072, 768], P('head'), may hold values from -0.109375 to 0.109375
- cotangent: bfloat16 [8, 8, 196, 768], P('clip', None, 'head'), may hold values from -6 to 6
- cls_cotangent: bfloat16 [8, 768], P('clip'), may hold values from -6 to 6
Outputs:
- output: bfloat16 [8, 8, 196, 768], P('clip', None, 'head')
- output_cls: bfloat16 [8, 768], P('clip')
- input_grad: float32 [8, 8, 196, 768], P('clip', None, 'head')
- cls_grad: float32 [8, 768], P('clip')
- gain_time_grad: float32 [768], replicated
- qkv_time_grad: float32 [768, 12, 3, 64], P(None, 'head')
- proj_time_grad: float32 [12, 64, 768], P('head')
- temporal_fc_grad: float32 [768, 768], replicated
- gain_space_grad: float32 [768], replicated
- qkv_space_grad: float32 [768, 12, 3, 64], P(None, 'head')
- proj_space_grad: float32 [12, 64, 768], P('head')
- gain_mlp_grad: float32 [768], replicated
- mlp_in_grad: float32 [768, 3072], P(None, 'head')
- mlp_out_grad: float32 [3072, 768], P('head')
Inputs may be any that keep to these rules, and one draw needn't show every extreme that they name: `keep_mask`: 1 keeps the patch token of that clip, frame and position; a dropped token's rows take no branch output.
All inputs are finite; a program needn't handle non-finite values. No bound on the sum of `keep_mask` on one device may be relied on, other than what follows from the above.
Results may differ from a plain program's by a relative error of at most 0.03.
The roundings to bfloat16 on the way count: a program that leaves them out, or rounds other values in their place, can miss the bound.
Values may be sent and summed in bfloat16 or wider, within the bound.
A program may use at most 128 MiB of HBM per device.

v0:
```python
from functools import partial

import jax
import jax.numpy as jnp
from jax import lax
from jax.sharding import PartitionSpec as P

EPSILON = 1e-06
NEGATIVE = -1e30


def norm_forward(values, gain):
    center = values - jnp.mean(values, axis=-1, keepdims=True)
    spread = jnp.mean(center * center, axis=-1, keepdims=True)
    factor = lax.rsqrt(spread + EPSILON)
    scaled = center * factor
    return (scaled * gain, scaled, factor)


def norm_backward(upstream, gain, scaled, factor):
    weighted = upstream * gain
    inner = weighted - jnp.mean(weighted, axis=-1, keepdims=True)
    inner = inner - scaled * jnp.mean(weighted * scaled, axis=-1, keepdims=True)
    return factor * inner


def gelu_back(hidden, upstream):
    ignored, pullback = jax.vjp(partial(jax.nn.gelu, approximate=False), hidden)
    return pullback(upstream)[0]


def cls_tile(row_values):
    members = lax.axis_size("head")
    return jnp.broadcast_to(
        row_values[:, None, None, :], (row_values.shape[0], 1, members, row_values.shape[1])
    )


def gather_rows(shard):
    return lax.all_gather(shard, "head", axis=2, tiled=True)


def gather_grads(shard):
    return lax.all_gather(shard, "head", axis=2, tiled=True)


def time_sum(partial_rows):
    return lax.psum_scatter(partial_rows, "head", scatter_dimension=2, tiled=True)


def branch_sum(partial_rows, cls_partial):
    summed, cls_summed = (
        lax.psum_scatter(
            partial_rows.astype(jnp.bfloat16), "head", scatter_dimension=2, tiled=True
        ).astype(jnp.float32),
        lax.psum_scatter(
            cls_tile(cls_partial).astype(jnp.bfloat16), "head", scatter_dimension=2, tiled=True
        ).astype(jnp.float32),
    )
    return (summed, cls_summed[:, 0, 0, :])


def input_back(grads_full, cls_grads, weight_local):
    width = weight_local.shape[0]
    flat_weight = weight_local.reshape(width, -1)
    partial_rows = jnp.einsum(
        "cfpk,dk->cfpd", grads_full, flat_weight, preferred_element_type=jnp.float32
    )
    if cls_grads is None:
        return (
            lax.psum_scatter(
                partial_rows.astype(jnp.bfloat16), "head", scatter_dimension=2, tiled=True
            ).astype(jnp.float32),
            None,
        )
    cls_partial = jnp.einsum(
        "ck,dk->cd", cls_grads, flat_weight, preferred_element_type=jnp.float32
    )
    summed, cls_summed = (
        lax.psum_scatter(
            partial_rows.astype(jnp.bfloat16), "head", scatter_dimension=2, tiled=True
        ).astype(jnp.float32),
        lax.psum_scatter(
            cls_tile(cls_partial).astype(jnp.bfloat16), "head", scatter_dimension=2, tiled=True
        ).astype(jnp.float32),
    )
    return (summed, cls_summed[:, 0, 0, :])


def time_attention(queries, keys, values, allowed, scaling):
    scores = (
        jnp.einsum("cfphe,cgphe->cphfg", queries, keys, preferred_element_type=jnp.float32)
        * scaling
    )
    masked = jnp.where(allowed, scores, NEGATIVE)
    highest = jnp.max(masked, axis=-1, keepdims=True)
    weights = jnp.where(allowed, jnp.exp(masked - highest), 0.0)
    total = jnp.sum(weights, axis=-1, keepdims=True)
    softmax_rows = (weights / total).astype(jnp.bfloat16)
    mixed = jnp.einsum(
        "cphfg,cgphe->cfphe", softmax_rows, values, preferred_element_type=jnp.float32
    )
    return (mixed.astype(jnp.bfloat16), highest + jnp.log(total))


def time_attention_back(queries, keys, values, allowed, scaling, log_total, upstream):
    scores = (
        jnp.einsum("cfphe,cgphe->cphfg", queries, keys, preferred_element_type=jnp.float32)
        * scaling
    )
    softmax_rows = jnp.where(allowed, jnp.exp(scores - log_total), 0.0)
    softmax_grads = jnp.einsum(
        "cfphe,cgphe->cphfg", upstream, values, preferred_element_type=jnp.float32
    )
    centre = jnp.sum(softmax_rows * softmax_grads, axis=-1, keepdims=True)
    score_grads = (softmax_rows * (softmax_grads - centre)).astype(jnp.bfloat16)
    query_grads = (
        jnp.einsum("cphfg,cgphe->cfphe", score_grads, keys, preferred_element_type=jnp.float32)
        * scaling
    )
    key_grads = (
        jnp.einsum("cphfg,cfphe->cgphe", score_grads, queries, preferred_element_type=jnp.float32)
        * scaling
    )
    value_grads = jnp.einsum(
        "cphfg,cfphe->cgphe",
        softmax_rows.astype(jnp.bfloat16),
        upstream,
        preferred_element_type=jnp.float32,
    )
    return jnp.stack([query_grads, key_grads, value_grads], axis=-2).astype(jnp.bfloat16)


def space_attention(queries, keys, values, cls_query, cls_key, cls_value, key_ok, scaling):
    allowed = key_ok[:, :, None, None, :]
    scores = (
        jnp.einsum("cfphe,cfkhe->cfhpk", queries, keys, preferred_element_type=jnp.float32)
        * scaling
    )
    side_scores = (
        jnp.einsum("cfphe,che->cfhp", queries, cls_key, preferred_element_type=jnp.float32)
        * scaling
    )
    masked = jnp.where(allowed, scores, NEGATIVE)
    highest = jnp.maximum(jnp.max(masked, axis=-1), side_scores)
    weights = jnp.where(allowed, jnp.exp(masked - highest[..., None]), 0.0)
    side_weight = jnp.exp(side_scores - highest)
    total = jnp.sum(weights, axis=-1) + side_weight
    softmax_rows = (weights / total[..., None]).astype(jnp.bfloat16)
    side_rows = (side_weight / total).astype(jnp.bfloat16)
    mixed = jnp.einsum(
        "cfhpk,cfkhe->cfphe", softmax_rows, values, preferred_element_type=jnp.float32
    )
    mixed = mixed + jnp.einsum(
        "cfhp,che->cfphe", side_rows, cls_value, preferred_element_type=jnp.float32
    )
    head_allowed = key_ok[:, :, None, :]
    head_scores = (
        jnp.einsum("che,cfkhe->cfhk", cls_query, keys, preferred_element_type=jnp.float32) * scaling
    )
    self_score = (
        jnp.einsum("che,che->ch", cls_query, cls_key, preferred_element_type=jnp.float32) * scaling
    )
    head_masked = jnp.where(head_allowed, head_scores, NEGATIVE)
    head_high = jnp.maximum(jnp.max(head_masked, axis=-1), self_score[:, None, :])
    head_weights = jnp.where(head_allowed, jnp.exp(head_masked - head_high[..., None]), 0.0)
    self_weight = jnp.exp(self_score[:, None, :] - head_high)
    head_total = jnp.sum(head_weights, axis=-1) + self_weight
    head_rows = (head_weights / head_total[..., None]).astype(jnp.bfloat16)
    self_rows = (self_weight / head_total).astype(jnp.bfloat16)
    cls_mixed = jnp.einsum(
        "cfhk,cfkhe->cfhe", head_rows, values, preferred_element_type=jnp.float32
    )
    cls_mixed = cls_mixed + jnp.einsum(
        "cfh,che->cfhe", self_rows, cls_value, preferred_element_type=jnp.float32
    )
    cls_mixed = jnp.mean(cls_mixed, axis=1)
    return (
        mixed.astype(jnp.bfloat16),
        cls_mixed.astype(jnp.bfloat16),
        highest + jnp.log(total),
        head_high + jnp.log(head_total),
    )


def space_attention_back(
    queries,
    keys,
    values,
    cls_query,
    cls_key,
    cls_value,
    key_ok,
    scaling,
    log_total,
    cls_log_total,
    upstream,
    cls_upstream,
):
    frames = keys.shape[1]
    allowed = key_ok[:, :, None, None, :]
    scores = (
        jnp.einsum("cfphe,cfkhe->cfhpk", queries, keys, preferred_element_type=jnp.float32)
        * scaling
    )
    side_scores = (
        jnp.einsum("cfphe,che->cfhp", queries, cls_key, preferred_element_type=jnp.float32)
        * scaling
    )
    softmax_rows = jnp.where(allowed, jnp.exp(scores - log_total[..., None]), 0.0)
    side_rows = jnp.exp(side_scores - log_total)
    softmax_grads = jnp.einsum(
        "cfphe,cfkhe->cfhpk", upstream, values, preferred_element_type=jnp.float32
    )
    side_grads = jnp.einsum(
        "cfphe,che->cfhp", upstream, cls_value, preferred_element_type=jnp.float32
    )
    centre = jnp.sum(softmax_rows * softmax_grads, axis=-1) + side_rows * side_grads
    score_grads = (softmax_rows * (softmax_grads - centre[..., None])).astype(jnp.bfloat16)
    side_score_grads = (side_rows * (side_grads - centre)).astype(jnp.bfloat16)
    query_grads = jnp.einsum(
        "cfhpk,cfkhe->cfphe", score_grads, keys, preferred_element_type=jnp.float32
    )
    query_grads = (
        query_grads
        + jnp.einsum(
            "cfhp,che->cfphe", side_score_grads, cls_key, preferred_element_type=jnp.float32
        )
    ) * scaling
    key_grads = (
        jnp.einsum("cfhpk,cfphe->cfkhe", score_grads, queries, preferred_element_type=jnp.float32)
        * scaling
    )
    cls_key_grads = (
        jnp.einsum("cfhp,cfphe->che", side_score_grads, queries, preferred_element_type=jnp.float32)
        * scaling
    )
    value_grads = jnp.einsum(
        "cfhpk,cfphe->cfkhe",
        softmax_rows.astype(jnp.bfloat16),
        upstream,
        preferred_element_type=jnp.float32,
    )
    cls_value_grads = jnp.einsum(
        "cfhp,cfphe->che",
        side_rows.astype(jnp.bfloat16),
        upstream,
        preferred_element_type=jnp.float32,
    )
    head_allowed = key_ok[:, :, None, :]
    head_scores = (
        jnp.einsum("che,cfkhe->cfhk", cls_query, keys, preferred_element_type=jnp.float32) * scaling
    )
    self_score = (
        jnp.einsum("che,che->ch", cls_query, cls_key, preferred_element_type=jnp.float32) * scaling
    )
    head_rows = jnp.where(head_allowed, jnp.exp(head_scores - cls_log_total[..., None]), 0.0)
    self_rows = jnp.exp(self_score[:, None, :] - cls_log_total)
    head_grads = (
        jnp.einsum("che,cfkhe->cfhk", cls_upstream, values, preferred_element_type=jnp.float32)
        / frames
    )
    self_grads = (
        jnp.einsum("che,che->ch", cls_upstream, cls_value, preferred_element_type=jnp.float32)[
            :, None, :
        ]
        / frames
    )
    head_centre = jnp.sum(head_rows * head_grads, axis=-1) + self_rows * self_grads
    head_score_grads = (head_rows * (head_grads - head_centre[..., None])).astype(jnp.bfloat16)
    self_score_grads = (self_rows * (self_grads - head_centre)).astype(jnp.bfloat16)
    cls_query_grads = jnp.einsum(
        "cfhk,cfkhe->che", head_score_grads, keys, preferred_element_type=jnp.float32
    )
    cls_query_grads = (
        cls_query_grads
        + jnp.einsum("cfh,che->che", self_score_grads, cls_key, preferred_element_type=jnp.float32)
    ) * scaling
    key_grads = (
        key_grads
        + jnp.einsum(
            "cfhk,che->cfkhe", head_score_grads, cls_query, preferred_element_type=jnp.float32
        )
        * scaling
    )
    cls_key_grads = (
        cls_key_grads
        + jnp.einsum(
            "cfh,che->che", self_score_grads, cls_query, preferred_element_type=jnp.float32
        )
        * scaling
    )
    value_grads = (
        value_grads
        + jnp.einsum(
            "cfhk,che->cfkhe",
            head_rows.astype(jnp.bfloat16),
            cls_upstream,
            preferred_element_type=jnp.float32,
        )
        / frames
    )
    cls_value_grads = (
        cls_value_grads
        + jnp.einsum(
            "cfh,che->che",
            self_rows.astype(jnp.bfloat16),
            cls_upstream,
            preferred_element_type=jnp.float32,
        )
        / frames
    )
    triple_grads = jnp.stack([query_grads, key_grads, value_grads], axis=-2).astype(jnp.bfloat16)
    cls_triple_grads = jnp.stack([cls_query_grads, cls_key_grads, cls_value_grads], axis=-2).astype(
        jnp.bfloat16
    )
    return (triple_grads, cls_triple_grads)


def local(
    patches,
    cls_token,
    keep_mask,
    gain_time,
    qkv_time,
    proj_time,
    temporal_fc,
    gain_space,
    qkv_space,
    proj_space,
    gain_mlp,
    mlp_in,
    mlp_out,
    cotangent,
    cls_cotangent,
):
    clips, frames, local_count, width = patches.shape
    count = keep_mask.shape[2]
    heads_here = qkv_time.shape[1]
    head_size = qkv_time.shape[3]
    scaling = head_size ** (-0.5)
    share = 1.0 / lax.axis_size("head")
    keep_here = lax.dynamic_slice_in_dim(
        keep_mask, lax.axis_index("head") * local_count, local_count, axis=2
    )
    keep_float = keep_here.astype(jnp.float32)[..., None]
    key_ok = keep_mask > 0
    allowed_time = (jnp.transpose(keep_mask, (0, 2, 1))[:, :, None, None, :] > 0) | jnp.eye(
        frames, dtype=bool
    )[None, None, None]
    row_axes = (0, 1, 2)
    patch_rows = patches.astype(jnp.float32)
    normed, scaled_time, factor_time = norm_forward(patch_rows, gain_time)
    low_time = normed.astype(jnp.bfloat16)
    full_time = gather_rows(low_time)
    triple_time = jnp.einsum(
        "cfpd,dk->cfpk", full_time, qkv_time.reshape(width, -1), preferred_element_type=jnp.float32
    )
    triple_time = triple_time.astype(jnp.bfloat16).reshape(
        clips, frames, count, heads_here, 3, head_size
    )
    mixed_time, log_time = time_attention(
        triple_time[..., 0, :],
        triple_time[..., 1, :],
        triple_time[..., 2, :],
        allowed_time,
        scaling,
    )
    flat_mixed = mixed_time.reshape(clips, frames, count, heads_here * head_size)
    proj_time_flat = proj_time.reshape(-1, width)
    partial_time = jnp.einsum(
        "cfpk,kd->cfpd", flat_mixed, proj_time_flat, preferred_element_type=jnp.float32
    )
    attended = time_sum(partial_time).astype(jnp.bfloat16)
    temporal = jnp.einsum(
        "cfpd,de->cfpe", attended, temporal_fc, preferred_element_type=jnp.float32
    )
    first = patch_rows + keep_float * temporal
    normed, scaled_space, factor_space = norm_forward(first, gain_space)
    low_space = normed.astype(jnp.bfloat16)
    cls_rows = cls_token.astype(jnp.float32)
    cls_normed, cls_scaled_space, cls_factor_space = norm_forward(cls_rows, gain_space)
    cls_low_space = cls_normed.astype(jnp.bfloat16)
    full_space = gather_rows(low_space)
    flat_qkv_space = qkv_space.reshape(width, -1)
    triple_space = jnp.einsum(
        "cfpd,dk->cfpk", full_space, flat_qkv_space, preferred_element_type=jnp.float32
    )
    triple_space = triple_space.astype(jnp.bfloat16).reshape(
        clips, frames, count, heads_here, 3, head_size
    )
    cls_triple = jnp.dot(cls_low_space, flat_qkv_space, preferred_element_type=jnp.float32)
    cls_triple = cls_triple.astype(jnp.bfloat16).reshape(clips, heads_here, 3, head_size)
    mixed_space, cls_mixed, log_space, log_cls = space_attention(
        triple_space[..., 0, :],
        triple_space[..., 1, :],
        triple_space[..., 2, :],
        cls_triple[..., 0, :],
        cls_triple[..., 1, :],
        cls_triple[..., 2, :],
        key_ok,
        scaling,
    )
    flat_space = mixed_space.reshape(clips, frames, count, -1)
    flat_cls = cls_mixed.reshape(clips, -1)
    proj_space_flat = proj_space.reshape(-1, width)
    spatial, cls_spatial = branch_sum(
        jnp.einsum(
            "cfpk,kd->cfpd", flat_space, proj_space_flat, preferred_element_type=jnp.float32
        ),
        jnp.dot(flat_cls, proj_space_flat, preferred_element_type=jnp.float32),
    )
    second = first + keep_float * spatial
    cls_second = cls_rows + cls_spatial
    normed, scaled_mlp, factor_mlp = norm_forward(second, gain_mlp)
    low_mlp = normed.astype(jnp.bfloat16)
    cls_normed, cls_scaled_mlp, cls_factor_mlp = norm_forward(cls_second, gain_mlp)
    cls_low_mlp = cls_normed.astype(jnp.bfloat16)
    full_mlp = gather_rows(low_mlp)
    hidden = jnp.einsum("cfpd,dk->cfpk", full_mlp, mlp_in, preferred_element_type=jnp.float32)
    cls_hidden = jnp.dot(cls_low_mlp, mlp_in, preferred_element_type=jnp.float32)
    active = jax.nn.gelu(hidden, approximate=False).astype(jnp.bfloat16)
    cls_active = jax.nn.gelu(cls_hidden, approximate=False).astype(jnp.bfloat16)
    block_out, cls_block = branch_sum(
        jnp.einsum("cfpk,kd->cfpd", active, mlp_out, preferred_element_type=jnp.float32),
        jnp.dot(cls_active, mlp_out, preferred_element_type=jnp.float32),
    )
    output = (second + keep_float * block_out).astype(jnp.bfloat16)
    output_cls = (cls_second + cls_block).astype(jnp.bfloat16)
    upstream = cotangent.astype(jnp.float32)
    cls_upstream = cls_cotangent.astype(jnp.float32)
    block_grad = (keep_float * upstream).astype(jnp.bfloat16)
    full_block_grad = gather_grads(block_grad)
    mlp_out_grad = jnp.einsum(
        "cfpk,cfpd->kd", active, full_block_grad, preferred_element_type=jnp.float32
    )
    mlp_out_grad = mlp_out_grad + jnp.einsum(
        "ck,cd->kd", cls_active, cls_cotangent, preferred_element_type=jnp.float32
    )
    active_grad = jnp.einsum(
        "cfpd,kd->cfpk", full_block_grad, mlp_out, preferred_element_type=jnp.float32
    )
    cls_active_grad = jnp.einsum(
        "cd,kd->ck", cls_cotangent, mlp_out, preferred_element_type=jnp.float32
    )
    hidden_grad = gelu_back(hidden, active_grad).astype(jnp.bfloat16)
    cls_hidden_grad = gelu_back(cls_hidden, cls_active_grad).astype(jnp.bfloat16)
    mlp_in_grad = jnp.einsum(
        "cfpd,cfpk->dk", full_mlp, hidden_grad, preferred_element_type=jnp.float32
    )
    mlp_in_grad = mlp_in_grad + jnp.einsum(
        "cd,ck->dk", cls_low_mlp, cls_hidden_grad, preferred_element_type=jnp.float32
    )
    normed_grad, cls_normed_grad = input_back(hidden_grad, cls_hidden_grad, mlp_in)
    gain_mlp_part = jnp.sum(normed_grad * scaled_mlp, axis=row_axes) + share * jnp.sum(
        cls_normed_grad * cls_scaled_mlp, axis=0
    )
    second_grad = upstream + norm_backward(normed_grad, gain_mlp, scaled_mlp, factor_mlp)
    cls_second_grad = cls_upstream + norm_backward(
        cls_normed_grad, gain_mlp, cls_scaled_mlp, cls_factor_mlp
    )
    space_grad = (keep_float * second_grad).astype(jnp.bfloat16)
    full_space_grad = gather_grads(space_grad)
    cls_space_grad = cls_second_grad.astype(jnp.bfloat16)
    proj_space_grad = jnp.einsum(
        "cfpk,cfpd->kd", flat_space, full_space_grad, preferred_element_type=jnp.float32
    )
    proj_space_grad = (
        proj_space_grad
        + jnp.einsum("ck,cd->kd", flat_cls, cls_space_grad, preferred_element_type=jnp.float32)
    ).reshape(proj_space.shape)
    mixed_grad = jnp.einsum(
        "cfpd,kd->cfpk", full_space_grad, proj_space_flat, preferred_element_type=jnp.float32
    )
    mixed_grad = mixed_grad.astype(jnp.bfloat16).reshape(
        clips, frames, count, heads_here, head_size
    )
    cls_mixed_grad = jnp.einsum(
        "cd,kd->ck", cls_space_grad, proj_space_flat, preferred_element_type=jnp.float32
    )
    cls_mixed_grad = cls_mixed_grad.astype(jnp.bfloat16).reshape(clips, heads_here, head_size)
    triple_grads, cls_triple_grads = space_attention_back(
        triple_space[..., 0, :],
        triple_space[..., 1, :],
        triple_space[..., 2, :],
        cls_triple[..., 0, :],
        cls_triple[..., 1, :],
        cls_triple[..., 2, :],
        key_ok,
        scaling,
        log_space,
        log_cls,
        mixed_grad,
        cls_mixed_grad,
    )
    flat_triple_grads = triple_grads.reshape(clips, frames, count, -1)
    cls_flat_grads = cls_triple_grads.reshape(clips, -1)
    qkv_space_grad = jnp.einsum(
        "cfpd,cfpk->dk", full_space, flat_triple_grads, preferred_element_type=jnp.float32
    )
    qkv_space_grad = (
        qkv_space_grad
        + jnp.einsum("cd,ck->dk", cls_low_space, cls_flat_grads, preferred_element_type=jnp.float32)
    ).reshape(qkv_space.shape)
    normed_grad, cls_normed_grad = input_back(flat_triple_grads, cls_flat_grads, qkv_space)
    gain_space_part = jnp.sum(normed_grad * scaled_space, axis=row_axes) + share * jnp.sum(
        cls_normed_grad * cls_scaled_space, axis=0
    )
    first_grad = second_grad + norm_backward(normed_grad, gain_space, scaled_space, factor_space)
    cls_grad = cls_second_grad + norm_backward(
        cls_normed_grad, gain_space, cls_scaled_space, cls_factor_space
    )
    time_grad = (keep_float * first_grad).astype(jnp.bfloat16)
    temporal_fc_part = jnp.einsum(
        "cfpd,cfpe->de", attended, time_grad, preferred_element_type=jnp.float32
    )
    attended_grad = jnp.einsum(
        "cfpe,de->cfpd", time_grad, temporal_fc, preferred_element_type=jnp.float32
    ).astype(jnp.bfloat16)
    full_attended_grad = gather_grads(attended_grad)
    proj_time_grad = jnp.einsum(
        "cfpk,cfpd->kd", flat_mixed, full_attended_grad, preferred_element_type=jnp.float32
    ).reshape(proj_time.shape)
    mixed_time_grad = jnp.einsum(
        "cfpd,kd->cfpk", full_attended_grad, proj_time_flat, preferred_element_type=jnp.float32
    )
    mixed_time_grad = mixed_time_grad.astype(jnp.bfloat16).reshape(
        clips, frames, count, heads_here, head_size
    )
    time_triple_grads = time_attention_back(
        triple_time[..., 0, :],
        triple_time[..., 1, :],
        triple_time[..., 2, :],
        allowed_time,
        scaling,
        log_time,
        mixed_time_grad,
    )
    flat_time_grads = time_triple_grads.reshape(clips, frames, count, -1)
    qkv_time_grad = jnp.einsum(
        "cfpd,cfpk->dk", full_time, flat_time_grads, preferred_element_type=jnp.float32
    ).reshape(qkv_time.shape)
    normed_grad, ignored = input_back(flat_time_grads, None, qkv_time)
    gain_time_part = jnp.sum(normed_grad * scaled_time, axis=row_axes)
    input_grad = first_grad + norm_backward(normed_grad, gain_time, scaled_time, factor_time)
    qkv_time_grad, proj_time_grad, qkv_space_grad, proj_space_grad, mlp_in_grad, mlp_out_grad = (
        lax.psum(
            (
                qkv_time_grad,
                proj_time_grad,
                qkv_space_grad,
                proj_space_grad,
                mlp_in_grad,
                mlp_out_grad,
            ),
            "clip",
        )
    )
    gain_time_grad, gain_space_grad, gain_mlp_grad, temporal_fc_grad = lax.psum(
        (gain_time_part, gain_space_part, gain_mlp_part, temporal_fc_part), ("clip", "head")
    )
    return (
        output,
        output_cls,
        input_grad,
        cls_grad,
        gain_time_grad,
        qkv_time_grad,
        proj_time_grad,
        temporal_fc_grad,
        gain_space_grad,
        qkv_space_grad,
        proj_space_grad,
        gain_mlp_grad,
        mlp_in_grad,
        mlp_out_grad,
    )


def solution(mesh):
    in_specs = (
        P("clip", None, "head", None),
        P("clip", None),
        P("clip", None, None),
        P(),
        P(None, "head", None, None),
        P("head", None, None),
        P(),
        P(),
        P(None, "head", None, None),
        P("head", None, None),
        P(),
        P(None, "head"),
        P("head", None),
        P("clip", None, "head", None),
        P("clip", None),
    )
    out_specs = (
        P("clip", None, "head", None),
        P("clip", None),
        P("clip", None, "head", None),
        P("clip", None),
        P(),
        P(None, "head", None, None),
        P("head", None, None),
        P(),
        P(),
        P(None, "head", None, None),
        P("head", None, None),
        P(),
        P(None, "head"),
        P("head", None),
    )
    return jax.shard_map(local, mesh=mesh, in_specs=in_specs, out_specs=out_specs, check_vma=False)
```

profile of v0, /device:TPU:0, one launch (start us, length us, event | category | flops | bytes accessed | tf_op | source)
XLA Modules:
  0.0 1033.7 jit_solution(6160047714941582970)
XLA Ops:
  12.6 27.0 %all-gather.8.cloned.1.call-done = bf16[1,8,196,768]{3,1,0,2:T(8,128)(2,1)} async-done(((bf16[1,8,49,768]{3,1,0,2:T(8,128)(2,1)}), bf16[1,8,196,768]{3,1,0,2:T(8,128)(2,1)}) %all-gather.8.cloned.1.call-update) | async-done | bytes 2408464 | tf_op jit(solution)/shard_map/all_gather | solution.py:40
  73.5 47.9 %reduce-scatter.11.cloned.1.call-done = f32[1,8,49,768]{3,1,0,2:T(8,128)} async-done(((f32[1,8,196,768]{3,1,0,2:T(8,128)}), f32[1,8,49,768]{3,1,0,2:T(8,128)}) %reduce-scatter.11.cloned.1.call-update) | async-done | bytes 1204240 | tf_op jit(solution)/shard_map/reduce_scatter | solution.py:48
  130.7 19.7 %all-gather.10.cloned.1.call-done = bf16[1,8,196,768]{3,1,0,2:T(8,128)(2,1)} async-done(((bf16[1,8,49,768]{3,1,0,2:T(8,128)(2,1)}), bf16[1,8,196,768]{3,1,0,2:T(8,128)(2,1)}) %all-gather.10.cloned.1.call-update) | async-done | bytes 2408464 | tf_op jit(solution)/shard_map/all_gather | solution.py:40
  150.4 5.4 fusion.54
  165.7 6.4 copy.413
  189.0 33.5 %reduce-scatter.13.cloned.1.call-done = bf16[1,8,49,768]{3,1,0,2:T(8,128)(2,1)} async-done(((bf16[1,8,196,768]{3,1,0,2:T(8,128)(2,1)}), bf16[1,8,49,768]{3,1,0,2:T(8,128)(2,1)}) %reduce-scatter.13.cloned.1.call-update) | async-done | bytes 602128 | tf_op jit(solution)/shard_map/reduce_scatter | solution.py:53
  228.8 10.7 %reduce-scatter.17.cloned.1.call-start = ((), (), s32[]{:S(2)}) async-start(), calls=%async_computation.13 | async-start | bytes 3010560 | tf_op jit(solution)/shard_map/reduce_scatter | solution.py:80
  239.5 11.7 %all-gather.12.cloned.1.call-done = bf16[1,8,196,768]{3,1,0,2:T(8,128)(2,1)} async-done(((bf16[1,8,49,768]{3,1,0,2:T(8,128)(2,1)}), bf16[1,8,196,768]{3,1,0,2:T(8,128)(2,1)}) %all-gather.12.cloned.1.call-update) | async-done | bytes 2408464 | tf_op jit(solution)/shard_map/all_gather | solution.py:40
  251.2 5.5 fusion.138
  258.9 12.1 %multiply_convert_fusion = (bf16[8,196,768]{2,1,0:T(8,128)(2,1)}, f32[8,196,768]{2,1,0:T(8,128)}) fusion(f32[8,196,768]{2,1,0:T(8,128)S(1)} %get-tuple-element.224, u8[196,768]{1,0:T(8,128)(4,1)S(1)} %get-tuple-element.141, u8[196,768]{1,0:T(8,128)(4,1)S(1)} %get-tuple-element.140), kind=kLoop, calls=%fused_computation.9 | loop fusion | flops 84295680 | bytes 12343296 | tf_op jit(solution)/shard_map/convert_element_type | solution.py:422
  271.0 6.0 all-gather.14.cloned.1.call-done
  277.0 8.6 add_convert_fusion
  305.6 17.8 %reduce-scatter.17.cloned.1.call-done = bf16[1,8,49,768]{3,1,0,2:T(8,128)(2,1)} async-done(((bf16[1,8,196,768]{3,1,0,2:T(8,128)(2,1)}), bf16[1,8,49,768]{3,1,0,2:T(8,128)(2,1)}) %reduce-scatter.17.cloned.1.call-update) | async-done | bytes 602128 | tf_op jit(solution)/shard_map/reduce_scatter | solution.py:80
  329.8 6.5 all-reduce
  343.1 6.9 all-reduce.2
  369.4 6.4 copy.436
  407.5 27.7 %reduce-scatter.19.cloned.1.call-done = bf16[1,8,49,768]{3,1,0,2:T(8,128)(2,1)} async-done(((bf16[1,8,196,768]{3,1,0,2:T(8,128)(2,1)}), bf16[1,8,49,768]{3,1,0,2:T(8,128)(2,1)}) %reduce-scatter.19.cloned.1.call-update) | async-done | bytes 602128 | tf_op jit(solution)/shard_map/reduce_scatter | solution.py:80
  437.4 33.6 %reduce-scatter.15.cloned.1.call-done = bf16[1,8,49,768]{3,1,0,2:T(8,128)(2,1)} async-done(((bf16[1,8,196,768]{3,1,0,2:T(8,128)(2,1)}), bf16[1,8,49,768]{3,1,0,2:T(8,128)(2,1)}) %reduce-scatter.15.cloned.1.call-update) | async-done | bytes 602128 | tf_op jit(solution)/shard_map/reduce_scatter | solution.py:53
  479.7 22.8 %all-gather.18.cloned.1.call-done = bf16[8,196,768]{2,0,1:T(8,128)(2,1)} async-done(((bf16[8,49,768]{2,0,1:T(8,128)(2,1)}), bf16[8,196,768]{2,0,1:T(8,128)(2,1)}) %all-gather.18.cloned.1.call-update) | async-done | bytes 2408464 | tf_op jit(solution)/shard_map/all_gather | solution.py:44
  533.7 6.5 bitcast_add_fusion
  564.5 10.3 all-reduce.6
  587.3 40.7 %all-reduce.4 = (f32[768]{0:T(1024)}, f32[768]{0:T(1024)}, f32[768]{0:T(1024)}) all-reduce(f32[768]{0:T(1024)S(1)} %get-tuple-element.146, f32[768]{0:T(1024)S(1)} %add.259, f32[768]{0:T(1024)S(1)} %add.262), channel_id=1, replica_groups=mesh['clip'=8,'head'=4] {'clip','head'}, use_global_device_ids=true, to_apply=%region_43.44 | all-reduce | flops 2304 | bytes 18432 | tf_op jit(solution)/shard_map/psum | solution.py:559
  628.0 78.4 %all-reduce.10.cloned.1.call-done = f32[768,768]{1,0:T(8,128)} async-done(((f32[768,768]{1,0:T(8,128)}), f32[768,768]{1,0:T(8,128)}) %all-reduce.10.cloned.1.call-update) | async-done | bytes 2359312 | tf_op jit(solution)/shard_map/psum | solution.py:559
  706.4 307.7 %all-reduce.12.cloned.1.call-done = (f32[768,3,3,64]{0,3,2,1:T(8,128)}, f32[3,64,768]{2,1,0:T(8,128)}, f32[768,3,3,64]{0,3,2,1:T(8,128)}, f32[3,64,768]{2,1,0:T(...) async-done(((f32[768,3,3,64]{0,3,2,1:T(8,128)}, f32[3,64,768]{2,1,0:T(8,128)}, f32[768,3,3,64]{0,3,2,1:T(8,128)}, f32[3,64,768]{2,1,0:T(8,128)}, f32[768,768]{1,0:T(8,128)}, ...) | async-done | bytes 9437200 | tf_op jit(solution)/shard_map/psum | solution.py:547
  (517 shorter events, 252.8 us)
Async XLA Ops:
  7.2 244.0 %copy-start = (bf16[768,768]{1,0:T(8,128)(2,1)S(1)}, bf16[768,768]{1,0:T(8,128)(2,1)}, u32[]{:S(2)}) copy-start(bf16[768,768]{1,0:T(8,128)(2,1)} %param.26) | copy-start | bytes 3538948
  7.2 32.4 %copy-start.126 = (bf16[768,3,3,64]{0,3,2,1:T(8,128)(2,1)S(1)}, bf16[768,3,3,64]{0,3,2,1:T(8,128)(2,1)}, u32[]{:S(2)}) copy-start(bf16[768,3,3,64]{0,3,2,1:T(8,128)(2,1)} %param.19) | copy-start | bytes 2654212
  7.2 32.4 %all-gather.8.cloned.1.call-start = ((), (), s32[]{:S(2)}) async-start(), calls=%async_computation.6 | async-start | bytes 3010560 | tf_op jit(solution)/shard_map/all_gather | solution.py:40
  12.4 108.9 %reduce-scatter.11.cloned.1.call-start = ((), (), s32[]{:S(2)}) async-start(), calls=%async_computation.7 | async-start | bytes 6021120 | tf_op jit(solution)/shard_map/reduce_scatter | solution.py:48
  72.7 50.0 %copy-start.5 = (bf16[1,8,49,768]{3,1,2,0:T(8,128)(2,1)S(1)}, bf16[1,8,49,768]{3,1,2,0:T(8,128)(2,1)}, u32[]{:S(2)}) copy-start(bf16[1,8,49,768]{3,1,2,0:T(8,128)(2,1)} %param.15) | copy-start | bytes 1806340
  72.7 50.0 %copy-start.124 = (bf16[768,768]{1,0:T(8,128)(2,1)S(1)}, bf16[768,768]{1,0:T(8,128)(2,1)}, u32[]{:S(2)}) copy-start(bf16[768,768]{1,0:T(8,128)(2,1)} %param.21) | copy-start | bytes 3538948
  72.7 77.7 %all-gather.10.cloned.1.call-start = ((), (), s32[]{:S(2)}) async-start(), calls=%async_computation.8 | async-start | bytes 3010560 | tf_op jit(solution)/shard_map/all_gather | solution.py:40
  73.5 50.1 %copy-start.84 = (f32[8,49]{1,0:T(8,128)}, f32[8,49]{1,0:T(8,128)S(1)}, u32[]{:S(2)}) copy-start(f32[8,49]{1,0:T(8,128)S(1)} %convert_bitcast_fusion.12) | copy-start | bytes 4708
  125.9 96.6 %reduce-scatter.13.cloned.1.call-start = ((), (), s32[]{:S(2)}) async-start(), calls=%async_computation.9 | async-start | bytes 3010560 | tf_op jit(solution)/shard_map/reduce_scatter | solution.py:53
  188.9 33.6 %copy-start.14 = (bf16[1,8,49,768]{3,1,2,0:T(8,128)(2,1)S(1)}, bf16[1,8,49,768]{3,1,2,0:T(8,128)(2,1)}, u32[]{:S(2)}) copy-start(bf16[1,8,49,768]{3,1,2,0:T(8,128)(2,1)} %param.28) | copy-start | bytes 1806340
  188.9 33.6 %copy-start.85 = (f32[8,49]{1,0:T(8,128)S(1)}, f32[8,49]{1,0:T(8,128)}, u32[]{:S(2)}) copy-start(f32[8,49]{1,0:T(8,128)} %copy-done.84) | copy-start | bytes 4708
  189.0 36.5 %copy-start.66 = (f32[768]{0:T(1024)S(1)}, f32[768]{0:T(1024)}, u32[]{:S(2)}) copy-start(f32[768]{0:T(1024)} %param.25) | copy-start | bytes 9220
  189.0 62.2 %all-gather.12.cloned.1.call-start = ((), (), s32[]{:S(2)}) async-start(), calls=%async_computation.10 | async-start | bytes 3010560 | tf_op jit(solution)/shard_map/all_gather | solution.py:40
  226.7 50.3 %all-gather.14.cloned.1.call-start = ((), (), s32[]{:S(2)}) async-start(), calls=%async_computation.12 | async-start | bytes 3010560 | tf_op jit(solution)/shard_map/all_gather | solution.py:44
  228.8 94.6 %reduce-scatter.17.cloned.1.call-start = ((), (), s32[]{:S(2)}) async-start(), calls=%async_computation.13 | async-start | bytes 3010560 | tf_op jit(solution)/shard_map/reduce_scatter | solution.py:80
  289.8 71.6 %all-gather.16.cloned.1.call-start = ((), (), s32[]{:S(2)}) async-start(), calls=%async_computation.14 | async-start | bytes 3010560 | tf_op jit(solution)/shard_map/all_gather | solution.py:44
  327.4 107.8 %reduce-scatter.19.cloned.1.call-start = ((), (), s32[]{:S(2)}) async-start(), calls=%async_computation.15 | async-start | bytes 3010560 | tf_op jit(solution)/shard_map/reduce_scatter | solution.py:80
  364.0 29.6 %copy-start.29 = (bf16[8,196,192]{1,2,0:T(8,128)(2,1)}, bf16[8,196,192]{1,2,0:T(8,128)(2,1)S(1)}, u32[]{:S(2)}) copy-start(bf16[8,196,192]{1,2,0:T(8,128)(2,1)S(1)} %fusion.99) | copy-start | bytes 1806340
  400.5 70.5 %reduce-scatter.15.cloned.1.call-start = ((), (), s32[]{:S(2)}) async-start(), calls=%async_computation.11 | async-start | bytes 3010560 | tf_op jit(solution)/shard_map/reduce_scatter | solution.py:53
  407.4 63.6 %copy-start.16 = (bf16[1,8,49,768]{3,1,0,2:T(8,128)(2,1)S(1)}, bf16[1,8,49,768]{3,1,0,2:T(8,128)(2,1)}, u32[]{:S(2)}) copy-start(bf16[1,8,49,768]{3,1,0,2:T(8,128)(2,1)} %reduce-scatter.17.cloned.1.call-done) | copy-start | bytes 1806340
  407.5 95.0 %all-gather.18.cloned.1.call-start = ((), (), s32[]{:S(2)}) async-start(), calls=%async_computation.18 | async-start | bytes 3010560 | tf_op jit(solution)/shard_map/all_gather | solution.py:44
  477.9 104.4 %reduce-scatter.21.cloned.1.call-start = ((), (), s32[]{:S(2)}) async-start(), calls=%async_computation.16 | async-start | bytes 3010560 | tf_op jit(solution)/shard_map/reduce_scatter | solution.py:71
  532.2 174.3 %all-reduce.10.cloned.1.call-start = ((), (), s32[]{:S(2)}) async-start(), calls=%async_computation.17 | async-start | bytes 4718592 | tf_op jit(solution)/shard_map/psum | solution.py:559
  547.7 466.4 %all-reduce.12.cloned.1.call-start = ((), (), s32[]{:S(2)}) async-start(), calls=%async_computation.19 | async-start | bytes 18874368 | tf_op jit(solution)/shard_map/psum | solution.py:547
  (125 other events, 723.8 us)
Sparse Core Ops, SparseCore 0:
  12.5 27.0 all-gather.7
  72.9 48.4 reduce-scatter.10
  126.0 24.3 all-gather.9
  189.1 33.3 reduce-scatter.12
  226.8 24.3 all-gather.11
  252.6 24.3 all-gather.13
  290.0 33.3 reduce-scatter.16
  327.5 24.5 all-gather.15
  400.6 34.5 reduce-scatter.18
  437.6 33.3 reduce-scatter.14
  478.0 24.3 all-gather.17
  532.3 33.3 reduce-scatter.20
  571.3 135.1 all-reduce.9
  713.4 300.6 all-reduce.11
where the time goes:
time: 1040 us; the launch traced here: 1030 us
  waiting for transfers between devices  634 us (61%)
  matrix products  114 us (11%)
  local copies, waits for them, and re-layouts  105 us (10%)
  other arithmetic  83.1 us (8%)
  blocking collectives  64.5 us (6%)
  between operations  21.3 us (2%)
  starting transfers between devices  12.1 us (1%)
    psum x1, waiting for transfers between devices, local(): lax.psum((qkv_time_grad, proj_time_grad, qkv_space_grad, proj_space_grad,...  308 us
    psum x1, waiting for transfers between devices, local(): lax.psum((gain_time_part, gain_space_part, gain_mlp_part, temporal_fc_par...  78.4 us
    reduce_scatter x2, waiting for transfers between devices, branch_sum(): lax.psum_scatter(partial_rows.astype(jnp.bfloat16), 'head', scatter_dimen...  67 us
    all_gather x3, waiting for transfers between devices, gather_rows(): return lax.all_gather(shard, 'head', axis=2, tiled=True)  58.4 us
    reduce_scatter x1, waiting for transfers between devices, time_sum(): lax.psum_scatter(partial_rows, 'head', scatter_dimension=2, tiled=True)  47.9 us
    reduce_scatter x3, waiting for transfers between devices, input_back(): lax.psum_scatter(partial_rows.astype(jnp.bfloat16), 'head', scatter_dimen...  45.5 us
    psum x1, blocking collectives, local(): lax.psum((gain_time_part, gain_space_part, gain_mlp_part, temporal_fc_par...  40.7 us
    unnamed x286, local copies, waits for them, and re-layouts  34.9 us
  transfers between devices with their start and end apart: 14, of which 12 were waited for; matrix products, arithmetic and copies ran while one was open for 10% of the time, Pallas kernels for 0%

commit v1 on v0

v1 whole, which is shorter than its diff:
```python
from functools import partial

import jax
import jax.numpy as jnp
from jax import lax
from jax.experimental import pallas as pl
from jax.experimental.pallas import tpu as pltpu
from jax.sharding import PartitionSpec as P

EPSILON = 1e-06
NEGATIVE = -1e30
F32 = jnp.float32
BF16 = jnp.bfloat16


def nn(a, b):
    return lax.dot_general(a, b, (((1,), (0,)), ((), ())), preferred_element_type=F32)


def nt(a, b):
    return lax.dot_general(a, b, (((1,), (1,)), ((), ())), preferred_element_type=F32)


def tn(a, b):
    return lax.dot_general(a, b, (((0,), (0,)), ((), ())), preferred_element_type=F32)


def tiles(total, size, body):
    def step(i, carry):
        body(pl.multiple_of(i * size, size))
        return carry

    lax.fori_loop(0, total // size, step, 0)


def stats(x):
    center = x - jnp.mean(x, axis=-1, keepdims=True)
    factor = lax.rsqrt(jnp.mean(center * center, axis=-1, keepdims=True) + EPSILON)
    return center * factor, factor


def norm_back(grad, gain, scaled, factor):
    weighted = grad * gain
    inner = weighted - jnp.mean(weighted, axis=-1, keepdims=True)
    return factor * (inner - scaled * jnp.mean(weighted * scaled, axis=-1, keepdims=True))


def pair_masks():
    lane = lax.broadcasted_iota(jnp.int32, (1, 128), 1)
    return (lane < 64).astype(F32).astype(BF16), (lane >= 64).astype(F32).astype(BF16)


def stacked(x):
    low, high = pair_masks()
    return jnp.concatenate([x * low, x * high], axis=0)


def unstacked(x):
    rows = x.shape[0] // 2
    lane = lax.broadcasted_iota(jnp.int32, (1, 128), 1)
    return jnp.where(lane < 64, x[:rows], x[rows:])


def norm_rows(x_ref, gain_ref, u_ref, chunk):
    def body(r):
        rows = pl.ds(r, chunk)
        scaled, _ = stats(x_ref[rows, :])
        u_ref[rows, :] = (scaled * gain_ref[...]).astype(BF16)

    tiles(x_ref.shape[0], chunk, body)


def project_qkv(u_ref, wt_ref, qkv_ref):
    width = u_ref.shape[1]

    def body(n):
        scale = jnp.where(n < width, 0.125, 1.0)
        out = nt(u_ref[...], wt_ref[pl.ds(n, 256), :]) * scale
        qkv_ref[:, pl.ds(n, 256)] = out.astype(BF16)

    tiles(wt_ref.shape[0], 256, body)


def qkv_grad_and_back(dqkv_ref, u_ref, wt_ref, dwt_ref, du_ref):
    def grad(n):
        dwt_ref[pl.ds(n, 256), :] = tn(dqkv_ref[:, pl.ds(n, 256)], u_ref[...]).astype(BF16)

    tiles(dqkv_ref.shape[1], 256, grad)

    def back(n):
        du_ref[:, pl.ds(n, 256)] = nn(dqkv_ref[...], wt_ref[:, pl.ds(n, 256)])

    tiles(u_ref.shape[1], 256, back)


def softmax(scores):
    highest = jnp.max(scores, axis=-1, keepdims=True)
    weights = jnp.exp(scores - highest)
    return weights * (1.0 / jnp.sum(weights, axis=-1, keepdims=True))


def attention(qkv_ref, p_ref, mix_ref, groups, bias_of):
    width = mix_ref.shape[1]

    def body(c):
        hp = c // 128
        for g, (start, size) in enumerate(groups):
            rows = pl.ds(start, size)
            q = qkv_ref[rows, pl.ds(c, 128)]
            k = qkv_ref[rows, pl.ds(pl.multiple_of(width + c, 128), 128)]
            v = qkv_ref[rows, pl.ds(pl.multiple_of(2 * width + c, 128), 128)]
            prob = softmax(nt(stacked(q), k) + bias_of(g, size))
            p_ref[hp, g, : 2 * size, :size] = prob
            mix_ref[rows, pl.ds(c, 128)] = unstacked(nn(prob.astype(BF16), v)).astype(BF16)

    tiles(width, 128, body)


def attention_back(qkv_ref, p_ref, dmix_ref, dqkv_ref, groups):
    width = dmix_ref.shape[1]

    def body(c):
        hp = c // 128
        kc = pl.multiple_of(width + c, 128)
        vc = pl.multiple_of(2 * width + c, 128)
        for g, (start, size) in enumerate(groups):
            rows = pl.ds(start, size)
            q = qkv_ref[rows, pl.ds(c, 128)]
            k = qkv_ref[rows, pl.ds(kc, 128)]
            v = qkv_ref[rows, pl.ds(vc, 128)]
            up = stacked(dmix_ref[rows, pl.ds(c, 128)])
            prob = p_ref[hp, g, : 2 * size, :size]
            dprob = nt(up, v)
            delta = jnp.sum(prob * dprob, axis=-1, keepdims=True)
            dscore = (prob * (dprob - delta)).astype(BF16)
            dqkv_ref[rows, pl.ds(c, 128)] = (unstacked(nn(dscore, k)) * 0.125).astype(BF16)
            dqkv_ref[rows, pl.ds(kc, 128)] = tn(dscore, stacked(q)).astype(BF16)
            dqkv_ref[rows, pl.ds(vc, 128)] = tn(prob.astype(BF16), up).astype(BF16)

    tiles(width, 128, body)


T_ROWS = 400
T_GROUPS = ((0, 96), (96, 96), (192, 96), (288, 112))


def time_bias(krow_ref):
    def bias_of(g, size):
        row = lax.broadcasted_iota(jnp.int32, (size, size), 0)
        col = lax.broadcasted_iota(jnp.int32, (size, size), 1)
        same = (row // 8) == (col // 8)
        kept = jnp.broadcast_to(krow_ref[g, :, :size], (size, size)) > 0.0
        ok = same & (kept | (row == col))
        bias = jnp.where(ok, 0.0, NEGATIVE)
        return jnp.concatenate([bias, bias], axis=0)

    return bias_of


def to_patch_order(src_ref, dst_ref, perm_ref):
    frames, count, width = src_ref.shape
    used = frames * count
    for j in range(width // 128):
        for f in range(frames):
            perm_ref[j, pl.ds(f, count, stride=frames), :] = src_ref[f, :, j * 128 : (j + 1) * 128].astype(F32)
        dst_ref[:used, j * 128 : (j + 1) * 128] = perm_ref[j, :used, :]
    dst_ref[used:, :] = jnp.zeros((T_ROWS - used, width), F32)


def to_frame_order(src_ref, dst_ref, perm_ref):
    frames, count, width = dst_ref.shape
    for j in range(width // 128):
        perm_ref[j, :, :] = src_ref[:, j * 128 : (j + 1) * 128]
        for f in range(frames):
            out = perm_ref[j, pl.ds(f, count, stride=frames), :]
            dst_ref[f, :, j * 128 : (j + 1) * 128] = out.astype(dst_ref.dtype)


def time_forward(
    patches_ref, krow_ref, kcol_ref, gain_ref, wt_ref, proj_ref, fc_ref,
    send_ref, u_ref, qkv_ref, p_ref, mix_ref, att_ref, x_ref, first_ref, perm_ref,
):
    width = patches_ref.shape[2]
    to_patch_order(patches_ref, x_ref, perm_ref)
    norm_rows(x_ref, gain_ref, u_ref, 80)
    project_qkv(u_ref, wt_ref, qkv_ref)
    attention(qkv_ref, p_ref, mix_ref, T_GROUPS, time_bias(krow_ref))

    def project(n):
        att_ref[:, pl.ds(n, 256)] = nn(mix_ref[...], proj_ref[:, pl.ds(n, 256)]).astype(BF16)

    tiles(width, 256, project)

    def branch(n):
        cols = pl.ds(n, 256)
        first_ref[:, cols] = x_ref[:, cols] + kcol_ref[...] * nn(att_ref[...], fc_ref[:, cols])

    tiles(width, 256, branch)
    to_frame_order(first_ref, send_ref, perm_ref)


def time_backward(
    dfirst_ref, patches_ref, kcol_ref, gain_ref, wt_ref, proj_ref, fc_ref, u_ref, qkv_ref, p_ref, mix_ref, att_ref,
    dx_ref, dwt_ref, dproj_ref, dfc_ref, dgain_ref,
    x_ref, df_ref, low_ref, datt_ref, dmix_ref, dqkv_ref, du_ref, perm_ref,
):
    width = patches_ref.shape[2]
    to_patch_order(patches_ref, x_ref, perm_ref)
    to_patch_order(dfirst_ref, df_ref, perm_ref)
    low_ref[...] = (df_ref[...] * kcol_ref[...]).astype(BF16)

    def first(n):
        cols = pl.ds(n, 256)
        dfc_ref[cols, :] = tn(att_ref[:, cols], low_ref[...]).astype(BF16)
        datt_ref[:, cols] = nt(low_ref[...], fc_ref[cols, :]).astype(BF16)

    tiles(width, 256, first)

    def second(n):
        cols = pl.ds(n, 256)
        dproj_ref[cols, :] = tn(mix_ref[:, cols], datt_ref[...]).astype(BF16)
        dmix_ref[:, cols] = nt(datt_ref[...], proj_ref[cols, :]).astype(BF16)

    tiles(width, 256, second)
    attention_back(qkv_ref, p_ref, dmix_ref, dqkv_ref, T_GROUPS)
    qkv_grad_and_back(dqkv_ref, u_ref, wt_ref, dwt_ref, du_ref)
    dgain_ref[...] = jnp.zeros_like(dgain_ref)

    def finish(r):
        rows = pl.ds(r, 80)
        scaled, factor = stats(x_ref[rows, :])
        grad = du_ref[rows, :]
        dgain_ref[...] += jnp.sum(grad * scaled, axis=0, keepdims=True)
        df_ref[rows, :] += norm_back(grad, gain_ref[...], scaled, factor)

    tiles(T_ROWS, 80, finish)
    to_frame_order(df_ref, dx_ref, perm_ref)


SEG = 208
S_ROWS = 416
S_GROUPS = ((0, 208), (208, 208))


def gather_frames(got_ref, cls_row, out_ref, sources, count):
    for f in range(2):
        base = f * SEG
        for s in range(sources):
            out_ref[base + s * count : base + (s + 1) * count, :] = got_ref[2 * s + f].astype(F32)
        at = base + sources * count
        out_ref[at : at + 1, :] = cls_row[f]
        out_ref[at + 1 : base + SEG, :] = jnp.zeros((SEG - 1 - sources * count, out_ref.shape[1]), F32)


def scatter_frames(x_ref, send_ref, sources, count):
    for f in range(2):
        for s in range(sources):
            at = f * SEG + s * count
            send_ref[2 * s + f] = x_ref[at : at + count, :].astype(send_ref.dtype)


def space_bias(krow_ref):
    def bias_of(g, size):
        bias = (krow_ref[g, :, :size] - 1.0) * -NEGATIVE
        return bias

    return bias_of


def space_forward(got_ref, cls_ref, krow_ref, gain_ref, wt_ref, x_ref, u_ref, qkv_ref, p_ref, mix_ref, cls_part_ref):
    sources, count = got_ref.shape[0] // 2, got_ref.shape[1]
    cls_row = cls_ref[...].astype(F32)
    gather_frames(got_ref, (cls_row, cls_row), x_ref, sources, count)
    norm_rows(x_ref, gain_ref, u_ref, 208)
    project_qkv(u_ref, wt_ref, qkv_ref)
    width = u_ref.shape[1]
    heads = width // 64
    at = sources * count
    lane = lax.broadcasted_iota(jnp.int32, (16, width), 1) // 64
    own = (lane == lax.broadcasted_iota(jnp.int32, (16, width), 0)).astype(F32)
    total = jnp.zeros((1, width), F32)
    for f in range(2):
        q = qkv_ref[f * SEG + at : f * SEG + at + 1, :width].astype(F32)
        k = qkv_ref[f * SEG : (f + 1) * SEG, width : 2 * width]
        v = qkv_ref[f * SEG : (f + 1) * SEG, 2 * width :]
        prob = softmax(nt((own * q).astype(BF16), k) + krow_bias(krow_ref, f))
        total += jnp.sum(own * nn(prob.astype(BF16), v), axis=0, keepdims=True)
    cls_part_ref[...] = total
    attention(qkv_ref, p_ref, mix_ref, S_GROUPS, lambda g, size: krow_bias(krow_ref, g))


def krow_bias(krow_ref, g):
    return (krow_ref[g, :, :SEG] - 1.0) * (-NEGATIVE)


def space_project(mix_ref, cls_total, x_ref, kcol_ref, proj_ref, second_ref, at):
    width = mix_ref.shape[1]
    rows = mix_ref[192:208, :]
    pick = lax.broadcasted_iota(jnp.int32, (16, 1), 0) == (at - 192)
    mix_ref[192:208, :] = jnp.where(pick, jnp.broadcast_to(cls_total, (16, width)), rows.astype(F32)).astype(BF16)

    def project(n):
        cols = pl.ds(n, 256)
        second_ref[:, cols] = x_ref[:, cols] + kcol_ref[...] * nn(mix_ref[...], proj_ref[:, cols])

    tiles(width, 256, project)


def mlp_stage(
    second_ref, cot_ref, kcol_ref, once_ref, gain_ref, w1_ref, w2_ref,
    out_ref, dsecond_ref, dw1_ref, dw2_ref, dgain_ref,
    u_ref, uw_ref, dz_ref, dzw_ref, acc_ref, du_ref,
):
    def prepare(r):
        rows = pl.ds(r, 208)
        scaled, _ = stats(second_ref[rows, :])
        u = (scaled * gain_ref[...]).astype(BF16)
        u_ref[rows, :] = u
        uw_ref[rows, :] = (u.astype(F32) * once_ref[rows, :]).astype(BF16)
        dz = cot_ref[rows, :] * kcol_ref[rows, :]
        dz_ref[rows, :] = dz.astype(BF16)
        dzw_ref[rows, :] = (dz * once_ref[rows, :]).astype(BF16)

    tiles(S_ROWS, 208, prepare)
    acc_ref[...] = jnp.zeros_like(acc_ref)
    du_ref[...] = jnp.zeros_like(du_ref)
    shard = w1_ref.shape[2]
    per = shard // 256

    def step(i, carry):
        s = i // per
        n = pl.multiple_of((i % per) * 256, 256)
        cols = pl.ds(n, 256)
        w1 = w1_ref[s, :, cols]
        w2 = w2_ref[s, cols, :]
        hid = nn(u_ref[...], w1)
        phi = 0.5 + 0.5 * lax.erf(hid * 0.7071067811865476)
        act = (hid * phi).astype(BF16)
        slope = phi + hid * (0.3989422804014327 * jnp.exp(hid * hid * -0.5))
        acc_ref[...] += nn(act, w2)
        dhid = (nt(dz_ref[...], w2) * slope).astype(BF16)
        dw2_ref[s, cols, :] = tn(act, dzw_ref[...]).astype(BF16)
        dw1_ref[s, :, cols] = tn(uw_ref[...], dhid).astype(BF16)
        du_ref[...] += nt(dhid, w1)
        return carry

    lax.fori_loop(0, w1_ref.shape[0] * per, step, 0)
    dgain_ref[...] = jnp.zeros_like(dgain_ref)

    def finish(r):
        rows = pl.ds(r, 208)
        x = second_ref[rows, :]
        scaled, factor = stats(x)
        out_ref[rows, :] = x + kcol_ref[rows, :] * acc_ref[rows, :]
        grad = du_ref[rows, :]
        dgain_ref[...] += jnp.sum(grad * scaled * once_ref[rows, :], axis=0, keepdims=True)
        dsecond_ref[rows, :] = cot_ref[rows, :] + norm_back(grad, gain_ref[...], scaled, factor)

    tiles(S_ROWS, 208, finish)


def space_backward(
    dsecond_ref, kcol_ref, once_ref, gain_ref, wt_ref, proj_ref, x_ref, u_ref, qkv_ref, p_ref, mix_ref,
    dfirst_ref, dwt_ref, dproj_ref, dgain_ref, dcls_ref,
    low_ref, loww_ref, dmix_ref, dqkv_ref, du_ref, at, frames,
):
    width = mix_ref.shape[1]
    low_ref[...] = (dsecond_ref[...] * kcol_ref[...]).astype(BF16)
    loww_ref[...] = (dsecond_ref[...] * (kcol_ref[...] * once_ref[...])).astype(BF16)
    pick = lax.broadcasted_iota(jnp.int32, (16, 1), 0) == (at - 192)
    cls_grad = jnp.broadcast_to(dsecond_ref[at : at + 1, :], (16, width))
    rest = low_ref[SEG + 192 : SEG + 208, :].astype(F32)
    low_ref[SEG + 192 : SEG + 208, :] = jnp.where(pick, cls_grad, rest).astype(BF16)

    def back(n):
        cols = pl.ds(n, 256)
        dproj_ref[cols, :] = tn(mix_ref[:, cols], loww_ref[...]).astype(BF16)
        dmix_ref[:, cols] = nt(low_ref[...], proj_ref[cols, :]).astype(BF16)

    tiles(width, 256, back)
    for f in range(2):
        rows = pl.ds(f * SEG + 192, 16)
        part = dmix_ref[rows, :].astype(F32)
        dmix_ref[rows, :] = jnp.where(pick, part * (1.0 / frames), part).astype(BF16)
    attention_back(qkv_ref, p_ref, dmix_ref, dqkv_ref, S_GROUPS)
    qkv_grad_and_back(dqkv_ref, u_ref, wt_ref, dwt_ref, du_ref)
    dgain_ref[...] = jnp.zeros_like(dgain_ref)
    dcls_ref[...] = du_ref[at : at + 1, :] + du_ref[SEG + at : SEG + at + 1, :]

    def finish(r):
        rows = pl.ds(r, 208)
        scaled, factor = stats(x_ref[rows, :])
        grad = du_ref[rows, :]
        dgain_ref[...] += jnp.sum(grad * scaled, axis=0, keepdims=True)
        dfirst_ref[rows, :] = dsecond_ref[rows, :] + norm_back(grad, gain_ref[...], scaled, factor)

    tiles(S_ROWS, 208, finish)


VM = pl.BlockSpec(memory_space=pltpu.VMEM)


def call(body, outs, scratch, *args):
    return pl.pallas_call(
        body,
        out_shape=[jax.ShapeDtypeStruct(s, d) for s, d in outs],
        in_specs=[VM] * len(args),
        out_specs=[VM] * len(outs),
        scratch_shapes=[pltpu.VMEM(s, d) for s, d in scratch],
        compiler_params=pltpu.CompilerParams(vmem_limit_bytes=60 << 20),
    )(*args)


def local(
    patches, cls_token, keep_mask, gain_time, qkv_time, proj_time, temporal_fc, gain_space, qkv_space, proj_space,
    gain_mlp, mlp_in, mlp_out, cotangent, cls_cotangent,
):
    _, frames, count, width = patches.shape
    members = lax.axis_size("head")
    me = lax.axis_index("head")
    heads_here, hd = qkv_time.shape[1], qkv_time.shape[3]
    at = members * count

    def swap(x, bit):
        return lax.ppermute(x, "head", [(i, i ^ bit) for i in range(members)])

    def gather(w):
        far = swap(w, 2)
        return jnp.stack([w, swap(w, 1), far, swap(far, 1)])

    def flat_t(w):
        return jnp.transpose(w, (2, 1, 3, 0)).reshape(3, heads_here * hd, width)

    def all_t(w):
        g = gather(flat_t(w))
        return jnp.transpose(g, (1, 0, 2, 3)).reshape(3 * width, width)

    wt_time, wt_space = all_t(qkv_time), all_t(qkv_space)
    pt = gather(proj_time.reshape(-1, width)).reshape(width, width)
    ps = gather(proj_space.reshape(-1, width)).reshape(width, width)
    w1, w2 = gather(mlp_in), gather(mlp_out)
    gt, gs, gm = gain_time[None], gain_space[None], gain_mlp[None]

    keep = keep_mask[0].astype(F32)
    here = lax.dynamic_slice_in_dim(keep, me * count, count, axis=1)
    kt = jnp.pad(here.T.reshape(-1), (0, T_ROWS - frames * count))
    kt_col = kt[:, None]
    kt_row = jnp.stack([jnp.pad(kt[s : s + n], (0, 128 - n)) for s, n in T_GROUPS])[:, None, :]
    mine = lax.dynamic_slice_in_dim(keep, me * 2, 2, axis=0)
    ks_row = jnp.pad(mine, ((0, 0), (0, 256 - at))).at[:, at].set(1.0)[:, None, :]
    first_only = jnp.array([1.0, 0.0], F32)[:, None]
    ks_col = jnp.concatenate([mine, first_only, jnp.zeros((2, SEG - 1 - at), F32)], axis=1).reshape(-1, 1)
    row_id = jnp.arange(S_ROWS)
    once = jnp.where((row_id == at) & (me != 0), 0.0, 1.0).astype(F32)[:, None]

    def exchange(x):
        return lax.all_to_all(x, "head", split_axis=0, concat_axis=0, tiled=True)

    cot = exchange(cotangent[0])
    cls_cot = cls_cotangent.astype(F32)

    send, u_t, qkv_t, p_t, mix_t, att_t = call(
        lambda *r: time_forward(*r[:7], *r[7:]),
        [((frames, count, width), BF16), ((T_ROWS, width), BF16), ((T_ROWS, 3 * width), BF16),
         ((6, 4, 224, 128), F32), ((T_ROWS, width), BF16), ((T_ROWS, width), BF16)],
        [((T_ROWS, width), F32), ((T_ROWS, width), F32), ((width // 128, T_ROWS, 128), F32)],
        patches[0], kt_row, kt_col, gt, wt_time, pt, temporal_fc,
    )
    got = exchange(send)
    x_s, u_s, qkv_s, p_s, mix_s, cls_part = call(
        space_forward,
        [((S_ROWS, width), F32), ((S_ROWS, width), BF16), ((S_ROWS, 3 * width), BF16),
         ((6, 2, 416, 256), F32), ((S_ROWS, width), BF16), ((1, width), F32)],
        [],
        got, cls_token, ks_row, gs, wt_space,
    )
    part = cls_part.reshape(members, -1)
    part = part + swap(part, 1)[jnp.array([1, 0, 3, 2])]
    part = part + swap(part, 2)[jnp.array([2, 3, 0, 1])]
    cls_total = part.reshape(1, width) * (1.0 / frames)

    def mlp_body(mix_ref, tot_ref, x_ref, kcol_ref, once_ref, ps_ref, cot_ref, ccot_ref, gain_ref, w1_ref, w2_ref,
                 out_ref, ocls_ref, dsec_ref, dw1_ref, dw2_ref, dg_ref, mixo_ref,
                 second_ref, cotx_ref, u_ref, uw_ref, dz_ref, dzw_ref, acc_ref, du_ref):
        mixo_ref[...] = mix_ref[...]
        space_project(mixo_ref, tot_ref[...], x_ref, kcol_ref, ps_ref, second_ref, at)
        zero = jnp.zeros((1, width), F32)
        gather_frames(cot_ref, (ccot_ref[...], zero), cotx_ref, members, count)
        mlp_stage(second_ref, cotx_ref, kcol_ref, once_ref, gain_ref, w1_ref, w2_ref,
                  acc_ref, dsec_ref, dw1_ref, dw2_ref, dg_ref, u_ref, uw_ref, dz_ref, dzw_ref, acc_ref, du_ref)
        scatter_frames(acc_ref, out_ref, members, count)
        ocls_ref[...] = acc_ref[at : at + 1, :].astype(BF16)

    out_send, out_cls, dsecond, dw1, dw2, dg_mlp, mix_s = call(
        mlp_body,
        [((frames, count, width), BF16), ((1, width), BF16), ((S_ROWS, width), F32),
         (w1.shape, BF16), (w2.shape, BF16), ((1, width), F32), ((S_ROWS, width), BF16)],
        [((S_ROWS, width), F32), ((S_ROWS, width), F32), ((S_ROWS, width), BF16), ((S_ROWS, width), BF16),
         ((S_ROWS, width), BF16), ((S_ROWS, width), BF16), ((S_ROWS, width), F32), ((S_ROWS, width), F32)],
        mix_s, cls_total, x_s, ks_col, once, ps, cot, cls_cot, gm, w1, w2,
    )
    output = exchange(out_send)

    def sb_body(*r):
        ins, outs, scr = r[:11], r[11:17], r[17:]
        dfs_ref, dcls_ref, dwt_ref, dproj_ref, dg_ref, dc2_ref = outs
        space_backward(*ins, scr[0], dwt_ref, dproj_ref, dg_ref, dcls_ref, *scr[1:], at, frames)
        scatter_frames(scr[0], dfs_ref, members, count)
        dc2_ref[...] = ins[0][at : at + 1, :]

    df_send, dcls_part, dwt_s, dps, dg_space, dcls_second = call(
        sb_body,
        [((frames, count, width), BF16), ((1, width), F32), ((3 * width, width), BF16), ((width, width), BF16),
         ((1, width), F32), ((1, width), F32)],
        [((S_ROWS, width), F32), ((S_ROWS, width), BF16), ((S_ROWS, width), BF16), ((S_ROWS, width), BF16),
         ((S_ROWS, 3 * width), BF16), ((S_ROWS, width), F32)],
        dsecond, ks_col, once, gs, wt_space, ps, x_s, u_s, qkv_s, p_s, mix_s,
    )
    dfirst = exchange(df_send)
    du_cls = lax.psum(dcls_part, "head")
    scaled, factor = stats(cls_token.astype(F32))
    cls_grad = dcls_second + norm_back(du_cls, gs, scaled, factor)

    dx, dwt_t, dpt, dfc, dg_time = call(
        lambda *r: time_backward(*r),
        [((frames, count, width), F32), ((3 * width, width), BF16), ((width, width), BF16), ((width, width), BF16),
         ((1, width), F32)],
        [((T_ROWS, width), F32), ((T_ROWS, width), F32), ((T_ROWS, width), BF16), ((T_ROWS, width), BF16),
         ((T_ROWS, width), BF16), ((T_ROWS, 3 * width), BF16), ((T_ROWS, width), F32),
         ((width // 128, T_ROWS, 128), F32)],
        dfirst, patches[0], kt_col, gt, wt_time, pt, temporal_fc, u_t, qkv_t, p_t, mix_t, att_t,
    )

    def reduce(g):
        pair = g[0::2] + swap(g[1::2], 1)
        own = pair[0] + swap(pair[1], 2)
        return lax.psum(own, "clip").astype(F32)

    def by_shard(dwt):
        return jnp.transpose(dwt.reshape(3, members, -1, width), (1, 0, 2, 3)).reshape(members, -1, width)

    def untie(own):
        return jnp.transpose(own.reshape(3, heads_here, hd, width), (3, 1, 0, 2))

    d_qt = untie(reduce(by_shard(dwt_t)))
    d_qs = untie(reduce(by_shard(dwt_s)))
    d_pt = reduce(dpt.reshape(members, -1, width)).reshape(proj_time.shape)
    d_ps = reduce(dps.reshape(members, -1, width)).reshape(proj_space.shape)
    d_w1, d_w2 = reduce(dw1), reduce(dw2)
    d_fc = lax.psum(dfc, ("clip", "head")).astype(F32)
    d_gt, d_gs, d_gm = lax.psum((dg_time[0], dg_space[0], dg_mlp[0]), ("clip", "head"))
    return (
        output[None], out_cls, dx[None], cls_grad, d_gt, d_qt, d_pt, d_fc, d_gs, d_qs, d_ps, d_gm, d_w1, d_w2,
    )


def solution(mesh):
    rows, wide, by_head = P("clip", None, "head", None), P("clip", None), P(None, "head", None, None)
    in_specs = (
        rows, wide, P("clip", None, None), P(), by_head, P("head", None, None), P(), P(), by_head,
        P("head", None, None), P(), P(None, "head"), P("head", None), rows, wide,
    )
    out_specs = (
        rows, wide, rows, wide, P(), by_head, P("head", None, None), P(), P(), by_head,
        P("head", None, None), P(), P(None, "head"), P("head", None),
    )
    return jax.shard_map(local, mesh=mesh, in_specs=in_specs, out_specs=out_specs, check_vma=False)
```

time: 1040 us -> 597 us (0.57)
  waiting for transfers between devices: 634 us -> 259 us
  Pallas kernels: 0 us -> 116 us
  matrix products: 114 us -> 0 us
  local copies, waits for them, and re-layouts: 105 us -> 51.7 us
  other arithmetic: 83.1 us -> 49.4 us
  starting transfers between devices: 12.1 us -> 31.5 us
    psum x2, waiting for transfers between devices: 386 us -> 123 us  [the longest x1 123 us: reduce(): return lax.psum(own, 'clip').astype(F32)]
    reduce_scatter x6 -> x0, waiting for transfers between devices: 160 us -> none  [the longest x2 67 us: branch_sum(): lax.psum_scatter(partial_rows.astype(jnp.bfloat16), 'head', scatter_dimen...]
    ppermute x0 -> x32, waiting for transfers between devices: none -> 132 us  [swap(): return lax.ppermute(x, 'head', [(i, i ^ bit) for i in range(members)])]
    pallas_call x0 -> x5, Pallas kernels: none -> 116 us  [call(): pl.pallas_call(body, out_shape=[jax.ShapeDtypeStruct(s, d) for s, d in ou...]
    dot_general x49 -> x0, matrix products: 114 us -> none  [the longest x1 8.64 us: local(): jnp.einsum('cfpd,kd->cfpk', full_block_grad, mlp_out, preferred_element_t...]
    all_gather x6 -> x0, waiting for transfers between devices: 87.2 us -> none  [the longest x3 58.4 us: gather_rows(): return lax.all_gather(shard, 'head', axis=2, tiled=True)]
    dot_general x12 -> x0, local copies, waits for them, and re-layouts: 31.2 us -> none  [the longest x1 6.44 us: space_attention_back(): jnp.einsum('cfphe,cfkhe->cfhpk', upstream, values, preferred_element_type...]
    convert_element_type x21 -> x0, local copies, waits for them, and re-layouts: 27.4 us -> none  [the longest x3 5.8 us: input_back(): partial_rows.astype(jnp.bfloat16)]
  transfers between devices with their start and end apart: 14 -> 37, of which waited for: 12 -> 11; matrix products, arithmetic and copies ran while one was open for 10% -> 14% of each run, Pallas kernels for 0% -> 10%
where the time goes in v1:
time: 597 us; the launch traced here: 596 us
  waiting for transfers between devices  259 us (43%)
  Pallas kernels  116 us (19%)
  blocking collectives  71.1 us (12%)
  local copies, waits for them, and re-layouts  51.7 us (9%)
  other arithmetic  49.4 us (8%)
  starting transfers between devices  31.5 us (5%)
  between operations  17.9 us (3%)
    ppermute x32, waiting for transfers between devices, swap(): return lax.ppermute(x, 'head', [(i, i ^ bit) for i in range(members)])  132 us
    psum x1, waiting for transfers between devices, reduce(): return lax.psum(own, 'clip').astype(F32)  123 us
    pallas_call x5, Pallas kernels, call(): pl.pallas_call(body, out_shape=[jax.ShapeDtypeStruct(s, d) for s, d in ou...  116 us
    psum x1, blocking collectives, local(): lax.psum((dg_time[0], dg_space[0], dg_mlp[0]), ('clip', 'head'))  45.4 us
    ppermute x32, starting transfers between devices, swap(): return lax.ppermute(x, 'head', [(i, i ^ bit) for i in range(members)])  20.6 us
    all_to_all x1, blocking collectives, exchange(): return lax.all_to_all(x, 'head', split_axis=0, concat_axis=0, tiled=True)  13.7 us
    another operation x4, other arithmetic, gather(): return jnp.stack([w, swap(w, 1), far, swap(far, 1)])  12.3 us
    psum x1, blocking collectives, local(): du_cls = lax.psum(dcls_part, 'head')  12 us
  transfers between devices with their start and end apart: 37, of which 11 were waited for; matrix products, arithmetic and copies ran while one was open for 14% of the time, Pallas kernels for 10%

profile of v1, /device:TPU:0, one launch (start us, length us, event | category | flops | bytes accessed | tf_op | source)
XLA Modules:
  0.0 595.7 jit_solution(1995170683216262168)
XLA Ops:
  8.6 3.0 collective-permute-start.1
  15.9 16.3 %collective-permute-done.1 = bf16[3,192,768]{2,1,0:T(8,128)(2,1)} collective-permute-done((bf16[3,192,768]{2,1,0:T(8,128)(2,1)S(1)}, bf16[3,192,768]{2,1,0:T(8,128)(2,1)}, u32[]{:S(2)}, u32[]{:S(2)}) %collective-permute-start.1) | collective-permute-done | bytes 884768 | tf_op jit(solution)/shard_map/ppermute | solution.py:425
  35.0 21.7 %collective-permute-done.4 = bf16[192,768]{1,0:T(8,128)(2,1)} collective-permute-done((bf16[192,768]{1,0:T(8,128)(2,1)}, bf16[192,768]{1,0:T(8,128)(2,1)}, u32[]{:S(2)}, u32[]{:S(2)}) %collective-permute-start.4) | collective-permute-done | bytes 294944 | tf_op jit(solution)/shard_map/ppermute | solution.py:425
  83.0 17.3 %shard_map.281 = (bf16[8,49,768]{2,1,0:T(8,128)(2,1)}, bf16[400,768]{1,0:T(8,128)(2,1)}, bf16[400,2304]{1,0:T(8,128)(2,1)}, f32[6,4,224,128]{3,2,1,0:T(8,128)}, ...) custom-call(bf16[8,49,768]{2,1,0:T(8,128)(2,1)} %bitcast.130, f32[4,1,128]{2,1,0:T(1,128)} %bitcast.160, ...), custom_call_target="tpu_custom_call" | custom-call | tf_op jit(solution)/shard_map/pallas_call | solution.py:404
  100.3 3.6 all-to-all-start
  114.5 3.7 all-to-all-done.got_ref
  118.2 3.5 all-to-all-start.1
  122.0 16.5 %shard_map.282 = (f32[416,768]{1,0:T(8,128)}, bf16[416,768]{1,0:T(8,128)(2,1)}, bf16[416,2304]{1,0:T(8,128)(2,1)}, f32[6,2,416,256]{3,2,1,0:T(8,128)}, bf16[416,768]{1,0:T(8,128)(2,1)}, /*index=5*/f32[1,768]{1,0:T(1,128)}) custom-call(bf16[8,49,768]{2,1,0:T(8,128)(2,1)} %copy-done.3, bf16[1,768]{1,0:T(2,128)(2,1)} %cls_ref.1, f32[2,1,256]{2,1,0:T(1,128)} %copy-done.23, ...), custom_call_target="tpu_custom_call" | custom-call | tf_op jit(solution)/shard_map/pallas_call | solution.py:404
  150.1 3.9 pad_maximum_fusion.w1_ref
  154.0 3.7 pad_maximum_fusion.1.w2_ref
  158.6 31.6 %shard_map.283 = (bf16[8,49,768]{2,1,0:T(8,128)(2,1)}, bf16[1,768]{1,0:T(2,128)(2,1)}, f32[416,768]{1,0:T(8,128)}, bf16[4,768,768]{2,1,0:T(8,128)(2,1)}, bf16[4,...) custom-call(bf16[416,768]{1,0:T(8,128)(2,1)} %get-tuple-element.57.mix_ref, ...), custom_call_target="tpu_custom_call" | custom-call | tf_op jit(solution)/shard_map/pallas_call | solution.py:404
  190.2 22.9 %shard_map.284 = (bf16[8,49,768]{2,1,0:T(8,128)(2,1)}, f32[1,768]{1,0:T(1,128)}, bf16[2304,768]{1,0:T(8,128)(2,1)}, bf16[768,768]{1,0:T(8,128)(2,1)}, f32[1,768]{1,0:T(1,128)}, /*index=5*/f32[1,768]{1,0:T(1,128)}) custom-call(f32[416,768]{1,0:T(8,128)} %get-tuple-element.62.r_0_, f32[416,1]{1,0:T(8,128)} %reshape.230.kcol_ref.r_1_, ...), custom_call_target="tpu_custom_call" | custom-call | tf_op jit(solution)/shard_map/pallas_call | solution.py:404
  218.0 13.7 %all_to_all.20.r_0_ = bf16[8,49,768]{2,1,0:T(8,128)(2,1)} all-to-all(bf16[8,49,768]{2,1,0:T(8,128)(2,1)S(1)} %copy-done.14), channel_id=1, replica_groups=mesh['clip'=8,'head'=4] {'head'}, dimensions={0} | all-to-all | bytes 1204224 | tf_op jit(solution)/shard_map/all_to_all | solution.py:457
  231.7 27.2 %shard_map.285 = (f32[8,49,768]{2,1,0:T(8,128)}, bf16[2304,768]{1,0:T(8,128)(2,1)}, bf16[768,768]{1,0:T(8,128)(2,1)}, bf16[768,768]{1,0:T(8,128)(2,1)}, f32[1,768]{1,0:T(1,128)}) custom-call(bf16[8,49,768]{2,1,0:T(8,128)(2,1)} %all_to_all.20.r_0_, bf16[8,49,768]{2,1,0:T(8,128)(2,1)} %bitcast.131, f32[400,1]{1,0:T(8,128)} %copy.47.r_2_, ...), custom_call_target="tpu_custom_call" | custom-call | tf_op jit(solution)/shard_map/pallas_call | solution.py:404
  263.7 3.3 slice.137
  288.8 3.5 collective-permute-done.23
  293.0 19.1 %collective-permute-done.25 = bf16[576,768]{1,0:T(8,128)(2,1)S(1)} collective-permute-done((bf16[576,768]{1,0:T(8,128)(2,1)S(1)}, bf16[576,768]{1,0:T(8,128)(2,1)S(1)}, u32[]{:S(2)}, u32[]{:S(2)}) %collective-permute-start.25) | collective-permute-done | bytes 884768 | tf_op jit(solution)/shard_map/ppermute | solution.py:425
  313.1 18.5 %collective-permute-done.21 = bf16[576,768]{1,0:T(8,128)(2,1)S(1)} collective-permute-done((bf16[576,768]{1,0:T(8,128)(2,1)S(1)}, bf16[576,768]{1,0:T(8,128)(2,1)S(1)}, u32[]{:S(2)}, u32[]{:S(2)}) %collective-permute-start.21) | collective-permute-done | bytes 884768 | tf_op jit(solution)/shard_map/ppermute | solution.py:425
  332.5 24.6 %collective-permute-done.31 = bf16[768,768]{1,0:T(8,128)(2,1)S(1)} collective-permute-done((bf16[768,768]{1,0:T(8,128)(2,1)S(1)}, bf16[768,768]{1,0:T(8,128)(2,1)S(1)}, u32[]{:S(2)}, u32[]{:S(2)}) %collective-permute-start.31) | collective-permute-done | bytes 1179680 | tf_op jit(solution)/shard_map/ppermute | solution.py:425
  358.3 25.4 %collective-permute-done.29 = bf16[768,768]{1,0:T(8,128)(2,1)S(1)} collective-permute-done((bf16[768,768]{1,0:T(8,128)(2,1)S(1)}, bf16[768,768]{1,0:T(8,128)(2,1)S(1)}, u32[]{:S(2)}, u32[]{:S(2)}) %collective-permute-start.29) | collective-permute-done | bytes 1179680 | tf_op jit(solution)/shard_map/ppermute | solution.py:425
  388.2 3.5 all-to-all-start.2
  391.7 12.0 %psum.77 = f32[1,768]{1,0:T(1,128)S(1)} all-reduce(f32[1,768]{1,0:T(1,128)S(1)} %copy-done.27), channel_id=1, replica_groups=mesh['clip'=8,'head'=4] {'head'}, use_global_device_ids=true, to_apply=%region_3.4 | all-reduce | flops 768 | bytes 6144 | tf_op jit(solution)/shard_map/psum | solution.py:520
  408.5 45.4 %all-reduce.5 = (f32[768]{0:T(1024)}, f32[768]{0:T(1024)}, f32[768]{0:T(1024)}) all-reduce(f32[768]{0:T(1024)S(1)} %reduce.12, f32[768]{0:T(1024)S(1)} %reduce.13, f32[768]{0:T(1024)S(1)} %reduce.14), channel_id=1, replica_groups=mesh['clip'=8,'head'=4] {'clip','head'}, use_global_device_ids=true, to_apply=%region_6.7 | all-reduce | flops 2304 | bytes 18432 | tf_op jit(solution)/shard_map/psum | solution.py:551
  456.8 123.1 %all-reduce.12.cloned.1.call-done = (bf16[768,3,3,64]{0,3,1,2:T(8,128)(2,1)}, bf16[768,3,3,64]{0,3,1,2:T(8,128)(2,1)}, bf16[3,64,768]{2,1,0:T(8,128)(2,1)}, bf16...) async-done(((bf16[768,3,3,64]{0,3,1,2:T(8,128)(2,1)}, bf16[768,3,3,64]{0,3,1,2:T(8,128)(2,1)}, bf16[3,64,768]{2,1,0:T(8,128)(2,1)}, ...) | async-done | bytes 4718608 | tf_op jit(solution)/shard_map/psum | solution.py:537
  (235 shorter events, 110.7 us)
Async XLA Ops:
  8.6 23.6 %collective-permute-start.1 = (bf16[3,192,768]{2,1,0:T(8,128)(2,1)S(1)}, bf16[3,192,768]{2,1,0:T(8,128)(2,1)}, u32[]{:S(2)}, u32[]{:S(2)}) collective-permute-start(bf16[3,192,768]{2,1,0:T(8,128)(2,1)S(1)} %bitcast.141), channel_id=1, source_target_pairs={{0,2},{1,3},{2,0},{3,1},{4,6},{5,7},{6,4},{7,5},{8,10},{9,11},{10,... | collective-permute-start | bytes 2654216 | tf_op jit(solution)/shard_map/ppermute | solution.py:425
  11.6 52.5 %collective-permute-start = (bf16[3,192,768]{2,1,0:T(8,128)(2,1)S(1)}, bf16[3,192,768]{2,1,0:T(8,128)(2,1)}, u32[]{:S(2)}, u32[]{:S(2)}) collective-permute-start(bf16[3,192,768]{2,1,0:T(8,128)(2,1)S(1)} %bitcast.142), channel_id=1, source_target_pairs={{0,1},{1,0},{2,3},{3,2},{4,5},{5,4},{6,7},{7,6},{8,9},{9,8},{10,11... | collective-permute-start | bytes 2654216 | tf_op jit(solution)/shard_map/ppermute | solution.py:425
  11.7 52.7 %collective-permute-start.7 = (bf16[3,192,768]{2,1,0:T(8,128)(2,1)S(1)}, bf16[3,192,768]{2,1,0:T(8,128)(2,1)}, u32[]{:S(2)}, u32[]{:S(2)}) collective-permute-start(bf16[3,192,768]{2,1,0:T(8,128)(2,1)S(1)} %bitcast.138), channel_id=1, source_target_pairs={{0,2},{1,3},{2,0},{3,1},{4,6},{5,7},{6,4},{7,5},{8,10},{9,11},{10,... | collective-permute-start | bytes 2654216 | tf_op jit(solution)/shard_map/ppermute | solution.py:425
  11.9 44.8 %collective-permute-start.4 = (bf16[192,768]{1,0:T(8,128)(2,1)}, bf16[192,768]{1,0:T(8,128)(2,1)}, u32[]{:S(2)}, u32[]{:S(2)}) collective-permute-start(bf16[192,768]{1,0:T(8,128)(2,1)} %bitcast.19), channel_id=1, source_target_pairs={{0,2},{1,3},{2,0},{3,1},{4,6},{5,7},{6,4},{7,5},{8,10},{9,11},{10,... | collective-permute-start | bytes 884744 | tf_op jit(solution)/shard_map/ppermute | solution.py:425
  13.8 44.6 %collective-permute-start.3 = (bf16[192,768]{1,0:T(8,128)(2,1)}, bf16[192,768]{1,0:T(8,128)(2,1)}, u32[]{:S(2)}, u32[]{:S(2)}) collective-permute-start(bf16[192,768]{1,0:T(8,128)(2,1)} %bitcast.19), channel_id=1, source_target_pairs={{0,1},{1,0},{2,3},{3,2},{4,5},{5,4},{6,7},{7,6},{8,9},{9,8},{10,11... | collective-permute-start | bytes 884744 | tf_op jit(solution)/shard_map/ppermute | solution.py:425
  32.2 46.7 %collective-permute-start.2 = (bf16[3,192,768]{2,1,0:T(8,128)(2,1)}, bf16[3,192,768]{2,1,0:T(8,128)(2,1)}, u32[]{:S(2)}, u32[]{:S(2)}) collective-permute-start(bf16[3,192,768]{2,1,0:T(8,128)(2,1)} %collective-permute-done.1), channel_id=1, source_target_pairs={{0,1},{1,0},{2,3},{3,2},{4,5},{5,4},{6,7},{7,6},{8,9},{9,8},{10,11... | collective-permute-start | bytes 2654216 | tf_op jit(solution)/shard_map/ppermute | solution.py:425
  56.7 53.2 %collective-permute-start.15 = (bf16[768,768]{1,0:T(8,128)(2,1)S(1)}, bf16[768,768]{1,0:T(8,128)(2,1)}, u32[]{:S(2)}, u32[]{:S(2)}) collective-permute-start(bf16[768,768]{1,0:T(8,128)(2,1)S(1)} %copy-done.5), channel_id=1, source_target_pairs={{0,2},{1,3},{2,0},{3,1},{4,6},{5,7},{6,4},{7,5},{8,10},{9,11},{10,... | collective-permute-start | bytes 3538952 | tf_op jit(solution)/shard_map/ppermute | solution.py:425
  63.6 46.2 %collective-permute-start.6 = (bf16[3,192,768]{2,1,0:T(8,128)(2,1)S(1)}, bf16[3,192,768]{2,1,0:T(8,128)(2,1)}, u32[]{:S(2)}, u32[]{:S(2)}) collective-permute-start(bf16[3,192,768]{2,1,0:T(8,128)(2,1)S(1)} %bitcast.139), channel_id=1, source_target_pairs={{0,1},{1,0},{2,3},{3,2},{4,5},{5,4},{6,7},{7,6},{8,9},{9,8},{10,11... | collective-permute-start | bytes 2654216 | tf_op jit(solution)/shard_map/ppermute | solution.py:425
  64.1 75.5 %collective-permute-start.18 = (bf16[768,768]{1,0:T(8,128)(2,1)}, bf16[768,768]{1,0:T(8,128)(2,1)}, u32[]{:S(2)}, u32[]{:S(2)}) collective-permute-start(bf16[768,768]{1,0:T(8,128)(2,1)} %param.32), channel_id=1, source_target_pairs={{0,2},{1,3},{2,0},{3,1},{4,6},{5,7},{6,4},{7,5},{8,10},{9,11},{10,... | collective-permute-start | bytes 3538952 | tf_op jit(solution)/shard_map/ppermute | solution.py:425
  64.4 46.0 %collective-permute-start.8 = (bf16[3,192,768]{2,1,0:T(8,128)(2,1)}, bf16[3,192,768]{2,1,0:T(8,128)(2,1)}, u32[]{:S(2)}, u32[]{:S(2)}) collective-permute-start(bf16[3,192,768]{2,1,0:T(8,128)(2,1)} %collective-permute-done.7), channel_id=1, source_target_pairs={{0,1},{1,0},{2,3},{3,2},{4,5},{5,4},{6,7},{7,6},{8,9},{9,8},{10,11... | collective-permute-start | bytes 2654216 | tf_op jit(solution)/shard_map/ppermute | solution.py:425
  103.9 35.5 %collective-permute-start.12 = (bf16[192,768]{1,0:T(8,128)(2,1)}, bf16[192,768]{1,0:T(8,128)(2,1)}, u32[]{:S(2)}, u32[]{:S(2)}) collective-permute-start(bf16[192,768]{1,0:T(8,128)(2,1)} %bitcast.157), channel_id=1, source_target_pairs={{0,2},{1,3},{2,0},{3,1},{4,6},{5,7},{6,4},{7,5},{8,10},{9,11},{10,... | collective-permute-start | bytes 884744 | tf_op jit(solution)/shard_map/ppermute | solution.py:425
  109.8 30.1 %collective-permute-start.11 = (bf16[192,768]{1,0:T(8,128)(2,1)}, bf16[192,768]{1,0:T(8,128)(2,1)}, u32[]{:S(2)}, u32[]{:S(2)}) collective-permute-start(bf16[192,768]{1,0:T(8,128)(2,1)} %bitcast.158), channel_id=1, source_target_pairs={{0,1},{1,0},{2,3},{3,2},{4,5},{5,4},{6,7},{7,6},{8,9},{9,8},{10,11... | collective-permute-start | bytes 884744 | tf_op jit(solution)/shard_map/ppermute | solution.py:425
  109.9 40.2 %collective-permute-start.14 = (bf16[768,768]{1,0:T(8,128)(2,1)S(1)}, bf16[768,768]{1,0:T(8,128)(2,1)}, u32[]{:S(2)}, u32[]{:S(2)}) collective-permute-start(bf16[768,768]{1,0:T(8,128)(2,1)S(1)} %copy-done.5), channel_id=1, source_target_pairs={{0,1},{1,0},{2,3},{3,2},{4,5},{5,4},{6,7},{7,6},{8,9},{9,8},{10,11... | collective-permute-start | bytes 3538952 | tf_op jit(solution)/shard_map/ppermute | solution.py:425
  110.4 39.7 %collective-permute-start.16 = (bf16[768,768]{1,0:T(8,128)(2,1)}, bf16[768,768]{1,0:T(8,128)(2,1)}, u32[]{:S(2)}, u32[]{:S(2)}) collective-permute-start(bf16[768,768]{1,0:T(8,128)(2,1)} %collective-permute-done.15), channel_id=1, source_target_pairs={{0,1},{1,0},{2,3},{3,2},{4,5},{5,4},{6,7},{7,6},{8,9},{9,8},{10,11... | collective-permute-start | bytes 3538952 | tf_op jit(solution)/shard_map/ppermute | solution.py:425
  118.2 39.5 %all-to-all-start.1 = ((bf16[8,49,768]{2,1,0:T(8,128)(2,1)}), bf16[8,49,768]{2,1,0:T(8,128)(2,1)S(1)}, u32[]{:S(2)}, u32[]{:S(2)}) async-start(bf16[8,49,768]{2,1,0:T(8,128)(2,1)} %bitcast.116), calls=%async_computation.1 | async-start | bytes 1376256 | tf_op jit(solution)/shard_map/all_to_all | solution.py:457
  121.7 332.2 %all-reduce.10.cloned.1.call-start = ((), (), s32[]{:S(2)}) async-start(), calls=%async_computation.4 | async-start | bytes 2359296 | tf_op jit(solution)/shard_map/psum | solution.py:550
  216.6 58.8 %collective-permute-start.24 = (bf16[2,576,768]{2,1,0:T(8,128)(2,1)}, bf16[2,576,768]{2,1,0:T(8,128)(2,1)}, u32[]{:S(2)}, u32[]{:S(2)}) collective-permute-start(bf16[2,576,768]{2,1,0:T(8,128)(2,1)} %slice.125), channel_id=1, source_target_pairs={{0,1},{1,0},{2,3},{3,2},{4,5},{5,4},{6,7},{7,6},{8,9},{9,8},{10,11... | collective-permute-start | bytes 5308424 | tf_op jit(solution)/shard_map/ppermute | solution.py:425
  217.9 52.1 %collective-permute-start.26 = (bf16[2,192,768]{2,1,0:T(8,128)(2,1)}, bf16[2,192,768]{2,1,0:T(8,128)(2,1)}, u32[]{:S(2)}, u32[]{:S(2)}) collective-permute-start(bf16[2,192,768]{2,1,0:T(8,128)(2,1)} %slice.129), channel_id=1, source_target_pairs={{0,1},{1,0},{2,3},{3,2},{4,5},{5,4},{6,7},{7,6},{8,9},{9,8},{10,11... | collective-permute-start | bytes 1769480 | tf_op jit(solution)/shard_map/ppermute | solution.py:425
  270.0 309.9 %all-reduce.12.cloned.1.call-start = ((), (), s32[]{:S(2)}) async-start(), calls=%async_computation.5 | async-start | bytes 9437184 | tf_op jit(solution)/shard_map/psum | solution.py:537
  278.9 33.2 %collective-permute-start.25 = (bf16[576,768]{1,0:T(8,128)(2,1)S(1)}, bf16[576,768]{1,0:T(8,128)(2,1)S(1)}, u32[]{:S(2)}, u32[]{:S(2)}) collective-permute-start(bf16[576,768]{1,0:T(8,128)(2,1)S(1)} %slice_bitcast_fusion.4), channel_id=1, source_target_pairs={{0,2},{1,3},{2,0},{3,1},{4,6},{5,7},{6,4},{7,5},{8,10},{9,11},{10,... | collective-permute-start | bytes 2654216 | tf_op jit(solution)/shard_map/ppermute | solution.py:425
  281.3 50.3 %collective-permute-start.21 = (bf16[576,768]{1,0:T(8,128)(2,1)S(1)}, bf16[576,768]{1,0:T(8,128)(2,1)S(1)}, u32[]{:S(2)}, u32[]{:S(2)}) collective-permute-start(bf16[576,768]{1,0:T(8,128)(2,1)S(1)} %slice_bitcast_fusion.6), channel_id=1, source_target_pairs={{0,2},{1,3},{2,0},{3,1},{4,6},{5,7},{6,4},{7,5},{8,10},{9,11},{10,... | collective-permute-start | bytes 2654216 | tf_op jit(solution)/shard_map/ppermute | solution.py:425
  285.5 71.7 %collective-permute-start.31 = (bf16[768,768]{1,0:T(8,128)(2,1)S(1)}, bf16[768,768]{1,0:T(8,128)(2,1)S(1)}, u32[]{:S(2)}, u32[]{:S(2)}) collective-permute-start(bf16[768,768]{1,0:T(8,128)(2,1)S(1)} %slice_bitcast_fusion), channel_id=1, source_target_pairs={{0,2},{1,3},{2,0},{3,1},{4,6},{5,7},{6,4},{7,5},{8,10},{9,11},{10,... | collective-permute-start | bytes 3538952 | tf_op jit(solution)/shard_map/ppermute | solution.py:425
  286.9 96.8 %collective-permute-start.29 = (bf16[768,768]{1,0:T(8,128)(2,1)S(1)}, bf16[768,768]{1,0:T(8,128)(2,1)S(1)}, u32[]{:S(2)}, u32[]{:S(2)}) collective-permute-start(bf16[768,768]{1,0:T(8,128)(2,1)S(1)} %slice_bitcast_fusion.2), channel_id=1, source_target_pairs={{0,2},{1,3},{2,0},{3,1},{4,6},{5,7},{6,4},{7,5},{8,10},{9,11},{10,... | collective-permute-start | bytes 3538952 | tf_op jit(solution)/shard_map/ppermute | solution.py:425
  388.2 19.4 %all-to-all-start.2 = ((bf16[8,49,768]{2,1,0:T(8,128)(2,1)}), bf16[8,49,768]{2,1,0:T(8,128)(2,1)S(1)}, u32[]{:S(2)}, u32[]{:S(2)}) async-start(bf16[8,49,768]{2,1,0:T(8,128)(2,1)} %get-tuple-element.60), calls=%async_computation.2 | async-start | bytes 1376256 | tf_op jit(solution)/shard_map/all_to_all | solution.py:457
  (51 other events, 566.7 us)
Sparse Core Ops, SparseCore 0:
  270.1 132.0 all-reduce.9
  408.2 171.5 all-reduce.11

commit v2 on v1

v2 whole, which is shorter than its diff:
```python
from functools import partial
from types import SimpleNamespace

import jax
import jax.numpy as jnp
from jax import lax
from jax.experimental import pallas as pl
from jax.experimental.pallas import tpu as pltpu
from jax.sharding import PartitionSpec as P

EPSILON = 1e-06
NEGATIVE = -1e30
F32 = jnp.float32
BF16 = jnp.bfloat16


def nn(a, b):
    return lax.dot_general(a, b, (((1,), (0,)), ((), ())), preferred_element_type=F32)


def nt(a, b):
    return lax.dot_general(a, b, (((1,), (1,)), ((), ())), preferred_element_type=F32)


def tn(a, b):
    return lax.dot_general(a, b, (((0,), (0,)), ((), ())), preferred_element_type=F32)


def tiles(total, size, body):
    def step(i, carry):
        body(pl.multiple_of(i * size, size))
        return carry

    lax.fori_loop(0, total // size, step, 0)


def stats(x):
    center = x - jnp.mean(x, axis=-1, keepdims=True)
    factor = lax.rsqrt(jnp.mean(center * center, axis=-1, keepdims=True) + EPSILON)
    return center * factor, factor


def norm_back(grad, gain, scaled, factor):
    weighted = grad * gain
    inner = weighted - jnp.mean(weighted, axis=-1, keepdims=True)
    return factor * (inner - scaled * jnp.mean(weighted * scaled, axis=-1, keepdims=True))


def pair_masks():
    lane = lax.broadcasted_iota(jnp.int32, (1, 128), 1)
    return (lane < 64).astype(F32).astype(BF16), (lane >= 64).astype(F32).astype(BF16)


def stacked(x):
    low, high = pair_masks()
    return jnp.concatenate([x * low, x * high], axis=0)


def unstacked(x):
    rows = x.shape[0] // 2
    lane = lax.broadcasted_iota(jnp.int32, (1, 128), 1)
    return jnp.where(lane < 64, x[:rows], x[rows:])


def norm_rows(x_ref, gain_ref, u_ref, total, chunk):
    def body(r):
        rows = pl.ds(r, chunk)
        scaled, _ = stats(x_ref[rows, :])
        u_ref[rows, :] = (scaled * gain_ref[...]).astype(BF16)

    tiles(total, chunk, body)


def project_qkv(u_ref, wt_ref, qkv_ref, rows, start, size):
    width = u_ref.shape[1]

    def body(t, carry):
        scale = jnp.where(t == 0, 0.125, 1.0)
        out = nt(u_ref[:rows, :], wt_ref[t, start : start + size, :]) * scale
        qkv_ref[:rows, pl.ds(pl.multiple_of(t * width + start, 128), size)] = out.astype(BF16)
        return carry

    lax.fori_loop(0, 3, body, 0)


def qkv_back(dqkv_ref, u_ref, wt_ref, du_ref, rows):
    width = u_ref.shape[1]

    def back(n):
        cols = pl.ds(n, 256)
        total = nn(dqkv_ref[:rows, :width], wt_ref[0, :, cols])
        total += nn(dqkv_ref[:rows, width : 2 * width], wt_ref[1, :, cols])
        total += nn(dqkv_ref[:rows, 2 * width :], wt_ref[2, :, cols])
        du_ref[:rows, cols] = total

    tiles(width, 256, back)

    def grad(i, carry):
        n = pl.multiple_of((i % 3) * 256, 256)
        cols = pl.ds(pl.multiple_of(i * 256, 256), 256)
        wt_ref[i // 3, pl.ds(n, 256), :] = tn(dqkv_ref[:rows, cols], u_ref[:rows, :]).astype(BF16)
        return carry

    lax.fori_loop(0, 9, grad, 0)


def softmax(scores):
    highest = jnp.max(scores, axis=-1, keepdims=True)
    weights = jnp.exp(scores - highest)
    return weights * (1.0 / jnp.sum(weights, axis=-1, keepdims=True))


def attention(qkv_ref, p_ref, mix_ref, groups, bias_of, first, last):
    width = mix_ref.shape[1]

    def body(hp, carry):
        qc = pl.ds(pl.multiple_of(hp * 128, 128), 128)
        kc = pl.ds(pl.multiple_of(width + hp * 128, 128), 128)
        vc = pl.ds(pl.multiple_of(2 * width + hp * 128, 128), 128)
        for g, (start, size) in enumerate(groups):
            rows = pl.ds(start, size)
            prob = softmax(nt(stacked(qkv_ref[rows, qc]), qkv_ref[rows, kc]) + bias_of(g, size))
            p_ref[hp, g, : 2 * size, :size] = prob
            mix_ref[rows, qc] = unstacked(nn(prob.astype(BF16), qkv_ref[rows, vc])).astype(BF16)
        return carry

    lax.fori_loop(first, last, body, 0)


def attention_back(qkv_ref, p_ref, dmix_ref, dqkv_ref, groups):
    width = dmix_ref.shape[1]

    def body(hp, carry):
        qc = pl.ds(pl.multiple_of(hp * 128, 128), 128)
        kc = pl.ds(pl.multiple_of(width + hp * 128, 128), 128)
        vc = pl.ds(pl.multiple_of(2 * width + hp * 128, 128), 128)
        for g, (start, size) in enumerate(groups):
            rows = pl.ds(start, size)
            up = stacked(dmix_ref[rows, qc])
            prob = p_ref[hp, g, : 2 * size, :size]
            dprob = nt(up, qkv_ref[rows, vc])
            delta = jnp.sum(prob * dprob, axis=-1, keepdims=True)
            dscore = (prob * (dprob - delta)).astype(BF16)
            dqkv_ref[rows, qc] = (unstacked(nn(dscore, qkv_ref[rows, kc])) * 0.125).astype(BF16)
            dqkv_ref[rows, kc] = tn(dscore, stacked(qkv_ref[rows, qc])).astype(BF16)
            dqkv_ref[rows, vc] = tn(prob.astype(BF16), up).astype(BF16)
        return carry

    lax.fori_loop(0, width // 128, body, 0)


T_ROWS = 400
T_GROUPS = ((0, 96), (96, 96), (192, 96), (288, 112))
SEG = 208
S_ROWS = 416
S_GROUPS = ((0, 208), (208, 208))


def time_bias(krow_ref):
    def bias_of(g, size):
        row = lax.broadcasted_iota(jnp.int32, (size, size), 0)
        col = lax.broadcasted_iota(jnp.int32, (size, size), 1)
        same = (row // 8) == (col // 8)
        kept = jnp.broadcast_to(krow_ref[g, :, :size], (size, size)) > 0.0
        ok = same & (kept | (row == col))
        bias = jnp.where(ok, 0.0, NEGATIVE)
        return jnp.concatenate([bias, bias], axis=0)

    return bias_of


def space_bias(krow_ref, g):
    return (krow_ref[g, :, :SEG] - 1.0) * (-NEGATIVE)


def to_patch_order(src_ref, dst_ref, perm_ref):
    frames, count, width = src_ref.shape
    used = frames * count
    for j in range(width // 128):
        for f in range(frames):
            perm_ref[j, pl.ds(f, count, stride=frames), :] = src_ref[f, :, j * 128 : (j + 1) * 128].astype(F32)
        dst_ref[:used, j * 128 : (j + 1) * 128] = perm_ref[j, :used, :]
    dst_ref[used:T_ROWS, :] = jnp.zeros((T_ROWS - used, width), F32)


def to_frame_order(src_ref, dst_ref, perm_ref):
    frames, count, width = dst_ref.shape
    for j in range(width // 128):
        perm_ref[j, :, :] = src_ref[:T_ROWS, j * 128 : (j + 1) * 128]
        for f in range(frames):
            out = perm_ref[j, pl.ds(f, count, stride=frames), :]
            dst_ref[f, :, j * 128 : (j + 1) * 128] = out.astype(dst_ref.dtype)


def gather_frames(got_ref, cls_row, out_ref):
    sources, count = got_ref.shape[0] // 2, got_ref.shape[1]
    for f in range(2):
        base = f * SEG
        for s in range(sources):
            out_ref[base + s * count : base + (s + 1) * count, :] = got_ref[2 * s + f].astype(F32)
        at = base + sources * count
        out_ref[at : at + 1, :] = cls_row[f]
        out_ref[at + 1 : base + SEG, :] = jnp.zeros((SEG - 1 - sources * count, out_ref.shape[1]), F32)


def scatter_frames(x_ref, send_ref):
    sources, count = send_ref.shape[0] // 2, send_ref.shape[1]
    for f in range(2):
        for s in range(sources):
            at = f * SEG + s * count
            send_ref[2 * s + f] = x_ref[at : at + count, :].astype(send_ref.dtype)


def cls_attention(qkv_ref, krow_ref, at, width):
    lane = lax.broadcasted_iota(jnp.int32, (16, width), 1) // 64
    own = (lane == lax.broadcasted_iota(jnp.int32, (16, width), 0)).astype(F32)
    total = jnp.zeros((1, width), F32)
    for f in range(2):
        q = qkv_ref[f * SEG + at : f * SEG + at + 1, :width].astype(F32)
        k = qkv_ref[f * SEG : (f + 1) * SEG, width : 2 * width]
        v = qkv_ref[f * SEG : (f + 1) * SEG, 2 * width :]
        prob = softmax(nt((own * q).astype(BF16), k) + space_bias(krow_ref, f))
        total += jnp.sum(own * nn(prob.astype(BF16), v), axis=0, keepdims=True)
    return total


def blocks_swapped(x, distance):
    width = x.shape[1]
    quarter = width // 4
    order = [i ^ distance for i in range(4)]
    return jnp.concatenate([x[:, i * quarter : (i + 1) * quarter] for i in order], axis=1)


def set_row(ref, base, at, row, dtype):
    start = base + at // 16 * 16
    pick = lax.broadcasted_iota(jnp.int32, (16, 1), 0) == at % 16
    kept = ref[start : start + 16, :].astype(F32)
    ref[start : start + 16, :] = jnp.where(pick, jnp.broadcast_to(row, kept.shape), kept).astype(dtype)


MESH = pl.DeviceIdType.MESH


def whole_step(names, frames, *refs):
    R = SimpleNamespace(**dict(zip(names, refs)))
    clip, head = lax.axis_index("clip"), lax.axis_index("head")
    side, turn = clip % 2, clip // 2 % 2
    width = R.wt_t.shape[2]
    count = R.patches.shape[1]
    at = 4 * count
    peer_c, peer_y, peer_d = (clip, head ^ 1), (clip, head ^ 2), (clip, head ^ 3)
    levels = lax.axis_size("clip").bit_length() - 1
    bits = [(clip ^ (1 << j), head) for j in range(levels)]

    pieces = (
        (R.wt_t, R.wt_t_in, 0), (R.pj_t, R.pj_t_in, 1), (R.wt_s, R.wt_s_in, 0), (R.pj_s, R.pj_s_in, 1),
        (R.w1, R.w1_in, 2), (R.w2, R.w2_in, 2),
    )

    def slot(i, s, half=None):
        ref, _, kind = pieces[i]
        if kind == 2:
            return ref.at[s] if half is None else ref.at[s, pl.ds(half * 384, 384), :]
        start, size = (s * 192, 192) if half is None else (s * 192 + half * 96, 96)
        return ref.at[:, pl.ds(start, size), :] if kind == 0 else ref.at[pl.ds(start, size), :]

    def source(i, half=None):
        _, ref, kind = pieces[i]
        if half is None:
            return ref
        if kind == 0:
            return ref.at[:, pl.ds(half * 96, 96), :]
        size = ref.shape[0] // 2
        return ref.at[pl.ds(half * size, size), :]

    def remote(src, dst, sems, index, peer):
        return pltpu.make_async_remote_copy(
            src_ref=src, dst_ref=dst, send_sem=sems[0].at[index], recv_sem=sems[1].at[index],
            device_id=peer, device_id_type=MESH,
        )

    def y_copy(i):
        return remote(source(i, side), slot(i, 2, side), (R.wy_s, R.wy_r), i, peer_y)

    def x_copy(i):
        return remote(slot(i, 2, side), slot(i, 2, side), (R.wx_s, R.wx_r), i, bits[0])

    def c_copy(i):
        return remote(source(i), slot(i, 1), (R.wc_s, R.wc_r), i, peer_c)

    def f_copy(i, other):
        half = 1 - side if other else side
        sems = (R.wg_s, R.wg_r) if other else (R.wf_s, R.wf_r)
        return remote(slot(i, 2, half), slot(i, 3, half), sems, i, peer_c)

    def own_copy(i):
        return pltpu.make_async_copy(source(i), slot(i, 0), R.wo.at[i])

    def pass_near(i):
        y_copy(i).wait_recv()
        x_copy(i).start()
        f_copy(i, False).start()

    def pass_far(i):
        x_copy(i).wait_recv()
        f_copy(i, True).start()

    def ready_near(i):
        own_copy(i).wait()
        c_copy(i).wait_recv()

    def ready_far(i):
        f_copy(i, False).wait_recv()
        f_copy(i, True).wait_recv()

    def sent(i):
        y_copy(i).wait_send()
        x_copy(i).wait_send()
        c_copy(i).wait_send()
        f_copy(i, False).wait_send()
        f_copy(i, True).wait_send()

    def exchange(k, src, dst):
        mine = pl.ds(2 * head, 2)
        copies = []
        for r, peer in ((2, peer_y), (3, peer_d), (1, peer_c)):
            there = pl.ds(2 * (head ^ r), 2)
            copies.append(remote(src.at[there], dst.at[mine], (R.ex_s, R.ex_r), 3 * k + r - 1, peer))
        copies.append(pltpu.make_async_copy(src.at[mine], dst.at[mine], R.exo.at[k]))
        return copies

    def all_start(copies):
        for copy in copies:
            copy.start()

    def all_wait(copies):
        for copy in copies:
            copy.wait()

    def sum_rows(k, buf, swapped):
        copies = [
            remote(buf.at[0], buf.at[r], (R.row_s, R.row_r), 3 * k + r - 1, peer)
            for r, peer in ((2, peer_y), (3, peer_d), (1, peer_c))
        ]
        all_start(copies)

        def finish():
            all_wait(copies)
            part = [buf[r] for r in range(4)]
            if swapped:
                part = [part[0]] + [blocks_swapped(part[r], r) for r in (1, 2, 3)]
            total = (part[0] + part[1]) + (part[2] + part[3])
            return total[0:1, :]

        return finish

    def unit(i):
        if i < 8:
            ref, n = (R.w1, i) if i < 4 else (R.w2, i - 4)
            return lambda s, start=0, size=192: ref.at[s, pl.ds(n * 192 + start, size), :]
        if i == 12:
            return lambda s, start=0, size=192: R.fc.at[pl.ds((head ^ s) * 192 + start, size), :]
        wt, pj = (R.wt_s, R.pj_s) if i < 12 else (R.wt_t, R.pj_t)
        n = i - 8 if i < 12 else i - 13
        if n == 0:
            return lambda s, start=0, size=192: pj.at[pl.ds(s * 192 + start, size), :]
        return lambda s, start=0, size=192: wt.at[n - 1, pl.ds(s * 192 + start, size), :]

    half = side * 96
    quarter = half + turn * 48

    def add(dst, src, size):
        def body(r, carry):
            rows = pl.ds(pl.multiple_of(r * 48, 48), 48)
            dst[rows, :] = dst[rows, :] + src[rows, :]
            return carry

        lax.fori_loop(0, size // 48, body, 0)

    def core_copies(i):
        u = unit(i)
        return [
            remote(u(1), R.near.at[i % 9, 0], (R.gc_s, R.gc_r), 2 * i, peer_c),
            remote(u(3), R.near.at[i % 9, 1], (R.gc_s, R.gc_r), 2 * i + 1, peer_c),
        ]

    def y_part(i):
        u = unit(i)
        return remote(u(2), u(3) if i == 12 else u(1), (R.gy_s, R.gy_r), i, peer_y)

    def landing(i, j):
        u = unit(i)
        if j == 0:
            return u(3, 0, 96)
        return u(3, 48 + 48 * j, 48) if j < 3 else u(2, 48 * (j - 3), 48)

    def bit_part(i, j):
        u = unit(i)
        if j == 0:
            src = u(0, 96 - half, 96)
        elif j == 1:
            src = u(0, half + 48 - turn * 48, 48)
        else:
            src = u(0, quarter, 48)
        return remote(src, landing(i, j), (R.gb_s, R.gb_r), i * levels + j, bits[j])

    def result(i, start, size):
        if i < 8:
            return (R.dw1 if i < 4 else R.dw2).at[pl.ds(i % 4 * 192 + start, size), :]
        if i == 12:
            return R.dfc.at[pl.ds(head * 192 + start, size), :]
        n = i - 8 if i < 12 else i - 13
        return (R.dsp if i < 12 else R.dti).at[n, pl.ds(start, size), :]

    def back_near(i):
        mine = unit(i)(0, quarter, 48)
        there = result(i, quarter, 48)
        return [
            remote(mine, there, (R.gq_s, R.gq_r), i, bits[1]),
            pltpu.make_async_copy(mine, there, R.go.at[i]),
        ]

    def back_far(i):
        rows = result(i, half, 96)
        return remote(rows, rows, (R.gh_s, R.gh_r), i, bits[0])

    def back_all(i):
        copies = []
        for r, peer in ((2, peer_y), (3, peer_d), (1, peer_c)):
            rows = R.dfc.at[pl.ds(head * 192, 192), :]
            copies.append(remote(rows, rows, (R.gf_s, R.gf_r), r - 1, peer))
        return copies

    def tell(sem, index, peer):
        pl.semaphore_signal(sem.at[index], inc=1, device_id=peer, device_id_type=MESH)

    stage = [0] * 17
    joined = [False] * 17

    def wait_core(i):
        if joined[i]:
            return
        joined[i] = True
        u = unit(i)
        all_wait(core_copies(i))
        tell(R.free_y, i, peer_y)
        for j in range(min(levels, 3)):
            tell(R.free_b, i * levels + j, bits[j])
        add(u(2), R.near.at[i % 9, 1], 192)
        add(u(0), R.near.at[i % 9, 0], 192)

    def advance(i):
        u, k = unit(i), stage[i]
        stage[i] += 1
        if k == 0:
            all_start(core_copies(i))
        elif k == 1:
            wait_core(i)
            pl.semaphore_wait(R.free_y.at[i], 1)
            y_part(i).start()
        elif k == 2:
            y_part(i).wait()
            for j in range(3, levels):
                tell(R.free_b, i * levels + j, bits[j])
            add(u(0), u(1), 192)
        elif k < 3 + levels:
            j = k - 3
            bit_part(i, j).wait()
            if j == 0:
                add(u(0, half, 96), landing(i, j), 96)
            else:
                add(u(0, quarter, 48), landing(i, j), 48)
        elif k == 3 + levels:
            all_wait(back_near(i))
            back_far(i).start()
        elif k == 4 + levels:
            back_far(i).wait()
            if i == 12:
                all_start(back_all(i))
        else:
            all_wait(back_all(i))
        if 2 <= k < 2 + levels:
            pl.semaphore_wait(R.free_b.at[i * levels + k - 2], 1)
            bit_part(i, k - 2).start()
        elif k == 2 + levels:
            all_start(back_near(i))

    last = 5 + levels

    def finish_units(between):
        while min(stage) < last:
            for i in reversed(range(17)):
                if stage[i] < last and (i == 0 or stage[i] < stage[i - 1] or stage[i - 1] >= last):
                    advance(i)
            next(between, None)
        for _ in between:
            pass
        advance(12)

    barrier = pltpu.get_barrier_semaphore()
    for peer in [peer_c, peer_y, peer_d] + bits:
        pl.semaphore_signal(barrier, inc=1, device_id=peer, device_id_type=MESH)
    pl.semaphore_wait(barrier, 3 + levels)

    load = [pltpu.make_async_copy(R.patches, R.patches_v, R.lo.at[0])]
    load.append(pltpu.make_async_copy(R.fc_in, R.fc, R.lo.at[1]))
    load[0].start()
    for i in range(4):
        y_copy(i).start()
    for i in range(4):
        own_copy(i).start()
        c_copy(i).start()
    load[1].start()
    for i in range(4, 6):
        own_copy(i).start()
        c_copy(i).start()

    rows_x, first = R.rows_x, R.rows_s
    qkv_t, p_t, mix_t, att_t, u_t = R.qkv_t, R.p_t, R.mix_t, R.att_t, R.u_t
    load[0].wait()
    to_patch_order(R.patches_v, rows_x, R.perm)
    norm_rows(rows_x, R.gain_t, u_t, T_ROWS, 80)
    ready_near(0)
    ready_near(1)
    project_qkv(u_t, R.wt_t, qkv_t, T_ROWS, 0, width // 2)
    pass_near(0)
    pass_near(1)
    attention(qkv_t, p_t, mix_t, T_GROUPS, time_bias(R.kt_row), 0, 3)
    pass_far(0)
    pass_far(1)
    ready_far(0)
    ready_far(1)
    project_qkv(u_t, R.wt_t, qkv_t, T_ROWS, width // 2, width // 2)
    attention(qkv_t, p_t, mix_t, T_GROUPS, time_bias(R.kt_row), 3, 6)
    pass_near(2)
    pass_near(3)
    load[1].wait()

    def project(n):
        cols = pl.ds(n, 256)
        att_t[:, cols] = nn(mix_t[...], R.pj_t[:, cols]).astype(BF16)

    tiles(width, 256, project)

    def branch(n):
        cols = pl.ds(n, 256)
        first[:T_ROWS, cols] = rows_x[:T_ROWS, cols] + R.kt_col[...] * nn(att_t[...], R.fc[:, cols])

    tiles(width, 256, branch)
    to_frame_order(first, R.send_a, R.perm)
    ex_first = exchange(0, R.send_a, R.got_first)
    all_start(ex_first)
    ex_cot = exchange(1, R.cot, R.got_cot)
    all_start(ex_cot)
    y_copy(4).start()
    pass_far(2)
    pass_far(3)

    qkv_s, p_s, mix_s, u_s = R.qkv_s, R.p_s, R.mix_s, R.u_s
    all_wait(ex_first)
    cls_row = R.cls[...].astype(F32)
    gather_frames(R.got_first, (cls_row, cls_row), rows_x)
    norm_rows(rows_x, R.gain_s, u_s, S_ROWS, 208)
    for i in (2, 3):
        ready_near(i)
        ready_far(i)
    project_qkv(u_s, R.wt_s, qkv_s, S_ROWS, 0, width)
    part = cls_attention(qkv_s, R.ks_row, at, width)
    R.cls_sum[0] = jnp.broadcast_to(part, (8, width))
    cls_total = sum_rows(0, R.cls_sum, True)
    y_copy(5).start()
    pass_near(4)
    attention(qkv_s, p_s, mix_s, S_GROUPS, lambda g, size: space_bias(R.ks_row, g), 0, 6)
    set_row(mix_s, 0, at, cls_total() * (1.0 / frames), BF16)
    set_row(mix_s, SEG, at, jnp.zeros((1, width), F32), BF16)
    pass_far(4)
    pass_near(5)
    second, cot = R.rows_s, R.rows_c

    def project_space(n):
        cols = pl.ds(n, 256)
        second[:, cols] = rows_x[:, cols] + R.ks_col[...] * nn(mix_s[...], R.pj_s[:, cols])

    tiles(width, 256, project_space)

    all_wait(ex_cot)
    gather_frames(R.got_cot, (R.ccot[...], jnp.zeros((1, width), F32)), cot)
    u, uw, dz, dzw = R.low_a, R.low_b, R.low_c, R.low_d
    acc, du = R.rows_a, R.rows_d
    kcol, once = R.ks_col, R.once

    def prepare(r):
        rows = pl.ds(r, 208)
        scaled, _ = stats(second[rows, :])
        low = (scaled * R.gain_m[...]).astype(BF16)
        u[rows, :] = low
        uw[rows, :] = (low.astype(F32) * once[rows, :]).astype(BF16)
        grad = cot[rows, :] * kcol[rows, :]
        dz[rows, :] = grad.astype(BF16)
        dzw[rows, :] = (grad * once[rows, :]).astype(BF16)

    tiles(S_ROWS, 208, prepare)
    acc[...] = jnp.zeros_like(acc)
    du[...] = jnp.zeros_like(du)
    w1_ref, w2_ref = R.w1, R.w2
    per = w1_ref.shape[2] // 256

    def hidden(i, carry):
        s = i // per
        cols = pl.ds(pl.multiple_of((i % per) * 256, 256), 256)
        w1 = w1_ref[s, :, cols]
        w2 = w2_ref[s, cols, :]
        hid = nn(u[...], w1)
        phi = 0.5 + 0.5 * lax.erf(hid * 0.7071067811865476)
        act = (hid * phi).astype(BF16)
        slope = phi + hid * (0.3989422804014327 * jnp.exp(hid * hid * -0.5))
        acc[...] += nn(act, w2)
        dhid = (nt(dz[...], w2) * slope).astype(BF16)
        du[...] += nt(dhid, w1)
        w2_ref[s, cols, :] = tn(act, dzw[...]).astype(BF16)
        w1_ref[s, :, cols] = tn(uw[...], dhid).astype(BF16)
        return carry

    for i in (4, 5):
        ready_near(i)
    for i in (4, 5):
        c_copy(i).wait_send()
    lax.fori_loop(0, 2 * per, hidden, 0)
    pass_far(5)
    for i in (4, 5):
        ready_far(i)
        y_copy(i).wait_send()
        x_copy(i).wait_send()
        f_copy(i, False).wait_send()
        f_copy(i, True).wait_send()
    lax.fori_loop(2 * per, 4 * per, hidden, 0)
    R.dgain_m[...] = jnp.zeros((1, width), F32)

    def finish_mlp(r):
        rows = pl.ds(r, 208)
        x = second[rows, :]
        scaled, factor = stats(x)
        acc[rows, :] = x + kcol[rows, :] * acc[rows, :]
        grad = du[rows, :]
        R.dgain_m[...] += jnp.sum(grad * scaled * once[rows, :], axis=0, keepdims=True)
        cot[rows, :] += norm_back(grad, R.gain_m[...], scaled, factor)

    tiles(S_ROWS, 208, finish_mlp)
    R.ocls[...] = acc[at : at + 1, :].astype(BF16)
    scatter_frames(acc, R.send_b)
    ex_out = exchange(2, R.send_b, R.out)
    all_start(ex_out)

    for i in range(8):
        advance(i)

    dsecond = cot
    low, loww, dmix, dqkv = R.low_a, R.low_b, R.low_c, R.dqkv
    low[...] = (dsecond[...] * kcol[...]).astype(BF16)
    loww[...] = (dsecond[...] * (kcol[...] * once[...])).astype(BF16)
    dcls_second = dsecond[at : at + 1, :]
    set_row(low, SEG, at, dcls_second, BF16)
    for i in (2, 3):
        sent(i)

    def back_space(n):
        cols = pl.ds(n, 256)
        dmix[:, cols] = nt(low[...], R.pj_s[cols, :]).astype(BF16)
        R.pj_s[cols, :] = tn(mix_s[:, cols], loww[...]).astype(BF16)

    tiles(width, 256, back_space)
    advance(0)
    advance(1)
    dcls_mix = dmix[SEG - 16 : SEG, :].astype(F32)[at - SEG + 16 : at - SEG + 17, :] * (1.0 / frames)
    set_row(dmix, 0, at, dcls_mix, BF16)
    set_row(dmix, SEG, at, dcls_mix, BF16)
    attention_back(qkv_s, p_s, dmix, dqkv, S_GROUPS)
    advance(2)
    advance(3)
    advance(0)
    qkv_back(dqkv, u_s, R.wt_s, du, S_ROWS)
    R.dcls_sum[0] = jnp.broadcast_to(du[at : at + 1, :] + du[SEG + at : SEG + at + 1, :], (8, width))
    R.dgain_s[...] = jnp.zeros((1, width), F32)
    dfirst = R.rows_a

    def finish_space(r):
        rows = pl.ds(r, 208)
        scaled, factor = stats(rows_x[rows, :])
        grad = du[rows, :]
        R.dgain_s[...] += jnp.sum(grad * scaled, axis=0, keepdims=True)
        dfirst[rows, :] = dsecond[rows, :] + norm_back(grad, R.gain_s[...], scaled, factor)

    tiles(S_ROWS, 208, finish_space)
    scatter_frames(dfirst, R.send_a)
    for i in range(4, 8):
        wait_core(i)
    ex_df = exchange(3, R.send_a, R.got_first)
    all_start(ex_df)
    dcls_total = sum_rows(1, R.dcls_sum, False)
    for i in range(4, 8):
        advance(i)
    advance(1)
    advance(0)

    df = R.rows_s
    to_patch_order(R.patches_v, rows_x, R.perm)
    all_wait(ex_df)
    for i in range(8, 12):
        advance(i)
    to_patch_order(R.got_first, df, R.perm)
    scaled, factor = stats(cls_row)
    R.dcls[...] = dcls_second + norm_back(dcls_total(), R.gain_s[...], scaled, factor)
    low, datt, dmix = R.low_a, R.low_b, R.low_c
    low[:T_ROWS, :] = (df[:T_ROWS, :] * R.kt_col[...]).astype(BF16)
    for i in (0, 1):
        sent(i)

    def back_fc(n):
        cols = pl.ds(n, 256)
        datt[:T_ROWS, cols] = nt(low[:T_ROWS, :], R.fc[cols, :]).astype(BF16)
        R.fc[cols, :] = tn(att_t[:, cols], low[:T_ROWS, :]).astype(BF16)

    tiles(width, 256, back_fc)
    advance(12)
    advance(8)

    def back_time(n):
        cols = pl.ds(n, 256)
        dmix[:T_ROWS, cols] = nt(datt[:T_ROWS, :], R.pj_t[cols, :]).astype(BF16)
        R.pj_t[cols, :] = tn(mix_t[:, cols], datt[:T_ROWS, :]).astype(BF16)

    tiles(width, 256, back_time)
    advance(13)
    advance(2)
    advance(1)
    advance(0)
    attention_back(qkv_t, p_t, dmix, dqkv, T_GROUPS)
    advance(9)
    advance(3)
    advance(2)
    advance(1)
    advance(0)
    qkv_back(dqkv, u_t, R.wt_t, du, T_ROWS)
    for i in (14, 15, 16):
        advance(i)
    advance(4)
    advance(3)
    advance(2)
    advance(1)
    advance(0)
    R.dgain_t[...] = jnp.zeros((1, width), F32)

    def finish_time(r):
        rows = pl.ds(r, 80)
        scaled, factor = stats(rows_x[rows, :])
        grad = du[rows, :]
        R.dgain_t[...] += jnp.sum(grad * scaled, axis=0, keepdims=True)
        df[rows, :] += norm_back(grad, R.gain_t[...], scaled, factor)

    tiles(T_ROWS, 80, finish_time)
    to_frame_order(df, R.dx_v, R.perm)
    store = pltpu.make_async_copy(R.dx_v, R.dx, R.lo.at[2])
    store.start()
    for n, gain in enumerate((R.dgain_t, R.dgain_s, R.dgain_m)):
        R.gains[0, n : n + 1, :] = gain[...]

    def gain_part(j):
        peer = ([peer_c, peer_y] + bits)[j]
        return remote(R.gains.at[0], R.gains.at[1 + j], (R.gg_s, R.gg_r), j, peer)

    def gain_steps():
        for j in range(2 + levels):
            gain_part(j).start()
            yield
            gain_part(j).wait()
            R.gains[0] = R.gains[0] + R.gains[1 + j]

    finish_units(gain_steps())
    R.gains_out[...] = R.gains[0]
    all_wait(ex_out)
    store.wait()


def local(
    patches, cls_token, keep_mask, gain_time, qkv_time, proj_time, temporal_fc, gain_space, qkv_space, proj_space,
    gain_mlp, mlp_in, mlp_out, cotangent, cls_cotangent,
):
    _, frames, count, width = patches.shape
    members = lax.axis_size("head")
    me = lax.axis_index("head")
    heads_here, hd = qkv_time.shape[1], qkv_time.shape[3]
    part = heads_here * hd
    at = members * count

    def flat_t(w):
        return jnp.transpose(w, (2, 1, 3, 0)).reshape(3, part, width)

    keep = keep_mask[0].astype(F32)
    here = lax.dynamic_slice_in_dim(keep, me * count, count, axis=1)
    kt = jnp.pad(here.T.reshape(-1), (0, T_ROWS - frames * count))
    kt_col = kt[:, None]
    kt_row = jnp.stack([jnp.pad(kt[s : s + n], (0, 128 - n)) for s, n in T_GROUPS])[:, None, :]
    mine = lax.dynamic_slice_in_dim(keep, me * 2, 2, axis=0)
    ks_row = jnp.pad(mine, ((0, 0), (0, 256 - at))).at[:, at].set(1.0)[:, None, :]
    first_only = jnp.array([1.0, 0.0], F32)[:, None]
    ks_col = jnp.concatenate([mine, first_only, jnp.zeros((2, SEG - 1 - at), F32)], axis=1).reshape(-1, 1)
    row_id = jnp.arange(S_ROWS)
    once = jnp.where((row_id == at) & (me != 0), 0.0, 1.0).astype(F32)[:, None]

    small = dict(
        cls=cls_token, ccot=cls_cotangent.astype(F32), gain_t=gain_time[None], gain_s=gain_space[None],
        gain_m=gain_mlp[None], kt_row=kt_row, kt_col=kt_col, ks_row=ks_row, ks_col=ks_col, once=once,
    )
    large = dict(
        patches=patches[0], cot=cotangent[0], wt_t_in=flat_t(qkv_time), pj_t_in=proj_time.reshape(-1, width),
        fc_in=temporal_fc, wt_s_in=flat_t(qkv_space), pj_s_in=proj_space.reshape(-1, width), w1_in=mlp_in, w2_in=mlp_out,
    )
    frame_rows, square, row = (frames, count, width), (width, width), (1, width)
    t_rows, s_rows = (T_ROWS, width), (S_ROWS, width)
    in_hbm = dict(
        out=(frame_rows, BF16), dx=(frame_rows, F32), dw1=(square, BF16), dw2=(square, BF16), dfc=(square, BF16),
        dsp=((4, part, width), BF16), dti=((4, part, width), BF16),
    )
    in_vmem = dict(ocls=(row, BF16), dcls=(row, F32), gains_out=((8, width), F32))
    levels = lax.axis_size("clip").bit_length() - 1
    vmem = dict(
        wt_t=((3, width, width), BF16), pj_t=(square, BF16), fc=(square, BF16), wt_s=((3, width, width), BF16),
        pj_s=(square, BF16), w1=((4, width, width), BF16), w2=((4, width, width), BF16),
        patches_v=(frame_rows, BF16), u_t=(t_rows, BF16), qkv_t=((T_ROWS, 3 * width), BF16),
        p_t=((6, 4, 224, 128), F32), mix_t=(t_rows, BF16), att_t=(t_rows, BF16),
        rows_x=(s_rows, F32), rows_s=(s_rows, F32), rows_c=(s_rows, F32), rows_a=(s_rows, F32), rows_d=(s_rows, F32),
        low_a=(s_rows, BF16), low_b=(s_rows, BF16), low_c=(s_rows, BF16), low_d=(s_rows, BF16),
        u_s=(s_rows, BF16), qkv_s=((S_ROWS, 3 * width), BF16), mix_s=(s_rows, BF16),
        p_s=((6, 2, 416, 256), F32), dqkv=((S_ROWS, 3 * width), BF16),
        perm=((width // 128, T_ROWS, 128), F32), dx_v=(frame_rows, F32), send_a=(frame_rows, BF16),
        send_b=(frame_rows, BF16), got_first=(frame_rows, BF16), got_cot=(frame_rows, BF16),
        cls_sum=((4, 8, width), F32), dcls_sum=((4, 8, width), F32),
        dgain_t=(row, F32), dgain_s=(row, F32), dgain_m=(row, F32), gains=((3 + levels, 8, width), F32),
        near=((9, 2, part, width), BF16),
    )
    pairs = dict(wy=6, wx=6, wc=6, wf=6, wg=6, ex=12, row=6, gc=34, gy=17, gb=17 * levels, gq=17, gh=17, gf=3, gg=2 + levels)
    sems = dict(wo=6, exo=4, lo=3, go=17)
    for name, n in pairs.items():
        sems[name + "_s"] = n
        sems[name + "_r"] = n
    flags = dict(free_y=17, free_b=17 * levels)
    names = [*large, *small, *in_hbm, *in_vmem, *vmem, *sems, *flags]
    hbm, vm = pl.BlockSpec(memory_space=pl.ANY), pl.BlockSpec(memory_space=pltpu.VMEM)
    output, dx, d_w1, d_w2, d_fc, d_sp, d_ti, out_cls, cls_grad, gains = pl.pallas_call(
        partial(whole_step, names, frames),
        out_shape=[jax.ShapeDtypeStruct(s, d) for s, d in [*in_hbm.values(), *in_vmem.values()]],
        in_specs=[hbm] * len(large) + [vm] * len(small),
        out_specs=[hbm] * len(in_hbm) + [vm] * len(in_vmem),
        scratch_shapes=[pltpu.VMEM(s, d) for s, d in vmem.values()]
        + [pltpu.SemaphoreType.DMA((n,)) for n in sems.values()]
        + [pltpu.SemaphoreType.REGULAR((n,)) for n in flags.values()],
        compiler_params=pltpu.CompilerParams(collective_id=0, has_side_effects=True, vmem_limit_bytes=60 << 20),
    )(*large.values(), *small.values())

    def untie(own):
        return jnp.transpose(own.astype(F32).reshape(3, heads_here, hd, width), (3, 1, 0, 2))

    return (
        output[None], out_cls, dx[None], cls_grad, gains[0], untie(d_ti[1:]), d_ti[0].astype(F32).reshape(proj_time.shape),
        d_fc.astype(F32), gains[1], untie(d_sp[1:]), d_sp[0].astype(F32).reshape(proj_space.shape), gains[2],
        d_w1.astype(F32), d_w2.astype(F32),
    )


def solution(mesh):
    rows, wide, by_head = P("clip", None, "head", None), P("clip", None), P(None, "head", None, None)
    in_specs = (
        rows, wide, P("clip", None, None), P(), by_head, P("head", None, None), P(), P(), by_head,
        P("head", None, None), P(), P(None, "head"), P("head", None), rows, wide,
    )
    out_specs = (
        rows, wide, rows, wide, P(), by_head, P("head", None, None), P(), P(), by_head,
        P("head", None, None), P(), P(None, "head"), P("head", None),
    )
    return jax.shard_map(local, mesh=mesh, in_specs=in_specs, out_specs=out_specs, check_vma=False)
```

time: 597 us -> 320 us (0.54)
  waiting for transfers between devices: 259 us -> 0 us
  Pallas kernels: 116 us -> 284 us
  blocking collectives: 71.1 us -> 0 us
  other arithmetic: 49.4 us -> 14.5 us
  local copies, waits for them, and re-layouts: 51.7 us -> 19.3 us
  starting transfers between devices: 31.5 us -> 0 us
  between operations: 17.9 us -> 1.44 us
    pallas_call x5 -> x1, Pallas kernels: 116 us -> 284 us  [local(): pl.pallas_call(partial(whole_step, names, frames), out_shape=[jax.ShapeDt...]
    ppermute x32 -> x0, waiting for transfers between devices: 132 us -> none  [swap(): return lax.ppermute(x, 'head', [(i, i ^ bit) for i in range(members)])]
    psum x2 -> x0, waiting for transfers between devices: 123 us -> none  [the longest x1 123 us: reduce(): return lax.psum(own, 'clip').astype(F32)]
    psum x2 -> x0, blocking collectives: 57.4 us -> none  [the longest x1 45.4 us: local(): lax.psum((dg_time[0], dg_space[0], dg_mlp[0]), ('clip', 'head'))]
    ppermute x32 -> x0, starting transfers between devices: 20.6 us -> none  [swap(): return lax.ppermute(x, 'head', [(i, i ^ bit) for i in range(members)])]
    add x14 -> x0, other arithmetic: 15.1 us -> none  [the longest x6 8.78 us: reduce(): pair = g[0::2] + swap(g[1::2], 1)]
    all_to_all x1 -> x0, blocking collectives: 13.7 us -> none  [exchange(): return lax.all_to_all(x, 'head', split_axis=0, concat_axis=0, tiled=True)]
    another operation x5 -> x1, other arithmetic: 12.9 us -> 0.64 us  [the longest x4 12.3 us: gather(): return jnp.stack([w, swap(w, 1), far, swap(far, 1)])]
  transfers between devices with their start and end apart: 37 -> 0, of which waited for: 11 -> 0; matrix products, arithmetic and copies ran while one was open for 14% -> 0% of each run, Pallas kernels for 10% -> 0%
where the time goes in v2:
time: 320 us; the launch traced here: 319 us
  Pallas kernels  284 us (89%)
  local copies, waits for them, and re-layouts  19.3 us (6%)
  other arithmetic  14.5 us (5%)
    pallas_call x1, Pallas kernels, local(): pl.pallas_call(partial(whole_step, names, frames), out_shape=[jax.ShapeDt...  284 us

profile of v2, /device:TPU:0, one launch (start us, length us, event | category | flops | bytes accessed | tf_op | source)
XLA Modules:
  0.0 319.0 jit_solution(10143742375888308603)
XLA Ops:
  2.0 1.3 broadcast_in_dim.38.refs_11_
  3.3 1.3 broadcast_in_dim.39.refs_12_
  4.6 1.3 broadcast_in_dim.40.refs_13_
  5.9 1.3 convert_element_type.42.refs_10_
  7.1 0.7 convert_element_type.43
  7.9 0.8 maximum_maximum_fusion
  11.0 0.8 copy.46.refs_15_
  11.8 0.9 reshape.127.refs_17_
  12.7 0.7 fusion.1.refs_18_
  13.4 2.2 copy.40
  15.7 1.0 copy.41
  16.6 1.3 copy_bitcast_fusion.2
  18.0 283.7 %shard_map.263 = (bf16[8,49,768]{2,1,0:T(8,128)(2,1)}, f32[8,49,768]{2,1,0:T(8,128)}, bf16[768,768]{1,0:T(8,128)(2,1)}, bf16[768,768]{1,0:T(8,128)(2,1)}, bf16[7...) custom-call(bf16[8,49,768]{2,1,0:T(8,128)(2,1)} %get-tuple-element.8, ...), custom_call_target="tpu_custom_call" | custom-call | tf_op jit(solution)/shard_map/pallas_call | solution.py:849
  301.7 2.1 copy.50
  303.8 1.5 slice_reduce_fusion
  305.3 1.0 slice.67
  306.4 0.9 convert.7
  307.3 0.9 convert.9
  308.2 1.4 copy_bitcast_fusion
  309.6 1.4 copy_bitcast_fusion.1
  311.5 1.4 copy.51
  312.9 1.6 convert_element_type.46
  314.6 1.6 convert_element_type.49
  316.2 1.6 convert_element_type.50
  (53 shorter events, 5.2 us)
Async XLA Ops:
  0.6 15.0 %copy-start.6 = (bf16[768,3,3,64]{0,3,2,1:T(8,128)(2,1)S(1)}, bf16[768,3,3,64]{0,3,2,1:T(8,128)(2,1)}, u32[]{:S(2)}) copy-start(bf16[768,3,3,64]{0,3,2,1:T(8,128)(2,1)} %param.26) | copy-start | bytes 2654212
  8.8 7.8 %copy-start.9 = (f32[2,1,256]{2,1,0:T(1,128)}, f32[2,1,256]{2,1,0:T(1,128)S(1)}, u32[]{:S(2)}) copy-start(f32[2,1,256]{2,1,0:T(1,128)S(1)} %scatter.4.refs_16_) | copy-start | bytes 6148
  13.4 3.2 %copy-start.7 = (bf16[1,8,49,768]{3,1,2,0:T(8,128)(2,1)S(1)}, bf16[1,8,49,768]{3,1,2,0:T(8,128)(2,1)}, u32[]{:S(2)}) copy-start(bf16[1,8,49,768]{3,1,2,0:T(8,128)(2,1)} %param.31) | copy-start | bytes 1806340
  13.4 3.2 %copy-start.8 = (bf16[1,8,49,768]{3,1,2,0:T(8,128)(2,1)S(1)}, bf16[1,8,49,768]{3,1,2,0:T(8,128)(2,1)}, u32[]{:S(2)}) copy-start(bf16[1,8,49,768]{3,1,2,0:T(8,128)(2,1)} %param.18) | copy-start | bytes 1806340
  301.7 4.6 %copy-start.5 = (bf16[4,192,768]{2,1,0:T(8,128)(2,1)S(1)}, bf16[4,192,768]{2,1,0:T(8,128)(2,1)}, u32[]{:S(2)}) copy-start(bf16[4,192,768]{2,1,0:T(8,128)(2,1)} %get-tuple-element.41) | copy-start | bytes 3538948
  303.8 3.4 %copy-start.4 = (bf16[4,192,768]{2,1,0:T(8,128)(2,1)S(1)}, bf16[4,192,768]{2,1,0:T(8,128)(2,1)}, u32[]{:S(2)}) copy-start(bf16[4,192,768]{2,1,0:T(8,128)(2,1)} %get-tuple-element.43) | copy-start | bytes 3538948
  309.6 1.9 copy-start
  311.5 1.4 copy-start.3
  312.9 1.7 copy-start.2
  314.6 1.7 copy-start.1
  316.2 1.6 copy-start.11
  316.2 2.2 copy-start.10

commit v3 on v2

v3 whole, which is shorter than its diff:
```python
from functools import partial
from types import SimpleNamespace

import jax
import jax.numpy as jnp
from jax import lax
from jax.experimental import pallas as pl
from jax.experimental.pallas import tpu as pltpu
from jax.sharding import PartitionSpec as P

EPSILON = 1e-06
NEGATIVE = -1e30
F32 = jnp.float32
BF16 = jnp.bfloat16


def nn(a, b):
    return lax.dot_general(a, b, (((1,), (0,)), ((), ())), preferred_element_type=F32)


def nt(a, b):
    return lax.dot_general(a, b, (((1,), (1,)), ((), ())), preferred_element_type=F32)


def tn(a, b):
    return lax.dot_general(a, b, (((0,), (0,)), ((), ())), preferred_element_type=F32)


def tiles(total, size, body):
    def step(i, carry):
        body(pl.multiple_of(i * size, size))
        return carry

    lax.fori_loop(0, total // size, step, 0)


def stats(x):
    center = x - jnp.mean(x, axis=-1, keepdims=True)
    factor = lax.rsqrt(jnp.mean(center * center, axis=-1, keepdims=True) + EPSILON)
    return center * factor, factor


def norm_back(grad, gain, scaled, factor):
    weighted = grad * gain
    inner = weighted - jnp.mean(weighted, axis=-1, keepdims=True)
    return factor * (inner - scaled * jnp.mean(weighted * scaled, axis=-1, keepdims=True))


def pair_masks():
    lane = lax.broadcasted_iota(jnp.int32, (1, 128), 1)
    return (lane < 64).astype(F32).astype(BF16), (lane >= 64).astype(F32).astype(BF16)


def stacked(x):
    low, high = pair_masks()
    return jnp.concatenate([x * low, x * high], axis=0)


def unstacked(x):
    rows = x.shape[0] // 2
    lane = lax.broadcasted_iota(jnp.int32, (1, 128), 1)
    return jnp.where(lane < 64, x[:rows], x[rows:])


def norm_rows(x_ref, gain_ref, u_ref, total, chunk):
    def body(r):
        rows = pl.ds(r, chunk)
        scaled, _ = stats(x_ref[rows, :])
        u_ref[rows, :] = (scaled * gain_ref[...]).astype(BF16)

    tiles(total, chunk, body)


def project_qkv(u_ref, wt_ref, qkv_ref, rows, first, last):
    width = u_ref.shape[1]
    size = (last - first) * 64

    def body(t, carry):
        scale = jnp.where(t == 0, 0.125, 1.0)
        out = nt(u_ref[:rows, :], wt_ref[t, first:last].reshape(size, width)) * scale
        qkv_ref[:rows, pl.ds(pl.multiple_of(t * width + first * 64, 128), size)] = out.astype(BF16)
        return carry

    lax.fori_loop(0, 3, body, 0)


def columns(ref, cols):
    part = ref[:, :, cols]
    return part.reshape(part.shape[0] * part.shape[1], part.shape[2])


def rows_of(ref, n):
    part = ref[pl.ds(n // 64, 4)]
    return part.reshape(256, part.shape[2])


def qkv_back(dqkv_ref, wt_ref, du_ref, rows):
    width = du_ref.shape[1]

    def back(n):
        cols = pl.ds(n, 256)
        total = nn(dqkv_ref[:rows, :width], columns(wt_ref.at[0], cols))
        total += nn(dqkv_ref[:rows, width : 2 * width], columns(wt_ref.at[1], cols))
        total += nn(dqkv_ref[:rows, 2 * width :], columns(wt_ref.at[2], cols))
        du_ref[:rows, cols] = total

    tiles(width, 256, back)


def qkv_grad(dqkv_ref, u_ref, wt_ref, rows):
    width = u_ref.shape[1]

    def grad(i, carry):
        cols = pl.ds(pl.multiple_of(i * 256, 256), 256)
        out = tn(dqkv_ref[:rows, cols], u_ref[:rows, :]).astype(BF16)
        wt_ref[i // 3, pl.ds((i % 3) * 4, 4)] = out.reshape(4, 64, width)
        return carry

    lax.fori_loop(0, 9, grad, 0)


def softmax(scores):
    highest = jnp.max(scores, axis=-1, keepdims=True)
    weights = jnp.exp(scores - highest)
    return weights * (1.0 / jnp.sum(weights, axis=-1, keepdims=True))


def attention(qkv_ref, p_ref, mix_ref, groups, bias_of, first, last):
    width = mix_ref.shape[1]

    def body(hp, carry):
        qc = pl.ds(pl.multiple_of(hp * 128, 128), 128)
        kc = pl.ds(pl.multiple_of(width + hp * 128, 128), 128)
        vc = pl.ds(pl.multiple_of(2 * width + hp * 128, 128), 128)
        for g, (start, size) in enumerate(groups):
            rows = pl.ds(start, size)
            prob = softmax(nt(stacked(qkv_ref[rows, qc]), qkv_ref[rows, kc]) + bias_of(g, size))
            p_ref[hp, g, : 2 * size, :size] = prob
            mix_ref[rows, qc] = unstacked(nn(prob.astype(BF16), qkv_ref[rows, vc])).astype(BF16)
        return carry

    lax.fori_loop(first, last, body, 0)


def attention_back(qkv_ref, p_ref, dmix_ref, dqkv_ref, groups, first, last):
    width = dmix_ref.shape[1]

    def body(hp, carry):
        qc = pl.ds(pl.multiple_of(hp * 128, 128), 128)
        kc = pl.ds(pl.multiple_of(width + hp * 128, 128), 128)
        vc = pl.ds(pl.multiple_of(2 * width + hp * 128, 128), 128)
        for g, (start, size) in enumerate(groups):
            rows = pl.ds(start, size)
            up = stacked(dmix_ref[rows, qc])
            prob = p_ref[hp, g, : 2 * size, :size]
            dprob = nt(up, qkv_ref[rows, vc])
            delta = jnp.sum(prob * dprob, axis=-1, keepdims=True)
            dscore = (prob * (dprob - delta)).astype(BF16)
            dqkv_ref[rows, qc] = (unstacked(nn(dscore, qkv_ref[rows, kc])) * 0.125).astype(BF16)
            dqkv_ref[rows, kc] = tn(dscore, stacked(qkv_ref[rows, qc])).astype(BF16)
            dqkv_ref[rows, vc] = tn(prob.astype(BF16), up).astype(BF16)
        return carry

    lax.fori_loop(first, last, body, 0)


T_ROWS = 400
T_GROUPS = ((0, 96), (96, 96), (192, 96), (288, 112))
SEG = 208
S_ROWS = 416
S_GROUPS = ((0, 208), (208, 208))


def time_bias(kcol, size):
    row = lax.broadcasted_iota(jnp.int32, (size, size), 0)
    col = lax.broadcasted_iota(jnp.int32, (size, size), 1)
    kept = jnp.sum(jnp.where(row == col, kcol, 0.0), axis=0, keepdims=True)
    ok = ((row // 8) == (col // 8)) & ((kept > 0.0) | (row == col))
    return jnp.where(ok, 0.0, NEGATIVE)


def patch_keep(keep_ref, head, count, frames):
    total = keep_ref.shape[1]
    row = lax.broadcasted_iota(jnp.int32, (T_ROWS, total), 0)
    col = lax.broadcasted_iota(jnp.int32, (T_ROWS, total), 1)
    pick = ((row // frames + head * count == col) & (row < frames * count)).astype(F32).astype(BF16)
    by_frame = nt(pick, keep_ref[...].astype(F32).astype(BF16))
    row = lax.broadcasted_iota(jnp.int32, (T_ROWS, frames), 0)
    col = lax.broadcasted_iota(jnp.int32, (T_ROWS, frames), 1)
    return jnp.sum(jnp.where(row % frames == col, by_frame, 0.0), axis=1, keepdims=True)


def space_bias(krow_ref, g):
    return (krow_ref[g, :, :SEG] - 1.0) * (-NEGATIVE)


def to_patch_order(src_ref, dst_ref, perm_ref):
    frames, count, width = src_ref.shape
    used = frames * count
    for j in range(width // 128):
        for f in range(frames):
            perm_ref[j, pl.ds(f, count, stride=frames), :] = src_ref[f, :, j * 128 : (j + 1) * 128].astype(F32)
        dst_ref[:used, j * 128 : (j + 1) * 128] = perm_ref[j, :used, :]
    dst_ref[used:T_ROWS, :] = jnp.zeros((T_ROWS - used, width), F32)


def to_frame_order(src_ref, dst_ref, perm_ref):
    frames, count, width = dst_ref.shape
    for j in range(width // 128):
        used = frames * count
        perm_ref[j, :used, :] = src_ref[:used, j * 128 : (j + 1) * 128].astype(F32)
        for f in range(frames):
            out = perm_ref[j, pl.ds(f, count, stride=frames), :]
            dst_ref[f, :, j * 128 : (j + 1) * 128] = out.astype(dst_ref.dtype)


def gather_frames(got_ref, cls_row, out_ref):
    sources, count = got_ref.shape[0] // 2, got_ref.shape[1]
    for f in range(2):
        base = f * SEG
        for s in range(sources):
            out_ref[base + s * count : base + (s + 1) * count, :] = got_ref[2 * s + f].astype(F32)
        at = base + sources * count
        out_ref[at : at + 1, :] = cls_row[f]
        out_ref[at + 1 : base + SEG, :] = jnp.zeros((SEG - 1 - sources * count, out_ref.shape[1]), F32)


def scatter_frames(x_ref, send_ref):
    sources, count = send_ref.shape[0] // 2, send_ref.shape[1]
    for f in range(2):
        for s in range(sources):
            at = f * SEG + s * count
            send_ref[2 * s + f] = x_ref[at : at + count, :].astype(send_ref.dtype)


def cls_attention(qkv_ref, krow_ref, at, width):
    lane = lax.broadcasted_iota(jnp.int32, (16, width), 1) // 64
    own = (lane == lax.broadcasted_iota(jnp.int32, (16, width), 0)).astype(F32)
    total = jnp.zeros((1, width), F32)
    for f in range(2):
        q = qkv_ref[f * SEG + at : f * SEG + at + 1, :width].astype(F32)
        k = qkv_ref[f * SEG : (f + 1) * SEG, width : 2 * width]
        v = qkv_ref[f * SEG : (f + 1) * SEG, 2 * width :]
        prob = softmax(nt((own * q).astype(BF16), k) + space_bias(krow_ref, f))
        total += jnp.sum(own * nn(prob.astype(BF16), v), axis=0, keepdims=True)
    return total


def blocks_swapped(x, distance):
    width = x.shape[1]
    quarter = width // 4
    order = [i ^ distance for i in range(4)]
    return jnp.concatenate([x[:, i * quarter : (i + 1) * quarter] for i in order], axis=1)


def set_row(ref, base, at, row, dtype):
    start = base + at // 16 * 16
    pick = lax.broadcasted_iota(jnp.int32, (16, 1), 0) == at % 16
    kept = ref[start : start + 16, :].astype(F32)
    ref[start : start + 16, :] = jnp.where(pick, jnp.broadcast_to(row, kept.shape), kept).astype(dtype)


MESH = pl.DeviceIdType.MESH

ROUTES = (0, 2, 0, 1, 0, 0, 1, 2, 0, 0, 0, 0, 0, 0, 0)
ORDER = (
    (0, 1),
    (2, 3, 0, 1),
    (4, 5, 2, 3),
    (0, 1, 4),
    (),
    (),
    (),
    (2, 3),
    (0, 1),
    (4, 2),
    (0, 5),
    (6, 8, 9, 7, 0, 1, 2, 3, 4),
    (10, 6, 8, 15),
    (11, 0, 1, 9, 7, 10),
    (2, 3, 4, 5, 11),
    (1, 6),
    (0,),
    (2, 5, 8, 7),
    (12, 13, 14, 3),
    (12, 13, 14, 9, 16, 8, 4, 1, 2, 10, 5, 9, 16, 3, 11, 15, 7, 10, 8, 4, 6, 16, 3, 9, 5, 10, 11, 12, 6, 16,
     8, 4, 9, 5, 13, 12, 11, 16, 10, 8, 6, 5, 14, 9, 7, 16, 12, 13, 10, 11, 8, 6, 14, 16, 12, 13, 11, 9, 14,
     7, 12, 16, 10, 13, 6, 14, 11, 7, 13, 16, 10, 14, 12, 10, 7, 13, 14, 16),
)


def whole_step(names, frames, *refs):
    R = SimpleNamespace(**dict(zip(names, refs)))
    clip, head = lax.axis_index("clip"), lax.axis_index("head")
    digit = (clip % 2, clip // 2 % 2, clip // 4 % 2)
    side, turn = digit[0], digit[1]
    width = R.wt_t.shape[3]
    count = R.patches.shape[0] // frames
    at = 4 * count
    peer_c, peer_y, peer_d = (clip, head ^ 1), (clip, head ^ 2), (clip, head ^ 3)
    levels = lax.axis_size("clip").bit_length() - 1
    bits = [(clip ^ (1 << j), head) for j in range(levels)]

    def part(ref, q, n):
        return ref.at[:, pl.ds(q * 16, n * 16), :]

    def hidden_tile(w1, w2, i, q, n):
        t = (i - 8) // 2
        if i % 2:
            return w1.at[:, pl.ds(q * 16, n * 16), pl.ds(t * 256, 256)]
        return part(w2.at[pl.ds(t * 4, 4)], q, n)

    def slot(i, s, q=0, n=4):
        if i >= 8:
            return hidden_tile(R.w1.at[s], R.w2.at[s], i, q, n)
        wt, pj = (R.wt_t, R.pj_t) if i < 4 else (R.wt_s, R.pj_s)
        if i % 4 == 3:
            return part(pj.at[pl.ds(s * 3, 3)], q, n)
        return part(wt.at[:, s * 3 + i % 4], q, n)

    def source(i, q=0, n=4):
        if i >= 8:
            return hidden_tile(R.w1_in, R.w2_in, i, q, n)
        wt, pj = (R.wt_t_in, R.pj_t_in) if i < 4 else (R.wt_s_in, R.pj_s_in)
        return part(pj if i % 4 == 3 else wt.at[i % 4], q, n)

    def remote(src, dst, sems, index, peer):
        return pltpu.make_async_remote_copy(
            src_ref=src, dst_ref=dst, send_sem=sems[0].at[index], recv_sem=sems[1].at[index],
            device_id=peer, device_id_type=MESH,
        )

    mine = side + 2 * turn

    def y_copy(i):
        return remote(source(i, mine, 1), slot(i, 2, mine, 1), (R.wy_s, R.wy_r), i, peer_y)

    def clip_copies(i):
        quarter = slot(i, 2, mine, 1)
        near = (bits[0], bits[1], (clip ^ 3, head))
        return [remote(quarter, quarter, (R.wx_s, R.wx_r), 3 * i + n, peer) for n, peer in enumerate(near)]

    def c_copy(i):
        return remote(source(i), slot(i, 1), (R.wc_s, R.wc_r), i, peer_c)

    def f_copy(i):
        return remote(slot(i, 2), slot(i, 3), (R.wf_s, R.wf_r), i, peer_c)

    def own_copy(i):
        return pltpu.make_async_copy(source(i), slot(i, 0), R.wo.at[i])

    def pass_near(*pieces):
        for i in pieces:
            y_copy(i).wait_recv()
            for copy in clip_copies(i):
                copy.start()

    def pass_far(*pieces):
        for i in pieces:
            for copy in clip_copies(i):
                copy.wait_recv()
            f_copy(i).start()

    def ready_near(*pieces):
        for i in pieces:
            own_copy(i).wait()
            c_copy(i).wait_recv()

    def ready_far(*pieces):
        for i in pieces:
            f_copy(i).wait_recv()

    def sent(*pieces):
        for i in pieces:
            y_copy(i).wait_send()
            c_copy(i).wait_send()
            f_copy(i).wait_send()
            for copy in clip_copies(i):
                copy.wait_send()

    def exchange(k, src, dst):
        here = pl.ds(2 * head, 2)
        copies = []
        for r, peer in ((2, peer_y), (3, peer_d), (1, peer_c)):
            there = pl.ds(2 * (head ^ r), 2)
            copies.append(remote(src.at[there], dst.at[here], (R.ex_s, R.ex_r), 3 * k + r - 1, peer))
        copies.append(pltpu.make_async_copy(src.at[here], dst.at[here], R.exo.at[k]))
        return copies

    def all_start(copies):
        for copy in copies:
            copy.start()

    def all_wait(copies):
        for copy in copies:
            copy.wait()

    def sum_rows(k, buf, swapped):
        copies = [
            remote(buf.at[0], buf.at[r], (R.row_s, R.row_r), 3 * k + r - 1, peer)
            for r, peer in ((2, peer_y), (3, peer_d), (1, peer_c))
        ]
        all_start(copies)

        def finish():
            all_wait(copies)
            terms = [buf[r] for r in range(4)]
            if swapped:
                terms = [terms[0]] + [blocks_swapped(terms[r], r) for r in (1, 2, 3)]
            total = (terms[0] + terms[1]) + (terms[2] + terms[3])
            return total[0:1, :]

        return finish

    def unit(i):
        if i < 6:
            n = i // 2
            if i % 2:
                return lambda s, q=0, k=4: R.w1.at[s, :, pl.ds(q * 16, k * 16), pl.ds(n * 256, 256)]
            return lambda s, q=0, k=4: part(R.w2.at[s, pl.ds(n * 4, 4)], q, k)
        if i == 10:
            return lambda s, q=0, k=4: part(R.fc.at[pl.ds((head ^ s) * 3, 3)], q, k)
        wt, pj = (R.wt_s, R.pj_s) if i < 10 else (R.wt_t, R.pj_t)
        n = i - 6 if i < 10 else i - 11
        if n == 0:
            return lambda s, q=0, k=4: part(pj.at[pl.ds(s * 3, 3)], q, k)
        return lambda s, q=0, k=4: part(wt.at[:, s * 3 + n - 1], q, k)

    def result(i, q, k):
        if i < 6:
            n = i // 2
            if i % 2:
                return R.dw1.at[:, pl.ds(q * 16, k * 16), pl.ds(n * 256, 256)]
            return part(R.dw2.at[pl.ds(n * 4, 4)], q, k)
        if i == 10:
            return part(R.dfc.at[pl.ds(head * 3, 3)], q, k)
        wt, pj = (R.dwt_s, R.dpj_s) if i < 10 else (R.dwt_t, R.dpj_t)
        n = i - 6 if i < 10 else i - 11
        return part(pj if n == 0 else wt.at[n - 1], q, k)

    def near_slot(i, k):
        if i < 6:
            return (R.near_c if i % 2 else R.near_b).at[i // 2, k]
        if i < 9:
            return R.near_b.at[i - 6, k, pl.ds(0, 3)]
        return R.near_a.at[i - 9, k]

    def add(dst, src):
        def body(r, carry):
            dst[r] = dst[r] + src[r]
            return carry

        lax.fori_loop(0, dst.shape[0], body, 0)

    def steps_of(i):
        u, route = unit(i), ROUTES[i]
        a, b = (1, 2) if route == 2 else (0, 1)
        half = 2 * digit[a]
        quarter = half + digit[b]
        counts = [0, 0]

        def copy(src, dst, peer):
            counts[0] += 1
            return remote(src, dst, (R.gu_s, R.gu_r), i * 16 + counts[0] - 1, peer)

        def land(k):
            at_q = counts[1]
            counts[1] += k
            s, q = ((1, at_q) if at_q < 4 else (3, at_q - 4) if at_q < 8 else (2, at_q - 8))
            return u(s, q, k), (s, q, k)

        steps = [([copy(u(1), near_slot(i, 0), peer_c), copy(u(3), near_slot(i, 1), peer_c)],
                  [(u(2), near_slot(i, 1)), (u(0), near_slot(i, 0))], None)]
        peers = []
        kept, joined = (0, 4), False
        whole_bits = [j for j in range(levels) if j not in (a, b)]
        order = ((-1, a, b), (a, -1, b), (a, b, -1))[route]
        for bit in list(order) + whole_bits:
            copies, sums = [], []
            if bit == -1:
                spot, (s, q, k) = land(kept[1])
                copies.append(copy(u(2, *kept), u(s ^ 2, q, k) if i == 10 else spot, peer_y))
                sums.append((u(0, *kept), spot))
                joined = True
                peers.append(peer_y)
            else:
                if bit == a:
                    kept, other = (half, 2), (2 - half, 2)
                elif bit == b:
                    kept, other = (quarter, 1), (half + 1 - digit[b], 1)
                else:
                    other = kept
                for s in (0,) if joined else (0, 2):
                    spot, _ = land(other[1])
                    copies.append(copy(u(s, *other), spot, bits[bit]))
                    sums.append((u(s, *kept), spot))
                peers.append(bits[bit])
            steps.append((copies, sums, len(peers) - 1))
        mine_q, there_q, rows = u(0, quarter, 1), result(i, quarter, 1), result(i, half, 2)
        steps.append(([copy(mine_q, there_q, bits[b]), pltpu.make_async_copy(mine_q, there_q, R.go.at[i])], [], None))
        steps.append(([copy(rows, rows, bits[a])], [], None))
        if i == 10:
            ours, far = R.dfc.at[pl.ds(head * 3, 3)], R.dfc.at[pl.ds((head ^ 2) * 3, 3)]
            steps.append(([copy(ours, ours, peer_y), copy(ours, ours, peer_c)], [], None))
            steps.append(([copy(far, far, peer_c)], [], None))
        return steps, peers

    units = [None] * 15
    stage = [0] * 15

    def tell(i, first, last):
        peers = units[i][1]
        for k in range(first, min(last, len(peers))):
            pl.semaphore_signal(R.free.at[i * 8 + k], inc=1, device_id=peers[k], device_id_type=MESH)

    def land_step(i):
        steps, _ = units[i]
        copies, sums, _ = steps[stage[i] - 1]
        all_wait(copies)
        if stage[i] == 1:
            tell(i, 0, 4)
        for dst, src in sums:
            add(dst, src)
        if stage[i] == 4:
            tell(i, 4, 8)

    landed = [0] * 15

    def advance(i):
        if units[i] is None:
            units[i] = steps_of(i)
        steps, _ = units[i]
        if stage[i] > landed[i]:
            land_step(i)
            landed[i] = stage[i]
        if stage[i] < len(steps):
            copies, _, credit = steps[stage[i]]
            if credit is not None:
                pl.semaphore_wait(R.free.at[i * 8 + credit], 1)
            all_start(copies)
        stage[i] += 1

    def join_core(i):
        if stage[i] == 1 and landed[i] == 0:
            land_step(i)
            landed[i] = 1

    extra = {}

    def service(k):
        for i in ORDER[k]:
            if i < 15:
                advance(i)
            else:
                next(extra[i], None)

    def finish_units():
        while any(stage[i] < 1 + len(units[i][0]) for i in range(15)):
            for i in reversed(range(15)):
                done = [stage[j] >= 1 + len(units[j][0]) for j in (i, i - 1)]
                if not done[0] and (i == 0 or done[1] or stage[i] < stage[i - 1]):
                    advance(i)
        for steps in extra.values():
            for _ in steps:
                pass

    barrier = pltpu.get_barrier_semaphore()
    for peer in [peer_c, peer_y, peer_d, (clip ^ 3, head)] + bits:
        pl.semaphore_signal(barrier, inc=1, device_id=peer, device_id_type=MESH)
    pl.semaphore_wait(barrier, 4 + levels)

    loads = (
        (R.patches, R.patches_v.at[pl.ds(0, frames * count)]), (R.keep, R.keep_v), (R.cot, R.low_d.at[pl.ds(0, frames * count)]), (R.fc_in, R.fc),
    )
    loads = [pltpu.make_async_copy(src, dst, R.lo.at[i]) for i, (src, dst) in enumerate(loads)]
    for i in range(3):
        loads[i].start()
    for i in range(14):
        y_copy(i).start()
    for i in range(14):
        own_copy(i).start()
        c_copy(i).start()
    loads[3].start()

    rows_x, first = R.rows_x, R.rows_s
    qkv_t, p_t, mix_t, att_t, u_t = R.qkv_t, R.p_t, R.mix_t, R.att_t, R.u_t
    patches, gains = R.patches_v, R.rows_in
    gain_t, gain_s, gain_m = gains.at[0:1], gains.at[1:2], gains.at[2:3]
    used = frames * count
    loads[0].wait()
    patches[used:, :] = jnp.zeros((T_ROWS - used, width), BF16)

    def norm_time(r):
        rows = pl.ds(r, 80)
        scaled, _ = stats(patches[rows, :].astype(F32))
        u_t[rows, :] = (scaled * gain_t[...]).astype(BF16)

    tiles(T_ROWS, 80, norm_time)
    pass_near(0)
    loads[1].wait()
    keep_col = patch_keep(R.keep_v, head, count, frames)
    R.kt_col[...] = keep_col
    for g, (start, size) in enumerate(T_GROUPS):
        R.bias_t[g, :size, :size] = time_bias(keep_col[start : start + size], size)
    R.ks_row[...] = jnp.zeros_like(R.ks_row)
    lane = lax.broadcasted_iota(jnp.int32, (1, 256), 1)
    row = lax.broadcasted_iota(jnp.int32, (SEG, SEG), 0)
    col = lax.broadcasted_iota(jnp.int32, (SEG, SEG), 1)
    for f in range(2):
        R.ks_row[f, :, :at] = R.keep_v[pl.ds(2 * head + f, 1), :].astype(F32)
        open_row = jnp.where(lane == at, 1.0, R.ks_row[f])
        R.ks_row[f] = open_row
        counted = (row == col) if f == 0 else (row == col) & (col != at)
        R.ks_col[f * SEG : (f + 1) * SEG, :] = jnp.sum(jnp.where(counted, open_row[:, :SEG], 0.0), axis=1, keepdims=True)
    row = lax.broadcasted_iota(jnp.int32, (S_ROWS, 1), 0)
    R.once[...] = jnp.where((row == at) & (head != 0), 0.0, 1.0)
    loads[2].wait()
    to_frame_order(R.low_d, R.send_b, R.perm)
    ex_cot = exchange(1, R.send_b, R.got_cot)
    all_start(ex_cot)
    pass_near(1, 2, 3)

    def time_bias_of(g, size):
        bias = R.bias_t[g, :size, :size]
        return jnp.concatenate([bias, bias], axis=0)

    ready_near(0, 1, 2, 3)
    project_qkv(u_t, R.wt_t, qkv_t, T_ROWS, 0, 6)
    attention(qkv_t, p_t, mix_t, T_GROUPS, time_bias_of, 0, 3)
    pass_near(4, 5, 6, 7)
    pass_far(0, 1, 2, 3)
    ready_far(0, 1, 2, 3)
    pass_near(8, 9)
    project_qkv(u_t, R.wt_t, qkv_t, T_ROWS, 6, 12)
    attention(qkv_t, p_t, mix_t, T_GROUPS, time_bias_of, 3, 6)
    pass_near(10, 11, 12, 13)
    loads[3].wait()

    def project(n):
        cols = pl.ds(n, 256)
        att_t[:, cols] = nn(mix_t[...], columns(R.pj_t, cols)).astype(BF16)

    tiles(width, 256, project)

    def branch(n):
        cols = pl.ds(n, 256)
        first[:T_ROWS, cols] = patches[:, cols].astype(F32) + R.kt_col[...] * nn(att_t[...], columns(R.fc, cols))

    tiles(width, 256, branch)
    to_frame_order(first, R.send_a, R.perm)
    ex_first = exchange(0, R.send_a, R.got_first)
    all_start(ex_first)
    pass_far(4, 5, 6, 7)

    qkv_s, p_s, mix_s, u_s = R.qkv_s, R.p_s, R.mix_s, R.u_s
    all_wait(ex_first)
    cls_row = gains[3:4, :]
    second, cot = R.rows_s, R.rows_c
    gather_frames(R.got_first, (cls_row, cls_row), rows_x)
    norm_rows(rows_x, gain_s, u_s, S_ROWS, 208)
    ready_near(4, 5, 6, 7)
    ready_far(4, 5, 6, 7)
    project_qkv(u_s, R.wt_s, qkv_s, S_ROWS, 0, 12)
    all_wait(ex_cot)
    gather_frames(R.got_cot, (gains[4:5, :], jnp.zeros((1, width), F32)), cot)
    cls_part = cls_attention(qkv_s, R.ks_row, at, width)
    R.cls_sum[0] = jnp.broadcast_to(cls_part, (8, width))
    cls_total = sum_rows(0, R.cls_sum, True)
    attention(qkv_s, p_s, mix_s, S_GROUPS, lambda g, size: space_bias(R.ks_row, g), 0, 6)
    set_row(mix_s, 0, at, cls_total() * (1.0 / frames), BF16)
    set_row(mix_s, SEG, at, jnp.zeros((1, width), F32), BF16)
    pass_far(8, 9)

    def project_space(n):
        cols = pl.ds(n, 256)
        second[:, cols] = rows_x[:, cols] + R.ks_col[...] * nn(mix_s[...], columns(R.pj_s, cols))

    tiles(width, 256, project_space)

    u, uw, dz, dzw = R.low_a, R.low_b, R.low_c, R.low_d
    acc, du = R.rows_a, R.rows_d
    kcol, once = R.ks_col, R.once

    def prepare(r):
        rows = pl.ds(r, 208)
        scaled, _ = stats(second[rows, :])
        low = (scaled * gain_m[...]).astype(BF16)
        u[rows, :] = low
        uw[rows, :] = (low.astype(F32) * once[rows, :]).astype(BF16)
        grad = cot[rows, :] * kcol[rows, :]
        dz[rows, :] = grad.astype(BF16)
        dzw[rows, :] = (grad * once[rows, :]).astype(BF16)

    tiles(S_ROWS, 208, prepare)
    acc[...] = jnp.zeros_like(acc)
    du[...] = jnp.zeros_like(du)
    w1_ref, w2_ref = R.w1, R.w2
    def hidden(s, n):
        cols = pl.ds(n * 256, 256)
        w1 = columns(w1_ref.at[s], cols)
        w2 = rows_of(w2_ref.at[s], n * 256)
        hid = nn(u[...], w1)
        phi = 0.5 + 0.5 * lax.erf(hid * 0.7071067811865476)
        act = (hid * phi).astype(BF16)
        slope = phi + hid * (0.3989422804014327 * jnp.exp(hid * hid * -0.5))
        acc[...] += nn(act, w2)
        dhid = (nt(dz[...], w2) * slope).astype(BF16)
        du[...] += nt(dhid, w1)
        w2_ref[s, n * 4 : n * 4 + 4] = tn(act, dzw[...]).astype(BF16).reshape(4, 64, width)
        w1_ref[s, :, :, cols] = tn(uw[...], dhid).astype(BF16).reshape(width // 64, 64, 256)

    for n in range(width // 256):
        if n:
            pass_far(8 + 2 * n, 9 + 2 * n)
        ready_near(8 + 2 * n, 9 + 2 * n)
        ready_far(8 + 2 * n, 9 + 2 * n)
        sent(8 + 2 * n, 9 + 2 * n)

        def by_slot(s, carry, n=n):
            hidden(s, n)
            return carry

        lax.fori_loop(0, 4, by_slot, 0)
        service(n)
    R.dgain_m[...] = jnp.zeros((1, width), F32)

    def finish_mlp(r):
        rows = pl.ds(r, 208)
        x = second[rows, :]
        scaled, factor = stats(x)
        acc[rows, :] = x + kcol[rows, :] * acc[rows, :]
        grad = du[rows, :]
        R.dgain_m[...] += jnp.sum(grad * scaled * once[rows, :], axis=0, keepdims=True)
        cot[rows, :] += norm_back(grad, gain_m[...], scaled, factor)

    tiles(S_ROWS, 208, finish_mlp)
    R.ocls[...] = acc[at : at + 1, :].astype(BF16)
    scatter_frames(acc, R.send_b)
    ex_out = exchange(2, R.send_b, R.got_cot)

    def out_steps():
        all_start(ex_out)
        yield
        all_wait(ex_out)
        to_patch_order(R.got_cot, rows_x, R.perm)
        R.low_d[:T_ROWS, :] = rows_x[:T_ROWS, :].astype(BF16)
        store_out.start()

    used = frames * count
    store_out = pltpu.make_async_copy(R.low_d.at[pl.ds(0, used)], R.out, R.lo.at[5])
    extra[15] = out_steps()
    service(3)

    dsecond = cot
    low, loww, dmix, dqkv = R.low_a, R.low_b, R.low_c, R.dqkv
    low[...] = (dsecond[...] * kcol[...]).astype(BF16)
    loww[...] = (dsecond[...] * (kcol[...] * once[...])).astype(BF16)
    dcls_second = dsecond[at : at + 1, :]
    set_row(low, SEG, at, dcls_second, BF16)
    sent(4, 5, 6, 7)

    def back_space(n):
        cols = pl.ds(n, 256)
        dmix[:, cols] = nt(low[...], rows_of(R.pj_s, n)).astype(BF16)
        R.pj_s[pl.ds(n // 64, 4)] = tn(mix_s[:, cols], loww[...]).astype(BF16).reshape(4, 64, width)

    tiles(width, 256, back_space)
    service(4)
    dcls_mix = dmix[SEG - 16 : SEG, :].astype(F32)[at - SEG + 16 : at - SEG + 17, :] * (1.0 / frames)
    set_row(dmix, 0, at, dcls_mix, BF16)
    set_row(dmix, SEG, at, dcls_mix, BF16)
    for n in range(3):
        attention_back(qkv_s, p_s, dmix, dqkv, S_GROUPS, 2 * n, 2 * n + 2)
        service(5 + n)
    qkv_back(dqkv, R.wt_s, du, S_ROWS)
    service(8)
    qkv_grad(dqkv, u_s, R.wt_s, S_ROWS)
    service(9)
    R.dcls_sum[0] = jnp.broadcast_to(du[at : at + 1, :] + du[SEG + at : SEG + at + 1, :], (8, width))
    R.dgain_s[...] = jnp.zeros((1, width), F32)
    dfirst = R.rows_a

    def finish_space(r):
        rows = pl.ds(r, 208)
        scaled, factor = stats(rows_x[rows, :])
        grad = du[rows, :]
        R.dgain_s[...] += jnp.sum(grad * scaled, axis=0, keepdims=True)
        dfirst[rows, :] = dsecond[rows, :] + norm_back(grad, gain_s[...], scaled, factor)

    tiles(S_ROWS, 208, finish_space)
    scatter_frames(dfirst, R.send_a)
    for i in range(6):
        join_core(i)
    ex_df = exchange(3, R.send_a, R.got_first)
    all_start(ex_df)
    dcls_total = sum_rows(1, R.dcls_sum, False)
    service(10)

    df = R.rows_s
    all_wait(ex_df)
    service(11)
    to_patch_order(R.got_first, df, R.perm)
    scaled, factor = stats(cls_row)
    R.dcls[...] = dcls_second + norm_back(dcls_total(), gain_s[...], scaled, factor)
    low, datt, dmix = R.low_a, R.low_b, R.low_c
    low[:T_ROWS, :] = (df[:T_ROWS, :] * R.kt_col[...]).astype(BF16)
    sent(0, 1, 2, 3)

    def back_fc(n):
        cols = pl.ds(n, 256)
        datt[:T_ROWS, cols] = nt(low[:T_ROWS, :], rows_of(R.fc, n)).astype(BF16)
        R.fc[pl.ds(n // 64, 4)] = tn(att_t[:, cols], low[:T_ROWS, :]).astype(BF16).reshape(4, 64, width)

    tiles(width, 256, back_fc)
    service(12)

    def back_time(n):
        cols = pl.ds(n, 256)
        dmix[:T_ROWS, cols] = nt(datt[:T_ROWS, :], rows_of(R.pj_t, n)).astype(BF16)
        R.pj_t[pl.ds(n // 64, 4)] = tn(mix_t[:, cols], datt[:T_ROWS, :]).astype(BF16).reshape(4, 64, width)

    tiles(width, 256, back_time)
    service(13)
    for n in range(3):
        attention_back(qkv_t, p_t, dmix, dqkv, T_GROUPS, 2 * n, 2 * n + 2)
        service(14 + n)
    qkv_back(dqkv, R.wt_t, du, T_ROWS)
    service(17)
    qkv_grad(dqkv, u_t, R.wt_t, T_ROWS)
    service(18)
    R.dgain_t[...] = jnp.zeros((1, width), F32)

    def finish_time(r):
        rows = pl.ds(r, 80)
        scaled, factor = stats(patches[rows, :].astype(F32))
        grad = du[rows, :]
        R.dgain_t[...] += jnp.sum(grad * scaled, axis=0, keepdims=True)
        df[rows, :] += norm_back(grad, gain_t[...], scaled, factor)

    tiles(T_ROWS, 80, finish_time)
    store = pltpu.make_async_copy(df.at[pl.ds(0, used)], R.dx, R.lo.at[4])
    store.start()
    for n, gain in enumerate((R.dgain_t, R.dgain_s, R.dgain_m)):
        R.gains[0, n : n + 1, :] = gain[...]
    def gain_part(j):
        peer = ([peer_c, peer_y] + bits)[j]
        return remote(R.gains.at[0], R.gains.at[1 + j], (R.gg_s, R.gg_r), j, peer)

    def gain_steps():
        for j in range(2 + levels):
            gain_part(j).start()
            yield
            gain_part(j).wait()
            R.gains[0] = R.gains[0] + R.gains[1 + j]

    extra[16] = gain_steps()
    service(19)
    finish_units()
    R.gains_out[...] = R.gains[0]
    store.wait()
    store_out.wait()


def local(
    patches, cls_token, keep_mask, gain_time, qkv_time, proj_time, temporal_fc, gain_space, qkv_space, proj_space,
    gain_mlp, mlp_in, mlp_out, cotangent, cls_cotangent,
):
    _, frames, count, width = patches.shape
    heads_here, hd = qkv_time.shape[1], qkv_time.shape[3]

    def by_patch(x):
        return jnp.transpose(x[0], (1, 0, 2)).reshape(count * frames, width)

    def by_head(w):
        return jnp.transpose(w, (1, 2, 3, 0))

    def blocks(w):
        return w.reshape(-1, 64, width)

    zero = jnp.zeros((3, width), F32)
    rows_in = jnp.concatenate(
        [gain_time[None], gain_space[None], gain_mlp[None], cls_token.astype(F32), cls_cotangent.astype(F32), zero]
    )
    large = dict(
        patches=by_patch(patches), cot=by_patch(cotangent), keep=keep_mask[0], wt_t_in=by_head(qkv_time),
        pj_t_in=proj_time, fc_in=blocks(temporal_fc), wt_s_in=by_head(qkv_space), pj_s_in=proj_space,
        w1_in=blocks(mlp_in), w2_in=blocks(mlp_out),
    )
    small = dict(rows_in=rows_in)
    frame_rows, square, row = (frames, count, width), (width // 64, 64, width), (1, width)
    heads = (heads_here, 3, hd, width)
    t_rows, s_rows, ours = (T_ROWS, width), (S_ROWS, width), (count * frames, width)
    in_hbm = dict(
        out=(ours, BF16), dx=(ours, F32), dw1=(square, BF16), dw2=(square, BF16), dfc=(square, BF16),
        dwt_s=(heads, BF16), dpj_s=(proj_space.shape, BF16), dwt_t=(heads, BF16), dpj_t=(proj_time.shape, BF16),
    )
    in_vmem = dict(ocls=(row, BF16), dcls=(row, F32), gains_out=((8, width), F32))
    levels = lax.axis_size("clip").bit_length() - 1
    vmem = dict(
        wt_t=((3,) + square, BF16), pj_t=(square, BF16), fc=(square, BF16), wt_s=((3,) + square, BF16),
        pj_s=(square, BF16), w1=((4,) + square, BF16), w2=((4,) + square, BF16),
        patches_v=(t_rows, BF16), keep_v=(keep_mask.shape[1:], jnp.int32),
        kt_col=((T_ROWS, 1), F32), ks_row=((2, 1, 256), F32), ks_col=((S_ROWS, 1), F32), once=((S_ROWS, 1), F32),
        bias_t=((4, 112, 128), F32), u_t=(t_rows, BF16), qkv_t=((T_ROWS, 3 * width), BF16),
        p_t=((6, 4, 224, 128), F32), mix_t=(t_rows, BF16), att_t=(t_rows, BF16),
        rows_x=(s_rows, F32), rows_s=(s_rows, F32), rows_c=(s_rows, F32), rows_a=(s_rows, F32), rows_d=(s_rows, F32),
        low_a=(s_rows, BF16), low_b=(s_rows, BF16), low_c=(s_rows, BF16), low_d=(s_rows, BF16),
        u_s=(s_rows, BF16), qkv_s=((S_ROWS, 3 * width), BF16), mix_s=(s_rows, BF16),
        p_s=((6, 2, 416, 256), F32), dqkv=((S_ROWS, 3 * width), BF16),
        perm=((width // 128, T_ROWS, 128), F32), send_a=(frame_rows, BF16),
        send_b=(frame_rows, BF16), got_first=(frame_rows, BF16), got_cot=(frame_rows, BF16),
        cls_sum=((4, 8, width), F32), dcls_sum=((4, 8, width), F32),
        dgain_t=(row, F32), dgain_s=(row, F32), dgain_m=(row, F32), gains=((3 + levels, 8, width), F32),
        near_a=((6, 2, 3, 64, width), BF16), near_b=((3, 2, 4, 64, width), BF16),
        near_c=((3, 2, width // 64, 64, 256), BF16),
    )
    pairs = dict(wy=14, wx=42, wc=14, wf=14, ex=12, row=6, gu=240, gg=2 + levels)
    sems = dict(wo=14, exo=4, lo=6, go=15)
    for name, n in pairs.items():
        sems[name + "_s"] = n
        sems[name + "_r"] = n
    flags = dict(free=120)
    names = [*large, *small, *in_hbm, *in_vmem, *vmem, *sems, *flags]
    hbm, vm = pl.BlockSpec(memory_space=pl.ANY), pl.BlockSpec(memory_space=pltpu.VMEM)
    output, dx, d_w1, d_w2, d_fc, d_qs, d_ps, d_qt, d_pt, out_cls, cls_grad, gains = pl.pallas_call(
        partial(whole_step, names, frames),
        out_shape=[jax.ShapeDtypeStruct(s, d) for s, d in [*in_hbm.values(), *in_vmem.values()]],
        in_specs=[hbm] * len(large) + [vm] * len(small),
        out_specs=[hbm] * len(in_hbm) + [vm] * len(in_vmem),
        scratch_shapes=[pltpu.VMEM(s, d) for s, d in vmem.values()]
        + [pltpu.SemaphoreType.DMA((n,)) for n in sems.values()]
        + [pltpu.SemaphoreType.REGULAR((n,)) for n in flags.values()],
        compiler_params=pltpu.CompilerParams(collective_id=0, has_side_effects=True, vmem_limit_bytes=60 << 20),
    )(*large.values(), *small.values())

    def by_frame(x):
        return jnp.transpose(x.reshape(count, frames, width), (1, 0, 2))[None]

    def by_width(w):
        return jnp.transpose(w.astype(F32), (3, 0, 1, 2))

    def whole(w):
        return w.astype(F32).reshape(width, width)

    return (
        by_frame(output), out_cls, by_frame(dx), cls_grad, gains[0], by_width(d_qt), d_pt.astype(F32), whole(d_fc),
        gains[1], by_width(d_qs), d_ps.astype(F32), gains[2], whole(d_w1), whole(d_w2),
    )


def solution(mesh):
    rows, wide, by_head = P("clip", None, "head", None), P("clip", None), P(None, "head", None, None)
    in_specs = (
        rows, wide, P("clip", None, None), P(), by_head, P("head", None, None), P(), P(), by_head,
        P("head", None, None), P(), P(None, "head"), P("head", None), rows, wide,
    )
    out_specs = (
        rows, wide, rows, wide, P(), by_head, P("head", None, None), P(), P(), by_head,
        P("head", None, None), P(), P(None, "head"), P("head", None),
    )
    return jax.shard_map(local, mesh=mesh, in_specs=in_specs, out_specs=out_specs, check_vma=False)
```

time: 320 us -> 258 us (0.81)
  Pallas kernels: 284 us -> 239 us
  local copies, waits for them, and re-layouts: 19.3 us -> 7.91 us
  other arithmetic: 14.5 us -> 9.86 us
    pallas_call x1, Pallas kernels: 284 us -> 239 us  [local(): pl.pallas_call(partial(whole_step, names, frames), out_shape=[jax.ShapeDt...]
    convert_element_type x7 -> x2, other arithmetic: 8.41 us -> 1.72 us  [the longest x1 0.86 us: local(): d_pt.astype(F32)]
    reshape x0 -> x2, other arithmetic: none -> 5.95 us  [whole(): return w.astype(F32).reshape(width, width)]
    transpose x4 -> x0, local copies, waits for them, and re-layouts: 3.38 us -> none  [the longest x2 3.21 us: flat_t(): return jnp.transpose(w, (2, 1, 3, 0)).reshape(3, part, width)]
where the time goes in v3:
time: 258 us
  Pallas kernels  239 us (93%)
  other arithmetic  9.86 us (4%)
  local copies, waits for them, and re-layouts  7.91 us (3%)
    pallas_call x1, Pallas kernels, local(): pl.pallas_call(partial(whole_step, names, frames), out_shape=[jax.ShapeDt...  239 us
    reshape x2, other arithmetic, whole(): return w.astype(F32).reshape(width, width)  5.95 us

profile of v3, /device:TPU:0, one launch (start us, length us, event | category | flops | bytes accessed | tf_op | source)
XLA Modules:
  0.0 257.6 jit_solution(5896450277616897966)
XLA Ops:
  0.6 0.7 broadcast_in_dim.18
  1.3 0.7 broadcast_in_dim.19
  2.0 0.7 broadcast_in_dim.20
  2.7 1.3 concatenate.3.refs_10_
  4.1 239.1 %shard_map.254 = (bf16[392,768]{1,0:T(8,128)(2,1)}, f32[392,768]{1,0:T(8,128)}, bf16[12,64,768]{2,1,0:T(8,128)(2,1)}, bf16[12,64,768]{2,1,0:T(8,128)(2,1)}, bf16...) custom-call(bf16[392,768]{1,0:T(8,128)(2,1)} %bitcast.46, ...), custom_call_target="tpu_custom_call" | custom-call | tf_op jit(solution)/shard_map/pallas_call | solution.py:925
  243.2 0.0 copy-start.2
  243.2 0.0 copy-start.3
  243.2 4.3 %bitcast_convert_fusion = (f32[768,768]{1,0:T(8,128)}, f32[768,768]{1,0:T(8,128)}) fusion(bf16[12,64,768]{2,1,0:T(8,128)(2,1)} %get-tuple-element.37, bf16[12,64,768]{2,1,0:T(8,128)(2,1)} %get-tuple-element.36), kind=kLoop, calls=%fused_computation.2 | loop fusion | flops 1179648 | bytes 7077888 | tf_op jit(solution)/shard_map/reshape | solution.py:943
  247.5 0.0 copy-done.2
  247.5 0.0 copy-done.3
  247.5 2.2 convert_bitcast_fusion
  249.7 1.5 slice_reduce_fusion
  251.2 0.0 copy-done.1
  251.2 1.7 bitcast_convert_fusion.2
  252.8 0.0 copy-done.6
  252.8 0.9 convert_element_type.19
  253.7 0.0 copy-done.5
  253.7 0.9 convert_element_type.20
  254.5 0.0 copy-done.4
  254.5 0.8 copy.33
  255.4 0.0 copy-done.8
  255.4 0.6 copy.34
  256.0 1.0 copy.35
  257.0 0.6 copy.36
  (10 shorter events, 0.0 us)
Async XLA Ops:
  243.2 4.3 %copy-start.2 = (bf16[3,3,64,768]{3,2,1,0:T(8,128)(2,1)S(1)}, bf16[3,3,64,768]{3,2,1,0:T(8,128)(2,1)}, u32[]{:S(2)}) copy-start(bf16[3,3,64,768]{3,2,1,0:T(8,128)(2,1)} %get-tuple-element.34) | copy-start | bytes 2654212
  243.2 4.3 %copy-start.3 = (bf16[3,3,64,768]{3,2,1,0:T(8,128)(2,1)S(1)}, bf16[3,3,64,768]{3,2,1,0:T(8,128)(2,1)}, u32[]{:S(2)}) copy-start(bf16[3,3,64,768]{3,2,1,0:T(8,128)(2,1)} %get-tuple-element.31) | copy-start | bytes 2654212
  247.5 3.7 %copy-start.1 = (bf16[12,64,768]{2,1,0:T(8,128)(2,1)S(1)}, bf16[12,64,768]{2,1,0:T(8,128)(2,1)}, u32[]{:S(2)}) copy-start(bf16[12,64,768]{2,1,0:T(8,128)(2,1)} %get-tuple-element.33) | copy-start | bytes 3538948
  251.2 1.7 copy-start.6
  251.2 2.5 copy-start.5
  252.8 1.7 copy-start.4
  253.7 1.7 copy-start.8
  253.7 2.3 copy-start
  256.0 1.0 copy-start.7

commit v4 on v3

--- a/solution.py
+++ b/solution.py
@@ -132,11 +132,13 @@
         qc = pl.ds(pl.multiple_of(hp * 128, 128), 128)
         kc = pl.ds(pl.multiple_of(width + hp * 128, 128), 128)
         vc = pl.ds(pl.multiple_of(2 * width + hp * 128, 128), 128)
-        for g, (start, size) in enumerate(groups):
-            rows = pl.ds(start, size)
-            prob = softmax(nt(stacked(qkv_ref[rows, qc]), qkv_ref[rows, kc]) + bias_of(g, size))
-            p_ref[hp, g, : 2 * size, :size] = prob
-            mix_ref[rows, qc] = unstacked(nn(prob.astype(BF16), qkv_ref[rows, vc])).astype(BF16)
+        all_rows = [pl.ds(start, size) for start, size in groups]
+        scores = [nt(stacked(qkv_ref[rows, qc]), qkv_ref[rows, kc]) for rows in all_rows]
+        probs = [softmax(scores[g] + bias_of(g, size)).astype(BF16) for g, (_, size) in enumerate(groups)]
+        mixes = [unstacked(nn(prob, qkv_ref[rows, vc])).astype(BF16) for prob, rows in zip(probs, all_rows)]
+        for g, (_, size) in enumerate(groups):
+            p_ref[hp, g, : 2 * size, :size] = probs[g]
+            mix_ref[all_rows[g], qc] = mixes[g]
         return carry
 
     lax.fori_loop(first, last, body, 0)
@@ -149,16 +151,22 @@
         qc = pl.ds(pl.multiple_of(hp * 128, 128), 128)
         kc = pl.ds(pl.multiple_of(width + hp * 128, 128), 128)
         vc = pl.ds(pl.multiple_of(2 * width + hp * 128, 128), 128)
-        for g, (start, size) in enumerate(groups):
-            rows = pl.ds(start, size)
-            up = stacked(dmix_ref[rows, qc])
-            prob = p_ref[hp, g, : 2 * size, :size]
-            dprob = nt(up, qkv_ref[rows, vc])
-            delta = jnp.sum(prob * dprob, axis=-1, keepdims=True)
-            dscore = (prob * (dprob - delta)).astype(BF16)
-            dqkv_ref[rows, qc] = (unstacked(nn(dscore, qkv_ref[rows, kc])) * 0.125).astype(BF16)
-            dqkv_ref[rows, kc] = tn(dscore, stacked(qkv_ref[rows, qc])).astype(BF16)
-            dqkv_ref[rows, vc] = tn(prob.astype(BF16), up).astype(BF16)
+        all_rows = [pl.ds(start, size) for start, size in groups]
+        ups = [stacked(dmix_ref[rows, qc]) for rows in all_rows]
+        probs = [p_ref[hp, g, : 2 * size, :size] for g, (_, size) in enumerate(groups)]
+        dprobs = [nt(up, qkv_ref[rows, vc]) for up, rows in zip(ups, all_rows)]
+        dvs = [tn(prob, up).astype(BF16) for prob, up in zip(probs, ups)]
+        dscores = []
+        for prob, dprob in zip(probs, dprobs):
+            wide = prob.astype(F32)
+            delta = jnp.sum(wide * dprob, axis=-1, keepdims=True)
+            dscores.append((wide * (dprob - delta)).astype(BF16))
+        dqs = [(unstacked(nn(ds, qkv_ref[rows, kc])) * 0.125).astype(BF16) for ds, rows in zip(dscores, all_rows)]
+        dks = [tn(ds, stacked(qkv_ref[rows, qc])).astype(BF16) for ds, rows in zip(dscores, all_rows)]
+        for g, rows in enumerate(all_rows):
+            dqkv_ref[rows, qc] = dqs[g]
+            dqkv_ref[rows, kc] = dks[g]
+            dqkv_ref[rows, vc] = dvs[g]
         return carry
 
     lax.fori_loop(first, last, body, 0)
@@ -262,31 +270,35 @@
 
 MESH = pl.DeviceIdType.MESH
 
-ROUTES = (0, 2, 0, 1, 0, 0, 1, 2, 0, 0, 0, 0, 0, 0, 0)
+ROUTES = (0, 2, 0, 2, 1, 0, 0, 1, 0, 0, 0, 1, 0, 0, 0)
 ORDER = (
     (0, 1),
     (2, 3, 0, 1),
     (4, 5, 2, 3),
-    (0, 1, 4),
+    (4, 5, 0, 1),
     (),
     (),
     (),
     (2, 3),
-    (0, 1),
-    (4, 2),
-    (0, 5),
-    (6, 8, 9, 7, 0, 1, 2, 3, 4),
-    (10, 6, 8, 15),
-    (11, 0, 1, 9, 7, 10),
-    (2, 3, 4, 5, 11),
-    (1, 6),
-    (0,),
-    (2, 5, 8, 7),
-    (12, 13, 14, 3),
-    (12, 13, 14, 9, 16, 8, 4, 1, 2, 10, 5, 9, 16, 3, 11, 15, 7, 10, 8, 4, 6, 16, 3, 9, 5, 10, 11, 12, 6, 16,
-     8, 4, 9, 5, 13, 12, 11, 16, 10, 8, 6, 5, 14, 9, 7, 16, 12, 13, 10, 11, 8, 6, 14, 16, 12, 13, 11, 9, 14,
-     7, 12, 16, 10, 13, 6, 14, 11, 7, 13, 16, 10, 14, 12, 10, 7, 13, 14, 16),
+    (),
+    (4, 0, 1),
+    (5, 2, 3, 0),
+    (6, 7, 8, 9),
+    (10, 6, 7, 4, 8, 5, 9, 2, 10, 1, 0, 15),
+    (11, 4, 3),
+    (11, 5),
+    (7, 1, 2, 0),
+    (3, 4),
+    (12, 13, 14, 6, 5),
+    (12, 13, 14, 11, 1, 2, 3, 0),
+    (8, 6, 4, 5, 16, 9, 2, 1, 8, 3, 6, 10, 16, 4, 8, 15, 7, 6, 8, 5, 7, 16, 6, 9, 12, 8, 7, 10, 9, 16, 7, 6,
+     13, 10, 12, 9, 10, 16, 8, 12, 14, 9, 7, 10, 11, 16, 12, 13, 11, 12, 14, 13, 11, 16, 9, 14, 13, 10, 11,
+     14, 12, 16, 13, 14, 11, 10, 13, 10, 14, 16),
 )
+
+
+def arrivals(route, levels, everywhere):
+    return 2 + (3, 4, 5)[route] + levels - 2 + 2 + (3 if everywhere else 0)
 
 
 def whole_step(names, frames, *refs):
@@ -420,7 +432,7 @@
             return lambda s, q=0, k=4: part(R.w2.at[s, pl.ds(n * 4, 4)], q, k)
         if i == 10:
             return lambda s, q=0, k=4: part(R.fc.at[pl.ds((head ^ s) * 3, 3)], q, k)
-        wt, pj = (R.wt_s, R.pj_s) if i < 10 else (R.wt_t, R.pj_t)
+        wt, pj = (R.wt_s, R.pj_s) if i < 10 else (R.dwt_own, R.pj_t)
         n = i - 6 if i < 10 else i - 11
         if n == 0:
             return lambda s, q=0, k=4: part(pj.at[pl.ds(s * 3, 3)], q, k)
@@ -457,11 +469,14 @@
         a, b = (1, 2) if route == 2 else (0, 1)
         half = 2 * digit[a]
         quarter = half + digit[b]
-        counts = [0, 0]
+        counts = [sum(arrivals(ROUTES[k], levels, k == 10) for k in range(i)), 0]
 
         def copy(src, dst, peer):
             counts[0] += 1
-            return remote(src, dst, (R.gu_s, R.gu_r), i * 16 + counts[0] - 1, peer)
+            return pltpu.make_async_remote_copy(
+                src_ref=src, dst_ref=dst, send_sem=R.gu_s.at[i * 2 + counts[0] % 2], recv_sem=R.gu_r.at[counts[0] - 1],
+                device_id=peer, device_id_type=MESH,
+            )
 
         def land(k):
             at_q = counts[1]
@@ -511,7 +526,7 @@
     def tell(i, first, last):
         peers = units[i][1]
         for k in range(first, min(last, len(peers))):
-            pl.semaphore_signal(R.free.at[i * 8 + k], inc=1, device_id=peers[k], device_id_type=MESH)
+            pl.semaphore_signal(R.free.at[i * (levels + 1) + k], inc=1, device_id=peers[k], device_id_type=MESH)
 
     def land_step(i):
         steps, _ = units[i]
@@ -536,7 +551,7 @@
         if stage[i] < len(steps):
             copies, _, credit = steps[stage[i]]
             if credit is not None:
-                pl.semaphore_wait(R.free.at[i * 8 + credit], 1)
+                pl.semaphore_wait(R.free.at[i * (levels + 1) + credit], 1)
             all_start(copies)
         stage[i] += 1
 
@@ -575,7 +590,7 @@
     loads = [pltpu.make_async_copy(src, dst, R.lo.at[i]) for i, (src, dst) in enumerate(loads)]
     for i in range(3):
         loads[i].start()
-    for i in range(14):
+    for i in range(12):
         y_copy(i).start()
     for i in range(14):
         own_copy(i).start()
@@ -617,7 +632,6 @@
     loads[2].wait()
     to_frame_order(R.low_d, R.send_b, R.perm)
     ex_cot = exchange(1, R.send_b, R.got_cot)
-    all_start(ex_cot)
     pass_near(1, 2, 3)
 
     def time_bias_of(g, size):
@@ -628,12 +642,14 @@
     project_qkv(u_t, R.wt_t, qkv_t, T_ROWS, 0, 6)
     attention(qkv_t, p_t, mix_t, T_GROUPS, time_bias_of, 0, 3)
     pass_near(4, 5, 6, 7)
-    pass_far(0, 1, 2, 3)
-    ready_far(0, 1, 2, 3)
+    pass_far(0, 1, 2)
+    ready_far(0, 1, 2)
+    pass_far(3)
     pass_near(8, 9)
     project_qkv(u_t, R.wt_t, qkv_t, T_ROWS, 6, 12)
     attention(qkv_t, p_t, mix_t, T_GROUPS, time_bias_of, 3, 6)
-    pass_near(10, 11, 12, 13)
+    pass_near(10, 11)
+    ready_far(3)
     loads[3].wait()
 
     def project(n):
@@ -650,6 +666,9 @@
     to_frame_order(first, R.send_a, R.perm)
     ex_first = exchange(0, R.send_a, R.got_first)
     all_start(ex_first)
+    for i in (12, 13):
+        y_copy(i).start()
+    all_start(ex_cot)
     pass_far(4, 5, 6, 7)
 
     qkv_s, p_s, mix_s, u_s = R.qkv_s, R.p_s, R.mix_s, R.u_s
@@ -661,6 +680,7 @@
     ready_near(4, 5, 6, 7)
     ready_far(4, 5, 6, 7)
     project_qkv(u_s, R.wt_s, qkv_s, S_ROWS, 0, 12)
+    pass_near(12, 13)
     all_wait(ex_cot)
     gather_frames(R.got_cot, (gains[4:5, :], jnp.zeros((1, width), F32)), cot)
     cls_part = cls_attention(qkv_s, R.ks_row, at, width)
@@ -762,7 +782,6 @@
     def back_space(n):
         cols = pl.ds(n, 256)
         dmix[:, cols] = nt(low[...], rows_of(R.pj_s, n)).astype(BF16)
-        R.pj_s[pl.ds(n // 64, 4)] = tn(mix_s[:, cols], loww[...]).astype(BF16).reshape(4, 64, width)
 
     tiles(width, 256, back_space)
     service(4)
@@ -774,8 +793,6 @@
         service(5 + n)
     qkv_back(dqkv, R.wt_s, du, S_ROWS)
     service(8)
-    qkv_grad(dqkv, u_s, R.wt_s, S_ROWS)
-    service(9)
     R.dcls_sum[0] = jnp.broadcast_to(du[at : at + 1, :] + du[SEG + at : SEG + at + 1, :], (8, width))
     R.dgain_s[...] = jnp.zeros((1, width), F32)
     dfirst = R.rows_a
@@ -794,6 +811,14 @@
     ex_df = exchange(3, R.send_a, R.got_first)
     all_start(ex_df)
     dcls_total = sum_rows(1, R.dcls_sum, False)
+    service(9)
+
+    def grad_space(n):
+        cols = pl.ds(n, 256)
+        R.pj_s[pl.ds(n // 64, 4)] = tn(mix_s[:, cols], loww[...]).astype(BF16).reshape(4, 64, width)
+
+    tiles(width, 256, grad_space)
+    qkv_grad(dqkv, u_s, R.wt_s, S_ROWS)
     service(10)
 
     df = R.rows_s
@@ -824,9 +849,9 @@
     for n in range(3):
         attention_back(qkv_t, p_t, dmix, dqkv, T_GROUPS, 2 * n, 2 * n + 2)
         service(14 + n)
+    qkv_grad(dqkv, u_t, R.dwt_own, T_ROWS)
+    service(17)
     qkv_back(dqkv, R.wt_t, du, T_ROWS)
-    service(17)
-    qkv_grad(dqkv, u_t, R.wt_t, T_ROWS)
     service(18)
     R.dgain_t[...] = jnp.zeros((1, width), F32)
 
@@ -859,6 +884,29 @@
     R.gains_out[...] = R.gains[0]
     store.wait()
     store_out.wait()
+
+
+def widen(*refs):
+    half = len(refs) // 2
+    for src, dst in zip(refs[:half], refs[half:]):
+        dst[...] = src[...].astype(dst.dtype)
+
+
+def widened(arrays):
+    steps = 4
+    specs = []
+    for x, _ in arrays:
+        rows = x.shape[0] // steps if x.shape[0] % (8 * steps) == 0 else x.shape[0]
+        last = x.shape[0] // rows - 1
+        specs.append(pl.BlockSpec((rows, x.shape[1]), lambda i, last=last: (jnp.minimum(i, last), 0)))
+    return pl.pallas_call(
+        widen,
+        grid=(steps,),
+        out_shape=[jax.ShapeDtypeStruct(x.shape, d) for x, d in arrays],
+        in_specs=specs,
+        out_specs=specs,
+        compiler_params=pltpu.CompilerParams(vmem_limit_bytes=60 << 20),
+    )(*[x for x, _ in arrays])
 
 
 def local(
@@ -902,11 +950,11 @@
         patches_v=(t_rows, BF16), keep_v=(keep_mask.shape[1:], jnp.int32),
         kt_col=((T_ROWS, 1), F32), ks_row=((2, 1, 256), F32), ks_col=((S_ROWS, 1), F32), once=((S_ROWS, 1), F32),
         bias_t=((4, 112, 128), F32), u_t=(t_rows, BF16), qkv_t=((T_ROWS, 3 * width), BF16),
-        p_t=((6, 4, 224, 128), F32), mix_t=(t_rows, BF16), att_t=(t_rows, BF16),
+        p_t=((6, 4, 224, 128), BF16), mix_t=(t_rows, BF16), att_t=(t_rows, BF16),
         rows_x=(s_rows, F32), rows_s=(s_rows, F32), rows_c=(s_rows, F32), rows_a=(s_rows, F32), rows_d=(s_rows, F32),
         low_a=(s_rows, BF16), low_b=(s_rows, BF16), low_c=(s_rows, BF16), low_d=(s_rows, BF16),
         u_s=(s_rows, BF16), qkv_s=((S_ROWS, 3 * width), BF16), mix_s=(s_rows, BF16),
-        p_s=((6, 2, 416, 256), F32), dqkv=((S_ROWS, 3 * width), BF16),
+        p_s=((6, 2, 416, 256), BF16), dwt_own=((3,) + square, BF16), dqkv=((S_ROWS, 3 * width), BF16),
         perm=((width // 128, T_ROWS, 128), F32), send_a=(frame_rows, BF16),
         send_b=(frame_rows, BF16), got_first=(frame_rows, BF16), got_cot=(frame_rows, BF16),
         cls_sum=((4, 8, width), F32), dcls_sum=((4, 8, width), F32),
@@ -914,12 +962,14 @@
         near_a=((6, 2, 3, 64, width), BF16), near_b=((3, 2, 4, 64, width), BF16),
         near_c=((3, 2, width // 64, 64, 256), BF16),
     )
-    pairs = dict(wy=14, wx=42, wc=14, wf=14, ex=12, row=6, gu=240, gg=2 + levels)
+    pairs = dict(wy=14, wx=42, wc=14, wf=14, ex=12, row=6, gg=2 + levels)
     sems = dict(wo=14, exo=4, lo=6, go=15)
     for name, n in pairs.items():
         sems[name + "_s"] = n
         sems[name + "_r"] = n
-    flags = dict(free=120)
+    sems["gu_s"] = 30
+    sems["gu_r"] = sum(arrivals(ROUTES[k], levels, k == 10) for k in range(15))
+    flags = dict(free=15 * (levels + 1))
     names = [*large, *small, *in_hbm, *in_vmem, *vmem, *sems, *flags]
     hbm, vm = pl.BlockSpec(memory_space=pl.ANY), pl.BlockSpec(memory_space=pltpu.VMEM)
     output, dx, d_w1, d_w2, d_fc, d_qs, d_ps, d_qt, d_pt, out_cls, cls_grad, gains = pl.pallas_call(
@@ -937,14 +987,13 @@
         return jnp.transpose(x.reshape(count, frames, width), (1, 0, 2))[None]
 
     def by_width(w):
-        return jnp.transpose(w.astype(F32), (3, 0, 1, 2))
-
-    def whole(w):
-        return w.astype(F32).reshape(width, width)
-
+        return jnp.transpose(w.reshape(heads), (3, 0, 1, 2))
+
+    grads = [(x.reshape(-1, width), F32) for x in (dx, d_w1, d_w2, d_fc, d_qs, d_ps, d_qt, d_pt)]
+    output, dx, d_w1, d_w2, d_fc, d_qs, d_ps, d_qt, d_pt = widened([(output, BF16)] + grads)
     return (
-        by_frame(output), out_cls, by_frame(dx), cls_grad, gains[0], by_width(d_qt), d_pt.astype(F32), whole(d_fc),
-        gains[1], by_width(d_qs), d_ps.astype(F32), gains[2], whole(d_w1), whole(d_w2),
+        by_frame(output), out_cls, by_frame(dx), cls_grad, gains[0], by_width(d_qt), d_pt.reshape(proj_time.shape), d_fc,
+        gains[1], by_width(d_qs), d_ps.reshape(proj_space.shape), gains[2], d_w1, d_w2,
     )
 
 

time: 258 us -> 242 us (0.938)
  other arithmetic: 9.86 us -> 0 us
  Pallas kernels: 239 us -> 235 us
    pallas_call x1, Pallas kernels: 239 us -> 227 us  [local(): pl.pallas_call(partial(whole_step, names, frames), out_shape=[jax.ShapeDt...]
    pallas_call x0 -> x1, Pallas kernels: none -> 8.59 us  [widened(): pl.pallas_call(widen, grid=(steps,), out_shape=[jax.ShapeDtypeStruct(x.sh...]
    reshape x2 -> x0, other arithmetic: 5.95 us -> none  [whole(): return w.astype(F32).reshape(width, width)]
where the time goes in v4:
time: 242 us
  Pallas kernels  235 us (97%)
  local copies, waits for them, and re-layouts  6.05 us (2%)
    pallas_call x1, Pallas kernels, local(): pl.pallas_call(partial(whole_step, names, frames), out_shape=[jax.ShapeDt...  227 us
    pallas_call x1, Pallas kernels, widened(): pl.pallas_call(widen, grid=(steps,), out_shape=[jax.ShapeDtypeStruct(x.sh...  8.59 us

profile of v4, /device:TPU:0, one launch (start us, length us, event | category | flops | bytes accessed | tf_op | source)
XLA Modules:
  0.0 242.0 jit_solution(13135725889158328908)
XLA Ops:
  0.6 0.7 broadcast_in_dim.18
  1.3 0.7 broadcast_in_dim.19
  2.0 0.7 broadcast_in_dim.20
  2.7 1.3 concatenate.3.refs_10_
  4.1 226.7 %shard_map.254 = (bf16[392,768]{1,0:T(8,128)(2,1)}, f32[392,768]{1,0:T(8,128)}, bf16[12,64,768]{2,1,0:T(8,128)(2,1)}, bf16[12,64,768]{2,1,0:T(8,128)(2,1)}, bf16...) custom-call(bf16[392,768]{1,0:T(8,128)(2,1)} %bitcast.51, ...), custom_call_target="tpu_custom_call" | custom-call | tf_op jit(solution)/shard_map/pallas_call | solution.py:975
  230.7 1.5 slice_reduce_fusion
  232.2 0.0 copy-start.1
  232.2 0.0 copy-start
  232.2 8.6 %shard_map.255 = (bf16[392,768]{1,0:T(8,128)(2,1)}, f32[392,768]{1,0:T(8,128)}, f32[768,768]{1,0:T(8,128)}, f32[768,768]{1,0:T(8,128)}, f32[768,768]{1,0:T(8,128...) custom-call(bf16[392,768]{1,0:T(8,128)(2,1)} %get-tuple-element.35.refs_0_, ...), custom_call_target="tpu_custom_call" | custom-call | tf_op jit(solution)/shard_map/pallas_call | solution.py:902
  240.8 0.0 copy-done.1
  240.8 0.6 copy.31
  241.4 0.0 copy-done
  241.4 0.6 copy.32
  (1 shorter events, 0.0 us)
Async XLA Ops:
  232.2 8.6 %copy-start.1 = (bf16[1,768]{1,0:T(2,128)(2,1)S(1)}, bf16[1,768]{1,0:T(2,128)(2,1)}, u32[]{:S(2)}) copy-start(bf16[1,768]{1,0:T(2,128)(2,1)} %get-tuple-element.74) | copy-start | bytes 4612
  232.2 9.2 %copy-start = (f32[1,768]{1,0:T(1,128)S(1)}, f32[1,768]{1,0:T(1,128)}, u32[]{:S(2)}) copy-start(f32[1,768]{1,0:T(1,128)} %get-tuple-element.76) | copy-start | bytes 9220

commit v5 on v4

--- a/solution.py
+++ b/solution.py
@@ -270,30 +270,29 @@
 
 MESH = pl.DeviceIdType.MESH
 
-ROUTES = (0, 2, 0, 2, 1, 0, 0, 1, 0, 0, 0, 1, 0, 0, 0)
+ROUTES = (0, 0, 1, 0, 2, 1, 1, 0, 0, 1, 0, 0, 0, 0, 0)
 ORDER = (
     (0, 1),
     (2, 3, 0, 1),
     (4, 5, 2, 3),
-    (4, 5, 0, 1),
+    (0, 4, 5),
     (),
     (),
+    (1,),
     (),
+    (0, 4),
     (2, 3),
-    (),
-    (4, 0, 1),
-    (5, 2, 3, 0),
-    (6, 7, 8, 9),
-    (10, 6, 7, 4, 8, 5, 9, 2, 10, 1, 0, 15),
-    (11, 4, 3),
-    (11, 5),
-    (7, 1, 2, 0),
-    (3, 4),
-    (12, 13, 14, 6, 5),
-    (12, 13, 14, 11, 1, 2, 3, 0),
-    (8, 6, 4, 5, 16, 9, 2, 1, 8, 3, 6, 10, 16, 4, 8, 15, 7, 6, 8, 5, 7, 16, 6, 9, 12, 8, 7, 10, 9, 16, 7, 6,
-     13, 10, 12, 9, 10, 16, 8, 12, 14, 9, 7, 10, 11, 16, 12, 13, 11, 12, 14, 13, 11, 16, 9, 14, 13, 10, 11,
-     14, 12, 16, 13, 14, 11, 10, 13, 10, 14, 16),
+    (0, 5),
+    (6, 7, 8, 9, 1, 4),
+    (10, 0, 3, 2, 6, 7, 1, 8, 9, 5, 10, 0, 4, 15),
+    (11, 3),
+    (2, 6, 1, 5, 11),
+    (3, 9, 7),
+    (0, 1, 2),
+    (12, 13, 14, 3, 4, 5, 7, 8, 2),
+    (1, 6, 4, 3, 12, 5, 13, 7, 8, 14, 10, 6, 11),
+    (9, 8, 7, 2, 16, 6, 10, 12, 4, 9, 5, 11, 16, 8, 7, 15, 13, 6, 12, 10, 9, 16, 7, 11, 14, 8, 13, 12, 10, 16,
+     6, 9, 11, 14, 13, 12, 8, 16, 10, 11, 9, 14, 13, 10, 12, 16, 14, 11, 13, 12, 14, 10, 13, 16, 10, 14),
 )
 
 
@@ -600,6 +599,10 @@
     rows_x, first = R.rows_x, R.rows_s
     qkv_t, p_t, mix_t, att_t, u_t = R.qkv_t, R.p_t, R.mix_t, R.att_t, R.u_t
     patches, gains = R.patches_v, R.rows_in
+    for n, row in enumerate((R.gain_t, R.gain_s, R.gain_m)):
+        gains[n : n + 1, :] = row[...].reshape(1, width)
+    gains[3:4, :] = R.cls[...].astype(F32)
+    gains[4:5, :] = R.ccot[...].astype(F32)
     gain_t, gain_s, gain_m = gains.at[0:1], gains.at[1:2], gains.at[2:3]
     used = frames * count
     loads[0].wait()
@@ -925,16 +928,12 @@
     def blocks(w):
         return w.reshape(-1, 64, width)
 
-    zero = jnp.zeros((3, width), F32)
-    rows_in = jnp.concatenate(
-        [gain_time[None], gain_space[None], gain_mlp[None], cls_token.astype(F32), cls_cotangent.astype(F32), zero]
-    )
     large = dict(
         patches=by_patch(patches), cot=by_patch(cotangent), keep=keep_mask[0], wt_t_in=by_head(qkv_time),
         pj_t_in=proj_time, fc_in=blocks(temporal_fc), wt_s_in=by_head(qkv_space), pj_s_in=proj_space,
         w1_in=blocks(mlp_in), w2_in=blocks(mlp_out),
     )
-    small = dict(rows_in=rows_in)
+    small = dict(gain_t=gain_time, gain_s=gain_space, gain_m=gain_mlp, cls=cls_token, ccot=cls_cotangent)
     frame_rows, square, row = (frames, count, width), (width // 64, 64, width), (1, width)
     heads = (heads_here, 3, hd, width)
     t_rows, s_rows, ours = (T_ROWS, width), (S_ROWS, width), (count * frames, width)
@@ -947,7 +946,7 @@
     vmem = dict(
         wt_t=((3,) + square, BF16), pj_t=(square, BF16), fc=(square, BF16), wt_s=((3,) + square, BF16),
         pj_s=(square, BF16), w1=((4,) + square, BF16), w2=((4,) + square, BF16),
-        patches_v=(t_rows, BF16), keep_v=(keep_mask.shape[1:], jnp.int32),
+        rows_in=((8, width), F32), patches_v=(t_rows, BF16), keep_v=(keep_mask.shape[1:], jnp.int32),
         kt_col=((T_ROWS, 1), F32), ks_row=((2, 1, 256), F32), ks_col=((S_ROWS, 1), F32), once=((S_ROWS, 1), F32),
         bias_t=((4, 112, 128), F32), u_t=(t_rows, BF16), qkv_t=((T_ROWS, 3 * width), BF16),
         p_t=((6, 4, 224, 128), BF16), mix_t=(t_rows, BF16), att_t=(t_rows, BF16),

time: 242 us -> 226 us (0.934)
  Pallas kernels: 235 us -> 222 us
  local copies, waits for them, and re-layouts: 6.05 us -> 2.64 us
    pallas_call x1, Pallas kernels: 227 us -> 213 us  [local(): pl.pallas_call(partial(whole_step, names, frames), out_shape=[jax.ShapeDt...]
where the time goes in v5:
time: 226 us; the launch traced here: 225 us
  Pallas kernels  222 us (98%)
  local copies, waits for them, and re-layouts  2.64 us (1%)
    pallas_call x1, Pallas kernels, local(): pl.pallas_call(partial(whole_step, names, frames), out_shape=[jax.ShapeDt...  213 us
    pallas_call x1, Pallas kernels, widened(): pl.pallas_call(widen, grid=(steps,), out_shape=[jax.ShapeDtypeStruct(x.sh...  8.59 us

profile of v5, /device:TPU:0, one launch (start us, length us, event | category | flops | bytes accessed | tf_op | source)
XLA Modules:
  0.0 225.2 jit_solution(16246270949519250550)
XLA Ops:
  0.7 213.3 %shard_map.254 = (bf16[392,768]{1,0:T(8,128)(2,1)}, f32[392,768]{1,0:T(8,128)}, bf16[12,64,768]{2,1,0:T(8,128)(2,1)}, bf16[12,64,768]{2,1,0:T(8,128)(2,1)}, bf16...) custom-call(bf16[392,768]{1,0:T(8,128)(2,1)} %bitcast.51, ...), custom_call_target="tpu_custom_call" | custom-call | tf_op jit(solution)/shard_map/pallas_call | solution.py:974
  214.0 1.5 slice_reduce_fusion
  215.4 0.0 copy-start.1
  215.4 0.0 copy-start
  215.4 8.6 %shard_map.255 = (bf16[392,768]{1,0:T(8,128)(2,1)}, f32[392,768]{1,0:T(8,128)}, f32[768,768]{1,0:T(8,128)}, f32[768,768]{1,0:T(8,128)}, f32[768,768]{1,0:T(8,128...) custom-call(bf16[392,768]{1,0:T(8,128)(2,1)} %get-tuple-element.35.refs_0_, ...), custom_call_target="tpu_custom_call" | custom-call | tf_op jit(solution)/shard_map/pallas_call | solution.py:905
  224.0 0.0 copy-done.1
  224.0 0.6 copy.31
  224.6 0.0 copy-done
  224.6 0.6 copy.32
Async XLA Ops:
  215.4 8.6 %copy-start.1 = (bf16[1,768]{1,0:T(2,128)(2,1)S(1)}, bf16[1,768]{1,0:T(2,128)(2,1)}, u32[]{:S(2)}) copy-start(bf16[1,768]{1,0:T(2,128)(2,1)} %get-tuple-element.74) | copy-start | bytes 4612
  215.4 9.2 %copy-start = (f32[1,768]{1,0:T(1,128)S(1)}, f32[1,768]{1,0:T(1,128)}, u32[]{:S(2)}) copy-start(f32[1,768]{1,0:T(1,128)} %get-tuple-element.76) | copy-start | bytes 9220

commit v6 on v5

--- a/solution.py
+++ b/solution.py
@@ -884,7 +884,8 @@
     extra[16] = gain_steps()
     service(19)
     finish_units()
-    R.gains_out[...] = R.gains[0]
+    for n, ref in enumerate((R.g_t, R.g_s, R.g_m)):
+        ref[...] = R.gains[0, n : n + 1, :].reshape(width)
     store.wait()
     store_out.wait()
 
@@ -899,6 +900,9 @@
     steps = 4
     specs = []
     for x, _ in arrays:
+        if x.ndim == 1 or x.shape[0] == 1:
+            specs.append(pl.BlockSpec(x.shape, lambda i, n=x.ndim: (0,) * n))
+            continue
         rows = x.shape[0] // steps if x.shape[0] % (8 * steps) == 0 else x.shape[0]
         last = x.shape[0] // rows - 1
         specs.append(pl.BlockSpec((rows, x.shape[1]), lambda i, last=last: (jnp.minimum(i, last), 0)))
@@ -941,7 +945,7 @@
         out=(ours, BF16), dx=(ours, F32), dw1=(square, BF16), dw2=(square, BF16), dfc=(square, BF16),
         dwt_s=(heads, BF16), dpj_s=(proj_space.shape, BF16), dwt_t=(heads, BF16), dpj_t=(proj_time.shape, BF16),
     )
-    in_vmem = dict(ocls=(row, BF16), dcls=(row, F32), gains_out=((8, width), F32))
+    in_vmem = dict(ocls=(row, BF16), dcls=(row, F32), g_t=((width,), F32), g_s=((width,), F32), g_m=((width,), F32))
     levels = lax.axis_size("clip").bit_length() - 1
     vmem = dict(
         wt_t=((3,) + square, BF16), pj_t=(square, BF16), fc=(square, BF16), wt_s=((3,) + square, BF16),
@@ -971,7 +975,7 @@
     flags = dict(free=15 * (levels + 1))
     names = [*large, *small, *in_hbm, *in_vmem, *vmem, *sems, *flags]
     hbm, vm = pl.BlockSpec(memory_space=pl.ANY), pl.BlockSpec(memory_space=pltpu.VMEM)
-    output, dx, d_w1, d_w2, d_fc, d_qs, d_ps, d_qt, d_pt, out_cls, cls_grad, gains = pl.pallas_call(
+    output, dx, d_w1, d_w2, d_fc, d_qs, d_ps, d_qt, d_pt, out_cls, cls_grad, *gains = pl.pallas_call(
         partial(whole_step, names, frames),
         out_shape=[jax.ShapeDtypeStruct(s, d) for s, d in [*in_hbm.values(), *in_vmem.values()]],
         in_specs=[hbm] * len(large) + [vm] * len(small),
@@ -989,7 +993,8 @@
         return jnp.transpose(w.reshape(heads), (3, 0, 1, 2))
 
     grads = [(x.reshape(-1, width), F32) for x in (dx, d_w1, d_w2, d_fc, d_qs, d_ps, d_qt, d_pt)]
-    output, dx, d_w1, d_w2, d_fc, d_qs, d_ps, d_qt, d_pt = widened([(output, BF16)] + grads)
+    rest = [(out_cls, BF16), (cls_grad, F32)] + [(x, F32) for x in gains]
+    output, dx, d_w1, d_w2, d_fc, d_qs, d_ps, d_qt, d_pt, out_cls, cls_grad, *gains = widened([(output, BF16)] + grads + rest)
     return (
         by_frame(output), out_cls, by_frame(dx), cls_grad, gains[0], by_width(d_qt), d_pt.reshape(proj_time.shape), d_fc,
         gains[1], by_width(d_qs), d_ps.reshape(proj_space.shape), gains[2], d_w1, d_w2,

time: 226 us -> 223 us (0.987)
  local copies, waits for them, and re-layouts: 2.64 us -> 0 us
where the time goes in v6:
time: 223 us
  Pallas kernels  222 us (100%)
    pallas_call x1, Pallas kernels, local(): pl.pallas_call(partial(whole_step, names, frames), out_shape=[jax.ShapeDt...  213 us
    pallas_call x1, Pallas kernels, widened(): pl.pallas_call(widen, grid=(steps,), out_shape=[jax.ShapeDtypeStruct(x.sh...  8.72 us

profile of v6, /device:TPU:0, one launch (start us, length us, event | category | flops | bytes accessed | tf_op | source)
XLA Modules:
  0.0 222.9 jit_solution(931630062416468482)
XLA Ops:
  0.7 213.3 %shard_map.254 = (bf16[392,768]{1,0:T(8,128)(2,1)}, f32[392,768]{1,0:T(8,128)}, bf16[12,64,768]{2,1,0:T(8,128)(2,1)}, bf16[12,64,768]{2,1,0:T(8,128)(2,1)}, bf16...) custom-call(bf16[392,768]{1,0:T(8,128)(2,1)} %bitcast.51, ...), custom_call_target="tpu_custom_call" | custom-call | tf_op jit(solution)/shard_map/pallas_call | solution.py:978
  214.0 8.7 %shard_map.255 = (bf16[392,768]{1,0:T(8,128)(2,1)}, f32[392,768]{1,0:T(8,128)}, f32[768,768]{1,0:T(8,128)}, f32[768,768]{1,0:T(8,128)}, f32[768,768]{1,0:T(8,128...) custom-call(bf16[392,768]{1,0:T(8,128)(2,1)} %get-tuple-element.42.r, ...), custom_call_target="tpu_custom_call" | custom-call | tf_op jit(solution)/shard_map/pallas_call | solution.py:909
